TPU v7x, 32 devices: a whole 2x2x4 slice. The times are simulated.
32 devices in a mesh: patch: 8 (over z, x), sub: 4 (over y, core).
Axes of the slice: x: 2, y: 2, z: 4, core: 2. Of those that a mesh axis runs over, the one named last changes fastest.
Arguments:
- displacement: float32 [3, 64, 8192], P(None, 'patch', 'sub'), may hold values from -3 to 3
- load: float32 [3, 64, 8192], P(None, 'patch', 'sub'), may hold values from -6 to 6
- foundation: float32 [3, 64, 8192], P(None, 'patch', 'sub'), may hold values from 0.2 to 2
- layup: int32 [64, 8192], P('patch', 'sub'), may hold values from 0 to 7
- layup_stiffness: float32 [8, 6, 6], replicated, as said below
- w_first: bfloat16 [128, 6], replicated, may hold values from -2.5 to 2.5
- w_mid: bfloat16 [3, 128, 128], replicated, may hold values from -0.5 to 0.5
- w_last: bfloat16 [6, 128], replicated, may hold values from -0.5 to 0.5
Outputs:
- residual: float32 [3, 64, 8192], P(None, 'patch', 'sub')
- adjoint: float32 [3, 64, 8192], P(None, 'patch', 'sub')
- grad_first: float32 [128, 6], replicated
- grad_mid: float32 [3, 128, 128], replicated
- grad_last: float32 [6, 128], replicated
Inputs may be any that keep to these rules, and one draw needn't show every extreme that they name: `layup_stiffness`: each of the 8 matrices is symmetric positive definite.
All inputs are finite; a program needn't handle non-finite values.
Results may differ from a plain program's by a relative error of at most 0.0006.
The roundings to bfloat16 on the way count: a program that leaves them out, or rounds other values in their place, can miss the bound.
Values sent between devices are 32-bit elements; how exact they have to be, the bound alone decides.
No kernel may reach another device: no remote copies, remote signals or barrier semaphores. Data moves between devices by JAX's collectives and lax.ppermute only.
A program may use at most 128 MiB of HBM per device.

v0:
```python
import jax
import jax.numpy as jnp
from jax import lax
from jax.experimental import pallas as pl
from jax.experimental.pallas import tpu as pltpu
from jax.sharding import PartitionSpec as P

HY = 16
LANES = 128
AXES = ("patch", "sub")


def ring(axis, step):
    count = lax.axis_size(axis)
    return [(i, (i + step) % count) for i in range(count)]


def from_both(array, axis, dim, width):
    size = array.shape[dim]
    tail = lax.slice_in_dim(array, size - width, size, axis=dim)
    head = lax.slice_in_dim(array, 0, width, axis=dim)
    before = lax.ppermute(tail, axis, ring(axis, 1))
    after = lax.ppermute(head, axis, ring(axis, -1))
    return before, after


def rolled(array, shift, axis):
    return jnp.roll(array, shift, axis=axis)


def y_parts(field):
    before, after = rolled(field, 1, -1), rolled(field, -1, -1)
    both = before + after
    return 0.125 * both + 0.75 * field, 0.5 * (after - before), both - 2.0 * field


def x_value(f):
    return 0.125 * (rolled(f, 1, -2) + rolled(f, -1, -2)) + 0.75 * f


def x_slope(f):
    return 0.5 * (rolled(f, -1, -2) - rolled(f, 1, -2))


def x_curve(f):
    return rolled(f, 1, -2) + rolled(f, -1, -2) - 2.0 * f


def strains(nodal):
    value_u, slope_u, _ = y_parts(nodal[0])
    value_v, slope_v, _ = y_parts(nodal[1])
    value_w, slope_w, curve_w = y_parts(nodal[2])
    return jnp.stack(
        [
            x_slope(value_u),
            x_value(slope_v + 0.25 * value_w),
            x_value(slope_u) + x_slope(value_v),
            -x_curve(value_w),
            -x_value(curve_w),
            -2.0 * x_slope(slope_w),
        ]
    )


def forces(s):
    def y_value(f):
        return y_parts(f)[0]

    def y_slope(f):
        return -y_parts(f)[1]

    def y_curve(f):
        return y_parts(f)[2]

    value_1 = x_value(s[1])
    return jnp.stack(
        [
            y_value(-x_slope(s[0])) + y_slope(x_value(s[2])),
            y_slope(value_1) + y_value(-x_slope(s[2])),
            y_value(0.25 * value_1 - x_curve(s[3]))
            - y_curve(x_value(s[4]))
            - 2.0 * y_slope(-x_slope(s[5])),
        ]
    )


def apply_layup(stiffness, strain):
    running = stiffness[:, 0] * strain[0]
    for column in range(1, 6):
        running = running + stiffness[:, column] * strain[column]
    return running


def outer_product(left, right):
    return lax.dot_general(
        left, right, (((1,), (1,)), ((), ())), preferred_element_type=jnp.float32
    )


def forward_mlp(inputs, w_first, w_mid, w_last):
    hidden = jnp.tanh(jnp.dot(w_first, inputs, preferred_element_type=jnp.float32)).astype(
        jnp.bfloat16
    )
    activations = [hidden]
    for k in range(w_mid.shape[0]):
        hidden = jnp.tanh(
            jnp.dot(w_mid[k], hidden, preferred_element_type=jnp.float32)
        ).astype(jnp.bfloat16)
        activations.append(hidden)
    return jnp.dot(w_last, hidden, preferred_element_type=jnp.float32), activations


def backward_mlp(inputs, activations, upstream, w_mid, w_last):
    grad_last = outer_product(upstream, activations[-1])
    signal = jnp.dot(w_last.T, upstream, preferred_element_type=jnp.float32)
    derivative = (signal * (1.0 - jnp.square(activations[-1].astype(jnp.float32)))).astype(
        jnp.bfloat16
    )
    mid_grads = []
    for k in range(w_mid.shape[0] - 1, -1, -1):
        mid_grads.append(outer_product(derivative, activations[k]))
        signal = jnp.dot(w_mid[k].T, derivative, preferred_element_type=jnp.float32)
        derivative = (signal * (1.0 - jnp.square(activations[k].astype(jnp.float32)))).astype(
            jnp.bfloat16
        )
    grad_first = outer_product(derivative, inputs)
    return grad_first, jnp.stack(mid_grads[::-1]), grad_last


def everyone(rows):
    return lax.all_to_all(rows, AXES, 0, 0, tiled=True)


def galerkin(matrix, target):
    size = len(target)
    matrix = [list(row) for row in matrix]
    target = list(target)
    scale = [matrix[i][i] for i in range(size)]
    inverse = []
    for i in range(size):
        pivot = matrix[i][i]
        usable = pivot > 1e-6 * scale[i]
        inverse.append(jnp.where(usable, 1.0 / jnp.where(usable, pivot, 1.0), 0.0))
        for j in range(i + 1, size):
            factor = matrix[i][j] * inverse[i]
            for k in range(j, size):
                matrix[j][k] = matrix[j][k] - factor * matrix[i][k]
            target[j] = target[j] - factor * target[i]
    answer = [None] * size
    for i in reversed(range(size)):
        running = target[i]
        for j in range(i + 1, size):
            running = running - matrix[i][j] * answer[j]
        answer[i] = running * inverse[i]
    return answer


DEGREE = 3
UPPER = [(a, b) for a in range(6) for b in range(a, 6)]
HALVING = (0.0625, 0.0625, 0.0625, -0.125, -0.125, -0.5)
SUMS = 14


def lanes_of(tile):
    if isinstance(tile, int):
        return pl.ds(tile * LANES, LANES)
    return pl.ds(pl.multiple_of(tile * LANES, LANES), LANES)


def beside(tile, tiles):
    if isinstance(tile, int):
        return (tile - 1) % tiles, (tile + 1) % tiles
    return jnp.where(tile == 0, tiles - 1, tile - 1), jnp.where(tile == tiles - 1, 0, tile + 1)


def x_pair(f):
    return pltpu.roll(f, 1, 0), pltpu.roll(f, f.shape[0] - 1, 0)


def spread_strains(u, v, w):
    value_u, slope_u = u[0] + u[1] + 6.0 * u[2], u[1] - u[0]
    value_v, slope_v = v[0] + v[1] + 6.0 * v[2], v[1] - v[0]
    both_w = w[0] + w[1]
    value_w, slope_w, curve_w = both_w + 6.0 * w[2], w[1] - w[0], both_w - 2.0 * w[2]
    b, a = x_pair(value_u)
    e0 = a - b
    hoop = slope_v + 0.0625 * value_w
    b, a = x_pair(hoop)
    e1 = b + a + 6.0 * hoop
    b = pltpu.roll(slope_u - value_v, 1, 0)
    a = pltpu.roll(slope_u + value_v, slope_u.shape[0] - 1, 0)
    e2 = b + a + 6.0 * slope_u
    b, a = x_pair(value_w)
    e3 = b + a - 2.0 * value_w
    b, a = x_pair(curve_w)
    e4 = b + a + 6.0 * curve_w
    b, a = x_pair(slope_w)
    e5 = a - b
    return e0, e1, e2, e3, e4, e5


def spread_forces(s):
    b, a = x_pair(s[0])
    lean_u = b - a
    b, a = x_pair(s[2])
    lean_v = b - a
    turn_u = b + a + 6.0 * s[2]
    b, a = x_pair(s[1])
    turn_v = b + a + 6.0 * s[1]
    b, a = x_pair(s[3])
    lean_w = 0.0625 * turn_v + (b + a - 2.0 * s[3])
    b, a = x_pair(s[4])
    bent_w = b + a + 6.0 * s[4]
    b, a = x_pair(s[5])
    turn_w = a - b
    sum_w = lean_w + bent_w
    return (
        (lean_u + turn_u, lean_u - turn_u, 6.0 * lean_u),
        (lean_v + turn_v, lean_v - turn_v, 6.0 * lean_v),
        (sum_w - turn_w, sum_w + turn_w, 6.0 * lean_w - 2.0 * bent_w),
    )


def chosen(layers, bits):
    if len(layers) == 1:
        return layers[0]
    half = len(layers) // 2
    return jnp.where(bits[-1], chosen(layers[half:], bits[:-1]), chosen(layers[:half], bits[:-1]))


def krylov_kernel(
    table, numbers, r_mid, r_up, r_down, fields, fl_up, fl_down, basis, sums,
    stiff, before, after, ahead, behind, middle, support,
):
    layups = table.shape[0] // 36
    rows = r_mid.shape[1]
    wide = r_mid.shape[2]
    tiles = wide // LANES
    own_tiles = tiles - 1
    halo = fl_up.shape[1]
    tall = 3 * rows
    lane = lax.broadcasted_iota(jnp.int32, (tall, LANES), 1)
    first, final = lane == 0, lane == LANES - 1
    depth = 1
    while (1 << depth) < layups:
        depth += 1

    def place(k, c, at, value):
        basis[k, c, :, at] = value
        before[c, :, at] = pltpu.roll(value, 1, 1)
        after[c, :, at] = pltpu.roll(value, LANES - 1, 1)

    def set_up(tile, carry):
        at = lanes_of(tile)
        for c in range(3):
            value = jnp.concatenate([r_up[c, :, at], r_mid[c, :, at], r_down[c, :, at]], axis=0)
            place(0, c, at, value)
        edge = jnp.zeros((rows - halo, LANES), jnp.float32)
        for c in range(4):
            support[c, 0 : rows - halo, at] = edge
            support[c, rows - halo : rows, at] = fl_up[c, :, at]
            support[c, rows : 2 * rows, at] = fields[3 + c, :, at]
            support[c, 2 * rows : 2 * rows + halo, at] = fl_down[c, :, at]
            support[c, 2 * rows + halo : tall, at] = edge
        ids = support[3, :, at].astype(jnp.int32)
        bits = [(ids & (1 << k)) != 0 for k in range(depth)]
        for n, (a, b) in enumerate(UPPER):
            layers = [table[min(l, layups - 1) * 36 + a * 6 + b] for l in range(1 << depth)]
            stiff[n, :, at] = jnp.broadcast_to(chosen(layers, bits), (tall, LANES))
        return carry

    lax.fori_loop(0, tiles, set_up, 0)

    def strain_of(k, tile):
        at = lanes_of(tile)
        left, right = beside(tile, tiles)
        at_left, at_right = lanes_of(left), lanes_of(right)
        triples = [
            (
                jnp.where(first, before[c, :, at_left], before[c, :, at]),
                jnp.where(final, after[c, :, at_right], after[c, :, at]),
                basis[k, c, :, at],
            )
            for c in range(3)
        ]
        return spread_strains(*triples)

    def stress_of(e, at):
        s = [None] * 6
        for n, (a, b) in enumerate(UPPER):
            value = stiff[n, :, at]
            for p, q in ((a, b), (b, a))[: 1 if a == b else 2]:
                term = value * e[q]
                s[p] = term if s[p] is None else s[p] + term
        return s

    def mine(value):
        return value[rows : 2 * rows]

    zero = jnp.zeros((rows, LANES), jnp.float32)
    totals = [None] * SUMS

    for k in range(DEGREE):
        def push(tile, carry, k=k):
            at = lanes_of(tile)
            for c, (alpha, beta, gamma) in enumerate(
                spread_forces(stress_of(strain_of(k, tile), at))
            ):
                ahead[c, :, at] = pltpu.roll(alpha, 1, 1)
                behind[c, :, at] = pltpu.roll(beta, LANES - 1, 1)
                middle[c, :, at] = gamma
            return carry

        lax.fori_loop(0, tiles, push, 0)

        centre, width, inverse = numbers[k], numbers[3 + k], numbers[6 + k]
        former = numbers[2 + k]

        def advance(tile, carry, k=k):
            at = lanes_of(tile)
            left, right = beside(tile, tiles)
            at_left, at_right = lanes_of(left), lanes_of(right)
            image, here, following = [], [], []
            for c in range(3):
                vector = basis[k, c, :, at]
                value = (
                    middle[c, :, at]
                    + jnp.where(first, ahead[c, :, at_left], ahead[c, :, at])
                    + jnp.where(final, behind[c, :, at_right], behind[c, :, at])
                    + support[c, :, at] * vector
                )
                step = value - centre * vector
                if k:
                    step = step - former * basis[k - 1, c, :, at]
                step = step * inverse
                place(k + 1, c, at, step)
                image.append(mine(value))
                here.append(mine(vector))
                following.append(mine(step))
            if carry is None:
                return None

            def dot(left_side, right_side):
                return (
                    left_side[0] * right_side[0]
                    + left_side[1] * right_side[1]
                    + left_side[2] * right_side[2]
                )

            def old(m):
                return [basis[m, c, rows : 2 * rows, at] for c in range(3)]

            fresh = []
            origin = here if k == 0 else old(0)
            if k == 0:
                fresh.append(dot(here, here))
            fresh.append(dot(origin, following))
            for j in range(k + 1):
                fresh.append(dot(here if j == k else (origin if j == 0 else old(j)), image))
            if k == DEGREE - 1:
                fresh.append(dot(old(1), following))
                fresh.append(dot(here, following))
                fresh.append(dot(following, following))
            return tuple(p + q for p, q in zip(carry, fresh))

        names = ([0] if k == 0 else []) + [k + 1] + [4 + k * (k + 1) // 2 + j for j in range(k + 1)]
        if k == DEGREE - 1:
            names += [10, 11, 12]
        found = lax.fori_loop(0, own_tiles, advance, (zero,) * len(names))
        advance(own_tiles, None)
        for name, value in zip(names, found):
            totals[name] = value

    def energy(tile, running):
        at = lanes_of(tile)
        e = strain_of(DEGREE, tile)
        e = [mine(value) for value in e]
        for n, (a, b) in enumerate(UPPER):
            term = stiff[n, rows : 2 * rows, at] * e[b] * e[a]
            running = running + (term if a == b else 2.0 * term)
        for c in range(3):
            vector = basis[DEGREE, c, rows : 2 * rows, at]
            running = running + support[c, rows : 2 * rows, at] * vector * vector
        return running

    totals[13] = lax.fori_loop(0, own_tiles, energy, zero)
    place_of = lax.broadcasted_iota(jnp.int32, (1, LANES), 1)
    line = jnp.zeros((1, LANES), jnp.float32)
    for n in range(SUMS):
        total = jnp.sum(jnp.sum(totals[n], axis=0, keepdims=True), axis=1, keepdims=True)
        line = jnp.where(place_of == n, jnp.broadcast_to(total, (1, LANES)), line)
    sums[...] = jnp.broadcast_to(line[None], sums.shape)


def solve_kernel(numbers, sums, basis, adjoint, upstream, combined):
    rows = adjoint.shape[1]
    wide = basis.shape[3]
    tiles = wide // LANES
    own_tiles = tiles - 1
    tall = 3 * rows
    line = jnp.sum(sums[...], axis=0)
    picks = [jnp.broadcast_to(line[:, n : n + 1], (1, LANES)) for n in range(SUMS)]
    centre = [numbers[k] for k in range(3)]
    width = [numbers[3 + k] for k in range(3)]
    matrix = [[None] * 4 for _ in range(4)]
    for k in range(3):
        for j in range(k + 1):
            matrix[j][k] = picks[4 + k * (k + 1) // 2 + j]
    cross = [picks[3], picks[10], picks[11], picks[12]]
    for j in range(3):
        value = width[j] * cross[j + 1] + centre[j] * cross[j]
        matrix[j][3] = value + width[j - 1] * cross[j - 1] if j else value
    matrix[3][3] = picks[13]
    weights = [jnp.broadcast_to(x, (tall, LANES)) for x in galerkin(matrix, picks[:4])]

    def combine(tile, carry):
        at = lanes_of(tile)
        for c in range(3):
            value = weights[0] * basis[0, c, :, at]
            for k in range(1, DEGREE + 1):
                value = value + weights[k] * basis[k, c, :, at]
            combined[c, :, at] = value
            combined[3 + c, :, at] = pltpu.roll(value, 1, 1)
            combined[6 + c, :, at] = pltpu.roll(value, LANES - 1, 1)
        return carry

    lax.fori_loop(0, tiles, combine, 0)
    lane = lax.broadcasted_iota(jnp.int32, (tall, LANES), 1)
    first, final = lane == 0, lane == LANES - 1

    def strain(tile, carry):
        at = lanes_of(tile)
        left, right = beside(tile, tiles)
        at_left, at_right = lanes_of(left), lanes_of(right)
        triples = [
            (
                jnp.where(first, combined[3 + c, :, at_left], combined[3 + c, :, at]),
                jnp.where(final, combined[6 + c, :, at_right], combined[6 + c, :, at]),
                combined[c, :, at],
            )
            for c in range(3)
        ]
        for c in range(3):
            adjoint[c, :, at] = combined[c, rows : 2 * rows, at]
        for n, value in enumerate(spread_strains(*triples)):
            upstream[n, :, at] = HALVING[n] * value[rows : 2 * rows]
        return carry

    lax.fori_loop(0, own_tiles, strain, 0)


def basis_constants(layup_stiffness):
    bending = 0.5 * (jnp.mean(layup_stiffness[:, 3, 3]) + jnp.mean(layup_stiffness[:, 4, 4]))
    centres = [11.5 * bending + 1.1, 9.8 * bending + 1.1, 8.4 * bending + 1.1]
    widths = [3.9 * bending + 0.4, 5.6 * bending + 0.4, 4.8 * bending + 0.4]
    return centres, widths


def per_device(displacement, load, foundation, layup, layup_stiffness, w_first, w_mid, w_last):
    rows, cols = layup.shape
    devices = lax.axis_size("patch") * lax.axis_size("sub")
    wide = cols + LANES
    fields = jnp.concatenate(
        [displacement, foundation, layup.astype(jnp.float32)[None], load]
    )
    before, after = from_both(fields, "sub", 2, HY)
    fields = jnp.concatenate(
        [fields, after, jnp.zeros(fields.shape[:2] + (LANES - 2 * HY,), jnp.float32), before], axis=2
    )
    up, down = from_both(fields[:3], "patch", 1, 2)
    nodal = jnp.concatenate([up, fields[:3], down], axis=1)
    up, down = from_both(fields[3:7], "patch", 1, 6)
    near = jnp.concatenate([up[3, -1:], fields[6], down[3, :1]], axis=0).astype(jnp.int32)
    onehot = (
        near[None] == jnp.arange(layup_stiffness.shape[0], dtype=jnp.int32)[:, None, None]
    ).astype(jnp.float32)
    stiffness = jnp.einsum(
        "lab,lxy->abxy", layup_stiffness, onehot, precision=lax.Precision.HIGHEST
    )
    beyond = (up, down)

    strain = strains(nodal)[:, 1:-1]
    own = strain[:, 1:-1, :cols]
    inputs = own.reshape(6, -1).astype(jnp.bfloat16)
    learned, activations = forward_mlp(inputs, w_first, w_mid, w_last)
    edge = jnp.concatenate(
        [strain[:, 0], strain[:, -1], strain[:, 1:-1, cols:].reshape(6, -1)], axis=1
    ).astype(jnp.bfloat16)
    learned_edge, _ = forward_mlp(edge, w_first, w_mid, w_last)
    learned = jnp.concatenate(
        [
            learned_edge[:, None, :wide],
            jnp.concatenate(
                [
                    learned.reshape(6, rows, cols),
                    learned_edge[:, 2 * wide :].reshape(6, rows, LANES),
                ],
                axis=2,
            ),
            learned_edge[:, None, wide : 2 * wide],
        ],
        axis=1,
    )
    stress = apply_layup(stiffness, strain) + learned
    wide_residual = forces(stress)[:, 1:-1] + fields[3:6] * fields[:3] - fields[7:]
    residual = wide_residual[:, :, :cols]

    up, down = from_both(wide_residual, "patch", 1, rows)
    halving = jnp.array(HALVING, jnp.float32)
    table = (layup_stiffness * halving[:, None] * halving[None, :]).reshape(-1)
    centres, widths = basis_constants(layup_stiffness)
    numbers = jnp.stack(centres + widths + [1.0 / x for x in widths])
    on_chip = pl.BlockSpec(memory_space=pltpu.VMEM)
    scalars = pl.BlockSpec(memory_space=pltpu.SMEM)
    tall = 3 * rows
    block = pltpu.VMEM((3, tall, wide), jnp.float32)
    basis, sums = pl.pallas_call(
        krylov_kernel,
        name="krylov",
        in_specs=[scalars, scalars] + [on_chip] * 6,
        out_specs=[on_chip, on_chip],
        out_shape=[
            jax.ShapeDtypeStruct((DEGREE + 1, 3, tall, wide), jnp.float32),
            jax.ShapeDtypeStruct((devices, 1, LANES), jnp.float32),
        ],
        scratch_shapes=[pltpu.VMEM((len(UPPER), tall, wide), jnp.float32)]
        + [block] * 5
        + [pltpu.VMEM((4, tall, wide), jnp.float32)],
        compiler_params=pltpu.CompilerParams(vmem_limit_bytes=32 << 20),
    )(table, numbers, wide_residual, up, down, fields, *beyond)
    sums = everyone(sums)
    adjoint, upstream = pl.pallas_call(
        solve_kernel,
        name="solve",
        in_specs=[scalars, on_chip, on_chip],
        out_specs=[on_chip, on_chip],
        out_shape=[
            jax.ShapeDtypeStruct((3, rows, cols), jnp.float32),
            jax.ShapeDtypeStruct((6, rows, cols), jnp.float32),
        ],
        scratch_shapes=[pltpu.VMEM((9, tall, wide), jnp.float32)],
        compiler_params=pltpu.CompilerParams(vmem_limit_bytes=32 << 20),
    )(numbers, sums, basis)
    upstream = upstream.reshape(6, -1).astype(jnp.bfloat16)
    grads = backward_mlp(inputs, activations, upstream, w_mid, w_last)
    flat = jnp.concatenate([g.reshape(-1) for g in grads])
    chunk = -(-flat.shape[0] // devices)
    padded = jnp.pad(flat, (0, devices * chunk - flat.shape[0])).reshape(devices, chunk)
    part = everyone(padded).sum(0)
    total = everyone(jnp.broadcast_to(part, padded.shape)).reshape(-1)
    outs, at = [], 0
    for g in grads:
        outs.append(total[at : at + g.size].reshape(g.shape))
        at += g.size
    return (residual, adjoint, *outs)


def solution(mesh):
    field = P(None, "patch", "sub")
    return jax.shard_map(
        per_device,
        mesh=mesh,
        in_specs=(field, field, field, P("patch", "sub"), P(), P(), P(), P()),
        out_specs=(field, field, P(), P(), P()),
        check_vma=False,
    )
```

profile of v0, /device:TPU:0, one launch (start us, length us, event | category | flops | bytes accessed | tf_op | source)
XLA Modules:
  0.0 141.3 jit_solution(16858835005666254857)
XLA Ops:
  0.6 0.9 convert_bitcast_fusion.1
  1.5 1.2 pad_maximum_fusion
  2.7 2.4 %collective-permute-start = (f32[10,8,16]{2,1,0:T(8,128)S(1)}, f32[10,8,16]{2,1,0:T(8,128)S(1)}, u32[]{:S(2)}, u32[]{:S(2)}) collective-permute-start(f32[10,8,16]{2,1,0:T(8,128)S(1)} %get-tuple-element.110), channel_id=1, source_target_pairs={{0,3},{1,0},{2,1},{3,2},{4,7},{5,4},{6,5},{7,6},{8,11},{9,8},{10,9... | collective-permute-start | bytes 15368 | tf_op jit(solution)/shard_map/ppermute | solution.py:23
  5.2 1.4 slice_reduce_fusion
  8.0 0.6 collective-permute-done.1
  8.7 0.9 fusion.141
  9.6 4.6 %collective-permute-start.5 = (f32[3,2,2176]{2,1,0:T(2,128)S(1)}, f32[3,2,2176]{2,1,0:T(2,128)S(1)}, u32[]{:S(2)}, u32[]{:S(2)}) collective-permute-start(f32[3,2,2176]{2,1,0:T(2,128)S(1)} %get-tuple-element.106), channel_id=1, source_target_pairs={{0,28},{4,0},{8,4},{12,8},{16,12},{20,16},{24,20},{28,24},{1,29},{... | collective-permute-start | bytes 156680 | tf_op jit(solution)/shard_map/ppermute | solution.py:23
  14.2 4.8 %collective-permute-start.3 = (f32[4,6,2176]{2,1,0:T(8,128)}, f32[4,6,2176]{2,1,0:T(8,128)S(1)}, u32[]{:S(2)}, u32[]{:S(2)}) collective-permute-start(f32[4,6,2176]{2,1,0:T(8,128)} %get-tuple-element.108), channel_id=1, source_target_pairs={{0,28},{4,0},{8,4},{12,8},{16,12},{20,16},{24,20},{28,24},{1,29},{... | collective-permute-start | bytes 626696 | tf_op jit(solution)/shard_map/ppermute | solution.py:23
  19.0 3.1 %collective-permute-done.4 = f32[3,2,2176]{2,1,0:T(2,128)S(1)} collective-permute-done((f32[3,2,2176]{2,1,0:T(2,128)S(1)}, f32[3,2,2176]{2,1,0:T(2,128)S(1)}, u32[]{:S(2)}, u32[]{:S(2)}) %collective-permute-start.4) | collective-permute-done | bytes 52256 | tf_op jit(solution)/shard_map/ppermute | solution.py:22
  23.4 0.2 constant_dynamic-update-slice_fusion.4
  24.1 0.6 copy.189
  24.7 0.6 copy.190
  25.4 2.0 %fusion.9 = bf16[5376,128]{1,0:T(8,128)(2,1)S(1)} fusion(bf16[128,6]{0,1:T(8,128)(2,1)S(1)} %copy-done, bf16[6,1024]{1,0:T(8,128)(2,1)S(1)} %bitcast.397, bf16[6,2176]{1,0:T(8,128)(2,1)} %bitcast.395, bf16[6,2176]{1,0:T(8,128)(2,1)} %bitcast.396, bf16[3,128,128]{2,1,0:T(8,128)(2,1)} %param.15), kind=kOutput, calls=%fused_computation.21 | convolution fusion | flops 185988096 | bytes 1492480 | tf_op jit(solution)/shard_map/dot_general | solution.py:107
  27.3 2.4 %fusion.10 = bf16[5376,128]{1,0:T(8,128)(2,1)} fusion(bf16[5376,128]{1,0:T(8,128)(2,1)S(1)} %fusion.9, bf16[3,128,128]{2,1,0:T(8,128)(2,1)} %param.15), kind=kOutput, calls=%fused_computation.22 | convolution fusion | flops 176848896 | bytes 2785280 | tf_op jit(solution)/shard_map/dot_general | solution.py:107
  29.7 2.4 %convolution_bitcast_fusion = f32[6,5376]{1,0:T(8,128)S(1)} fusion(bf16[6,128]{1,0:T(8,128)(2,1)} %param.16, bf16[5376,128]{1,0:T(8,128)(2,1)} %fusion.10, bf16[3,128,128]{2,1,0:T(8,128)(2,1)} %param.15), kind=kOutput, calls=%fused_computation.24 | convolution fusion | flops 185106432 | bytes 1540096 | tf_op jit(solution)/shard_map/dot_general | solution.py:110
  32.1 1.1 slice_bitcast_fusion.6
  33.4 1.8 %fusion.3 = bf16[16384,128]{1,0:T(8,128)(2,1)S(1)} fusion(bf16[6,16384]{1,0:T(8,128)(2,1)S(1)} %bitcast.388, bf16[128,6]{0,1:T(8,128)(2,1)S(1)} %copy-done), kind=kOutput, calls=%fused_computation.11 | convolution fusion | flops 27262976 | bytes 4392448 | tf_op jit(solution)/shard_map/dot_general | solution.py:101
  35.2 2.0 %copy-done.6 = bf16[16384,128]{1,0:T(8,128)(2,1)} copy-done((bf16[16384,128]{1,0:T(8,128)(2,1)}, bf16[16384,128]{1,0:T(8,128)(2,1)S(1)}, u32[]{:S(2)}) %copy-start.6) | copy-done | bytes 4194328
  37.2 1.3 fusion.4
  38.4 1.2 fusion.5
  39.7 0.7 copy-done.2
  40.5 1.2 fusion.6
  41.7 0.8 copy-done.4
  42.7 1.2 fusion.146
  43.8 0.2 copy.188
  44.1 0.4 copy-done.8
  44.6 2.0 %fusion.26 = f32[10,2176,6,6]{1,3,2,0:T(8,128)S(1)} fusion(s32[10,2176]{1,0:T(8,128)S(1)} %maximum_convert_fusion, f32[8,6,6]{2,0,1:T(8,128)S(1)} %copy-done.14), kind=kOutput, calls=%fused_computation.51 | convolution fusion | flops 75376640 | bytes 3221632 | tf_op jit(solution)/shard_map/lab,lxy->abxy/dot_general | solution.py:477
  46.7 1.1 copy.187
  47.8 0.5 fusion.15
  48.3 0.2 fusion.137
  50.3 0.2 fusion.63
  50.5 0.2 fusion.53
  50.7 0.3 fusion.74
  51.0 2.5 %collective-permute-start.6 = (f32[3,8,2176]{2,1,0:T(8,128)S(1)}, f32[3,8,2176]{2,1,0:T(8,128)S(1)}, u32[]{:S(2)}, u32[]{:S(2)}) collective-permute-start(f32[3,8,2176]{2,1,0:T(8,128)S(1)} %slice_subtract_fusion.r_mid), channel_id=1, source_target_pairs={{0,4},{4,8},{8,12},{12,16},{16,20},{20,24},{24,28},{28,0},{1,5},{5... | collective-permute-start | bytes 626696 | tf_op jit(solution)/shard_map/ppermute | solution.py:22
  53.6 2.2 %collective-permute-start.7 = (f32[3,8,2176]{2,1,0:T(8,128)S(1)}, f32[3,8,2176]{2,1,0:T(8,128)S(1)}, u32[]{:S(2)}, u32[]{:S(2)}) collective-permute-start(f32[3,8,2176]{2,1,0:T(8,128)S(1)} %slice_subtract_fusion.r_mid), channel_id=1, source_target_pairs={{0,28},{4,0},{8,4},{12,8},{16,12},{20,16},{24,20},{28,24},{1,29},{... | collective-permute-start | bytes 626696 | tf_op jit(solution)/shard_map/ppermute | solution.py:23
  56.1 3.6 %collective-permute-done.6.r_up = f32[3,8,2176]{2,1,0:T(8,128)S(1)} collective-permute-done((f32[3,8,2176]{2,1,0:T(8,128)S(1)}, f32[3,8,2176]{2,1,0:T(8,128)S(1)}, u32[]{:S(2)}, u32[]{:S(2)}) %collective-permute-start.6) | collective-permute-done | bytes 208928 | tf_op jit(solution)/shard_map/ppermute | solution.py:22
  59.7 1.9 %collective-permute-done.7.r_down = f32[3,8,2176]{2,1,0:T(8,128)S(1)} collective-permute-done((f32[3,8,2176]{2,1,0:T(8,128)S(1)}, f32[3,8,2176]{2,1,0:T(8,128)S(1)}, u32[]{:S(2)}, u32[]{:S(2)}) %collective-permute-start.7) | collective-permute-done | bytes 208928 | tf_op jit(solution)/shard_map/ppermute | solution.py:23
  61.6 15.5 %krylov.1 = (f32[4,3,24,2176]{3,2,1,0:T(8,128)S(1)}, f32[32,1,128]{2,1,0:T(1,128)S(1)}) custom-call(f32[288]{0:T(512)S(1)} %reshape.1405.table, f32[9]{0:T(128)S(1)} %stack.68.numbers, f32[3,8,2176]{2,1,0:T(8,128)S(1)} %slice_subtract_fusion.r_mid, f32[3,8,2176]{2,1,0:T(8,128)S(1)} %collective-permute-done.6.r_up, ...), custom_call_target="tpu_custom_call" | custom-call | tf_op jit(solution)/shard_map/krylov/pallas_call | solution.py:517
  77.1 10.9 %all_to_all.20.sums = f32[32,1,128]{2,1,0:T(1,128)S(1)} all-to-all(f32[32,1,128]{2,1,0:T(1,128)S(1)} %get-tuple-element.9), channel_id=1, replica_groups=mesh['patch'=8,'sub'=4] {'patch','sub'}, dimensions={0} | all-to-all | bytes 32768 | tf_op jit(solution)/shard_map/all_to_all | solution.py:131
  88.0 3.3 %solve.1 = (f32[3,8,2048]{2,1,0:T(8,128)}, f32[6,8,2048]{2,1,0:T(8,128)S(1)}) custom-call(f32[9]{0:T(128)S(1)} %stack.68.numbers, f32[32,1,128]{2,1,0:T(1,128)S(1)} %all_to_all.20.sums, f32[4,3,24,2176]{3,2,1,0:T(8,128)S(1)} %get-tuple-element.10.basis), custom_call_target="tpu_custom_call" | custom-call | tf_op jit(solution)/shard_map/solve/pallas_call | solution.py:532
  91.4 0.7 convolution_bitcast_fusion.4
  92.1 2.1 %fusion.7 = bf16[16384,128]{1,0:T(8,128)(2,1)S(1)} fusion(bf16[6,16384]{1,0:T(8,128)(2,1)S(1)} %bitcast.391, bf16[6,128]{1,0:T(8,128)(2,1)S(1)} %copy-done.15, bf16[16384,128]{1,0:T(8,128)(2,1)S(1)} %copy-done.9), kind=kOutput, calls=%fused_computation.15 | convolution fusion | flops 35651584 | bytes 8586752 | tf_op jit(solution)/shard_map/dot_general | solution.py:115
  94.3 1.3 convolution_bitcast_fusion.1
  95.6 1.6 %fusion = bf16[16384,128]{1,0:T(8,128)(2,1)S(1)} fusion(bf16[16384,128]{1,0:T(8,128)(2,1)S(1)} %fusion.7, bf16[16384,128]{1,0:T(8,128)(2,1)S(1)} %copy-done.5, bf16[3,128,128]{2,1,0:T(8,128)(2,1)S(1)} %copy-done.13), kind=kOutput, calls=%fused_computation.8 | convolution fusion | flops 547356672 | bytes 12615680 | tf_op jit(solution)/shard_map/dot_general | solution.py:122
  97.2 0.6 copy-done.3
  97.8 1.4 convolution_bitcast_fusion.2
  99.2 1.6 %fusion.1 = bf16[16384,128]{1,0:T(8,128)(2,1)S(1)} fusion(bf16[16384,128]{1,0:T(8,128)(2,1)S(1)} %fusion, bf16[16384,128]{1,0:T(8,128)(2,1)S(1)} %copy-done.3, bf16[3,128,128]{2,1,0:T(8,128)(2,1)S(1)} %copy-done.13), kind=kOutput, calls=%fused_computation.9 | convolution fusion | flops 547356672 | bytes 12615680 | tf_op jit(solution)/shard_map/dot_general | solution.py:122
  100.8 2.0 %copy-done.10 = bf16[16384,128]{1,0:T(8,128)(2,1)} copy-done((bf16[16384,128]{1,0:T(8,128)(2,1)}, bf16[16384,128]{1,0:T(8,128)(2,1)S(1)}, u32[]{:S(2)}) %copy-start.10) | copy-done | bytes 4194328
  102.8 1.4 convolution_bitcast_fusion.3
  104.1 6.2 %fusion.12 = f32[128,6]{1,0:T(8,128)S(1)} fusion(bf16[6,16384]{1,0:T(8,128)(2,1)S(1)} %bitcast.389, bf16[16384,128]{1,0:T(8,128)(2,1)} %copy-done.10, bf16[16384,128]{1,0:T(8,128)(2,1)} %copy-done.6, bf16[3,128,128]{2,1,0:T(8,128)(2,1)S(1)} %copy-done.13), kind=kOutput, calls=%fused_computation.26 | convolution fusion | flops 572522496 | bytes 8686592 | tf_op jit(solution)/shard_map/dot_general | solution.py:95
  110.5 0.3 all_to_all.14
  110.8 11.1 %all_to_all.21 = f32[32,1,1584]{2,1,0:T(1,128)S(1)} all-to-all(f32[32,1,1584]{2,1,0:T(1,128)S(1)} %all_to_all.14), channel_id=1, replica_groups=mesh['patch'=8,'sub'=4] {'patch','sub'}, dimensions={0} | all-to-all | bytes 405504 | tf_op jit(solution)/shard_map/all_to_all | solution.py:131
  122.1 0.8 broadcast_in_dim.21
  122.9 2.6 %all-to-all-start.2 = ((f32[32,1,1584]{2,1,0:T(1,128)}), f32[32,1,1584]{2,1,0:T(1,128)S(1)}, u32[]{:S(2)}, u32[]{:S(2)}) async-start(f32[32,1,1584]{2,1,0:T(1,128)} %broadcast_in_dim.21), calls=%async_computation.2 | async-start | bytes 425984 | tf_op jit(solution)/shard_map/all_to_all | solution.py:131
  125.5 0.7 slice.875
  126.2 8.7 %all-to-all-done.2 = f32[32,1,1584]{2,1,0:T(1,128)S(1)} async-done(((f32[32,1,1584]{2,1,0:T(1,128)}), f32[32,1,1584]{2,1,0:T(1,128)S(1)}, u32[]{:S(2)}, u32[]{:S(2)}) %all-to-all-start.2) | async-done | bytes 202784 | tf_op jit(solution)/shard_map/all_to_all | solution.py:131
  134.9 0.5 reduce.3
  135.4 2.7 %slice.740 = f32[8448,6]{1,0:T(8,128)} reshape(f32[32,1584]{1,0:T(8,128)S(1)} %reduce.3) | data formatting | bytes 405504 | tf_op jit(solution)/shard_map/slice | solution.py:553
  138.1 0.2 reshape.1409
  138.3 0.2 slice.743
  138.5 0.8 slice.876
  139.3 0.7 copy.168
  140.0 0.7 slice.877
  140.7 0.6 slice.878
  (119 shorter events, 4.9 us)
Async XLA Ops:
  0.6 24.7 %copy-start = (bf16[128,6]{0,1:T(8,128)(2,1)S(1)}, bf16[128,6]{0,1:T(8,128)(2,1)}, u32[]{:S(2)}) copy-start(bf16[128,6]{0,1:T(8,128)(2,1)} %param.14) | copy-start | bytes 4612
  2.7 5.3 %collective-permute-start = (f32[10,8,16]{2,1,0:T(8,128)S(1)}, f32[10,8,16]{2,1,0:T(8,128)S(1)}, u32[]{:S(2)}, u32[]{:S(2)}) collective-permute-start(f32[10,8,16]{2,1,0:T(8,128)S(1)} %get-tuple-element.110), channel_id=1, source_target_pairs={{0,3},{1,0},{2,1},{3,2},{4,7},{5,4},{6,5},{7,6},{8,11},{9,8},{10,9... | collective-permute-start | bytes 15368 | tf_op jit(solution)/shard_map/ppermute | solution.py:23
  5.2 3.4 %collective-permute-start.1 = (f32[10,8,16]{2,1,0:T(8,128)S(1)}, f32[10,8,16]{2,1,0:T(8,128)S(1)}, u32[]{:S(2)}, u32[]{:S(2)}) collective-permute-start(f32[10,8,16]{2,1,0:T(8,128)S(1)} %get-tuple-element.109), channel_id=1, source_target_pairs={{0,1},{1,2},{2,3},{3,0},{4,5},{5,6},{6,7},{7,4},{8,9},{9,10},{10,1... | collective-permute-start | bytes 15368 | tf_op jit(solution)/shard_map/ppermute | solution.py:22
  9.6 9.4 %collective-permute-start.5 = (f32[3,2,2176]{2,1,0:T(2,128)S(1)}, f32[3,2,2176]{2,1,0:T(2,128)S(1)}, u32[]{:S(2)}, u32[]{:S(2)}) collective-permute-start(f32[3,2,2176]{2,1,0:T(2,128)S(1)} %get-tuple-element.106), channel_id=1, source_target_pairs={{0,28},{4,0},{8,4},{12,8},{16,12},{20,16},{24,20},{28,24},{1,29},{... | collective-permute-start | bytes 156680 | tf_op jit(solution)/shard_map/ppermute | solution.py:23
  14.2 7.9 %collective-permute-start.4 = (f32[3,2,2176]{2,1,0:T(2,128)S(1)}, f32[3,2,2176]{2,1,0:T(2,128)S(1)}, u32[]{:S(2)}, u32[]{:S(2)}) collective-permute-start(f32[3,2,2176]{2,1,0:T(2,128)S(1)} %get-tuple-element.105), channel_id=1, source_target_pairs={{0,4},{4,8},{8,12},{12,16},{16,20},{20,24},{24,28},{28,0},{1,5},{5... | collective-permute-start | bytes 156680 | tf_op jit(solution)/shard_map/ppermute | solution.py:22
  14.2 30.3 %collective-permute-start.3 = (f32[4,6,2176]{2,1,0:T(8,128)}, f32[4,6,2176]{2,1,0:T(8,128)S(1)}, u32[]{:S(2)}, u32[]{:S(2)}) collective-permute-start(f32[4,6,2176]{2,1,0:T(8,128)} %get-tuple-element.108), channel_id=1, source_target_pairs={{0,28},{4,0},{8,4},{12,8},{16,12},{20,16},{24,20},{28,24},{1,29},{... | collective-permute-start | bytes 626696 | tf_op jit(solution)/shard_map/ppermute | solution.py:23
  19.0 25.5 %collective-permute-start.2 = (f32[4,6,2176]{2,1,0:T(8,128)}, f32[4,6,2176]{2,1,0:T(8,128)S(1)}, u32[]{:S(2)}, u32[]{:S(2)}) collective-permute-start(f32[4,6,2176]{2,1,0:T(8,128)} %get-tuple-element.107), channel_id=1, source_target_pairs={{0,4},{4,8},{8,12},{12,16},{16,20},{20,24},{24,28},{28,0},{1,5},{5... | collective-permute-start | bytes 626696 | tf_op jit(solution)/shard_map/ppermute | solution.py:22
  23.9 1.4 copy-start.11
  29.7 7.5 %copy-start.12 = (bf16[3,128,128]{2,1,0:T(8,128)(2,1)S(1)}, bf16[3,128,128]{2,1,0:T(8,128)(2,1)}, u32[]{:S(2)}) copy-start(bf16[3,128,128]{2,1,0:T(8,128)(2,1)} %param.15) | copy-start | bytes 294916
  35.2 2.0 %copy-start.6 = (bf16[16384,128]{1,0:T(8,128)(2,1)}, bf16[16384,128]{1,0:T(8,128)(2,1)S(1)}, u32[]{:S(2)}) copy-start(bf16[16384,128]{1,0:T(8,128)(2,1)S(1)} %fusion.3) | copy-start | bytes 12582916
  38.4 2.0 %copy-start.2 = (bf16[16384,128]{1,0:T(8,128)(2,1)}, bf16[16384,128]{1,0:T(8,128)(2,1)S(1)}, u32[]{:S(2)}) copy-start(bf16[16384,128]{1,0:T(8,128)(2,1)S(1)} %fusion.4) | copy-start | bytes 12582916
  40.4 2.1 %copy-start.4 = (bf16[16384,128]{1,0:T(8,128)(2,1)}, bf16[16384,128]{1,0:T(8,128)(2,1)S(1)}, u32[]{:S(2)}) copy-start(bf16[16384,128]{1,0:T(8,128)(2,1)S(1)} %fusion.5) | copy-start | bytes 12582916
  40.5 2.2 %copy-start.15 = (bf16[6,128]{1,0:T(8,128)(2,1)S(1)}, bf16[6,128]{1,0:T(8,128)(2,1)}, u32[]{:S(2)}) copy-start(bf16[6,128]{1,0:T(8,128)(2,1)} %param.16) | copy-start | bytes 4612
  42.5 1.9 %copy-start.8 = (bf16[16384,128]{1,0:T(8,128)(2,1)}, bf16[16384,128]{1,0:T(8,128)(2,1)S(1)}, u32[]{:S(2)}) copy-start(bf16[16384,128]{1,0:T(8,128)(2,1)S(1)} %fusion.6) | copy-start | bytes 12582916
  42.6 2.0 %copy-start.14 = (f32[8,6,6]{2,0,1:T(8,128)S(1)}, f32[8,6,6]{2,0,1:T(8,128)}, u32[]{:S(2)}) copy-start(f32[8,6,6]{2,0,1:T(8,128)} %param.13) | copy-start | bytes 3460
  49.8 6.0 %copy-start.16 = (f32[6]{0:T(128)S(1)}, f32[6]{0:T(128)}, u32[]{:S(2)}) copy-start(f32[6]{0:T(128)} %constant.61.clone) | copy-start | bytes 76
  51.0 8.7 %collective-permute-start.6 = (f32[3,8,2176]{2,1,0:T(8,128)S(1)}, f32[3,8,2176]{2,1,0:T(8,128)S(1)}, u32[]{:S(2)}, u32[]{:S(2)}) collective-permute-start(f32[3,8,2176]{2,1,0:T(8,128)S(1)} %slice_subtract_fusion.r_mid), channel_id=1, source_target_pairs={{0,4},{4,8},{8,12},{12,16},{16,20},{20,24},{24,28},{28,0},{1,5},{5... | collective-permute-start | bytes 626696 | tf_op jit(solution)/shard_map/ppermute | solution.py:22
  53.6 8.0 %collective-permute-start.7 = (f32[3,8,2176]{2,1,0:T(8,128)S(1)}, f32[3,8,2176]{2,1,0:T(8,128)S(1)}, u32[]{:S(2)}, u32[]{:S(2)}) collective-permute-start(f32[3,8,2176]{2,1,0:T(8,128)S(1)} %slice_subtract_fusion.r_mid), channel_id=1, source_target_pairs={{0,28},{4,0},{8,4},{12,8},{16,12},{20,16},{24,20},{28,24},{1,29},{... | collective-permute-start | bytes 626696 | tf_op jit(solution)/shard_map/ppermute | solution.py:23
  56.1 35.3 %copy-start.9 = (bf16[16384,128]{1,0:T(8,128)(2,1)S(1)}, bf16[16384,128]{1,0:T(8,128)(2,1)}, u32[]{:S(2)}) copy-start(bf16[16384,128]{1,0:T(8,128)(2,1)} %copy-done.8) | copy-start | bytes 12582916
  92.1 2.2 %copy-start.5 = (bf16[16384,128]{1,0:T(8,128)(2,1)S(1)}, bf16[16384,128]{1,0:T(8,128)(2,1)}, u32[]{:S(2)}) copy-start(bf16[16384,128]{1,0:T(8,128)(2,1)} %copy-done.4) | copy-start | bytes 12582916
  94.3 1.3 copy-start.13
  95.6 2.2 %copy-start.3 = (bf16[16384,128]{1,0:T(8,128)(2,1)S(1)}, bf16[16384,128]{1,0:T(8,128)(2,1)}, u32[]{:S(2)}) copy-start(bf16[16384,128]{1,0:T(8,128)(2,1)} %copy-done.2) | copy-start | bytes 12582916
  99.2 3.6 %copy-start.7 = (bf16[16384,128]{1,0:T(8,128)(2,1)S(1)}, bf16[16384,128]{1,0:T(8,128)(2,1)}, u32[]{:S(2)}) copy-start(bf16[16384,128]{1,0:T(8,128)(2,1)} %copy-done.6) | copy-start | bytes 12582916
  100.8 2.0 %copy-start.10 = (bf16[16384,128]{1,0:T(8,128)(2,1)}, bf16[16384,128]{1,0:T(8,128)(2,1)S(1)}, u32[]{:S(2)}) copy-start(bf16[16384,128]{1,0:T(8,128)(2,1)S(1)} %fusion.1) | copy-start | bytes 12582916
  110.5 30.8 %copy-start.1 = (bf16[128,6]{0,1:T(8,128)(2,1)S(1)}, bf16[128,6]{0,1:T(8,128)(2,1)}, u32[]{:S(2)}) copy-start(bf16[128,6]{0,1:T(8,128)(2,1)} %param.14) | copy-start | bytes 4612
  122.9 12.0 %all-to-all-start.2 = ((f32[32,1,1584]{2,1,0:T(1,128)}), f32[32,1,1584]{2,1,0:T(1,128)S(1)}, u32[]{:S(2)}, u32[]{:S(2)}) async-start(f32[32,1,1584]{2,1,0:T(1,128)} %broadcast_in_dim.21), calls=%async_computation.2 | async-start | bytes 425984 | tf_op jit(solution)/shard_map/all_to_all | solution.py:131
where the time goes:
time: 142 us; the launch traced here: 141 us
  matrix products  31.6 us (22%)
  local copies, waits for them, and re-layouts  22.2 us (16%)
  blocking collectives  22 us (15%)
  starting transfers between devices  19.1 us (13%)
  Pallas kernels  18.8 us (13%)
  waiting for transfers between devices  17.9 us (13%)
  other arithmetic  6.81 us (5%)
  between operations  2.85 us (2%)
    all_to_all x2, blocking collectives, everyone(): return lax.all_to_all(rows, AXES, 0, 0, tiled=True)  22 us
    pallas_call x1, Pallas kernels, per_device(): pl.pallas_call(krylov_kernel, name='krylov', in_specs=[scalars, scalars]...  15.5 us
    ppermute x4, starting transfers between devices, from_both(): after = lax.ppermute(head, axis, ring(axis, -1))  14 us
    dot_general x5, matrix products, outer_product(): lax.dot_general(left, right, (((1,), (1,)), ((), ())), preferred_element_...  10.8 us
    unnamed x45, local copies, waits for them, and re-layouts  10.1 us
    all_to_all x1, waiting for transfers between devices, everyone(): return lax.all_to_all(rows, AXES, 0, 0, tiled=True)  8.73 us
    dot_general x5, matrix products, forward_mlp(): jnp.dot(w_mid[k], hidden, preferred_element_type=jnp.float32)  8.09 us
    ppermute x4, waiting for transfers between devices, from_both(): before = lax.ppermute(tail, axis, ring(axis, 1))  7.23 us
  transfers between devices with their start and end apart: 9, of which 5 were waited for; matrix products, arithmetic and copies ran while one was open for 15% of the time, Pallas kernels for 0%

commit v1 on v0

v1 whole, which is shorter than its diff:
```python
import jax
import jax.numpy as jnp
from jax import lax
from jax.experimental import pallas as pl
from jax.experimental.pallas import tpu as pltpu
from jax.sharding import PartitionSpec as P

HY = 16
LANES = 128
AXES = ("patch", "sub")


def ring(axis, step):
    count = lax.axis_size(axis)
    return [(i, (i + step) % count) for i in range(count)]


def from_both(array, axis, dim, width):
    size = array.shape[dim]
    tail = lax.slice_in_dim(array, size - width, size, axis=dim)
    head = lax.slice_in_dim(array, 0, width, axis=dim)
    before = lax.ppermute(tail, axis, ring(axis, 1))
    after = lax.ppermute(head, axis, ring(axis, -1))
    return before, after


def everyone(rows):
    return lax.all_to_all(rows, AXES, 0, 0, tiled=True)


def galerkin(matrix, target):
    size = len(target)
    matrix = [list(row) for row in matrix]
    target = list(target)
    scale = [matrix[i][i] for i in range(size)]
    inverse = []
    for i in range(size):
        pivot = matrix[i][i]
        usable = pivot > 1e-6 * scale[i]
        inverse.append(jnp.where(usable, 1.0 / jnp.where(usable, pivot, 1.0), 0.0))
        for j in range(i + 1, size):
            factor = matrix[i][j] * inverse[i]
            for k in range(j, size):
                matrix[j][k] = matrix[j][k] - factor * matrix[i][k]
            target[j] = target[j] - factor * target[i]
    answer = [None] * size
    for i in reversed(range(size)):
        running = target[i]
        for j in range(i + 1, size):
            running = running - matrix[i][j] * answer[j]
        answer[i] = running * inverse[i]
    return answer


DEGREE = 3
UPPER = [(a, b) for a in range(6) for b in range(a, 6)]
HALVING = (0.0625, 0.0625, 0.0625, -0.125, -0.125, -0.5)
SUMS = 14


def lanes_of(tile):
    if isinstance(tile, int):
        return pl.ds(tile * LANES, LANES)
    return pl.ds(pl.multiple_of(tile * LANES, LANES), LANES)


def beside(tile, tiles):
    if isinstance(tile, int):
        return (tile - 1) % tiles, (tile + 1) % tiles
    return jnp.where(tile == 0, tiles - 1, tile - 1), jnp.where(tile == tiles - 1, 0, tile + 1)


def x_pair(f):
    return pltpu.roll(f, 1, 0), pltpu.roll(f, f.shape[0] - 1, 0)


def spread_strains(u, v, w):
    value_u, slope_u = u[0] + u[1] + 6.0 * u[2], u[1] - u[0]
    value_v, slope_v = v[0] + v[1] + 6.0 * v[2], v[1] - v[0]
    both_w = w[0] + w[1]
    value_w, slope_w, curve_w = both_w + 6.0 * w[2], w[1] - w[0], both_w - 2.0 * w[2]
    b, a = x_pair(value_u)
    e0 = a - b
    hoop = slope_v + 0.0625 * value_w
    b, a = x_pair(hoop)
    e1 = b + a + 6.0 * hoop
    b = pltpu.roll(slope_u - value_v, 1, 0)
    a = pltpu.roll(slope_u + value_v, slope_u.shape[0] - 1, 0)
    e2 = b + a + 6.0 * slope_u
    b, a = x_pair(value_w)
    e3 = b + a - 2.0 * value_w
    b, a = x_pair(curve_w)
    e4 = b + a + 6.0 * curve_w
    b, a = x_pair(slope_w)
    e5 = a - b
    return e0, e1, e2, e3, e4, e5


def spread_forces(s):
    b, a = x_pair(s[0])
    lean_u = b - a
    b, a = x_pair(s[2])
    lean_v = b - a
    turn_u = b + a + 6.0 * s[2]
    b, a = x_pair(s[1])
    turn_v = b + a + 6.0 * s[1]
    b, a = x_pair(s[3])
    lean_w = 0.0625 * turn_v + (b + a - 2.0 * s[3])
    b, a = x_pair(s[4])
    bent_w = b + a + 6.0 * s[4]
    b, a = x_pair(s[5])
    turn_w = a - b
    sum_w = lean_w + bent_w
    return (
        (lean_u + turn_u, lean_u - turn_u, 6.0 * lean_u),
        (lean_v + turn_v, lean_v - turn_v, 6.0 * lean_v),
        (sum_w - turn_w, sum_w + turn_w, 6.0 * lean_w - 2.0 * bent_w),
    )


def chosen(layers, bits):
    if len(layers) == 1:
        return layers[0]
    half = len(layers) // 2
    return jnp.where(bits[-1], chosen(layers[half:], bits[:-1]), chosen(layers[:half], bits[:-1]))


MARGIN = 2
FIELDS = 8
PADDED = 16


def triples_of(centre, before, after, tile, tiles, first, final):
    at = lanes_of(tile)
    left, right = beside(tile, tiles)
    at_left, at_right = lanes_of(left), lanes_of(right)
    return [
        (
            jnp.where(first, before[c, :, at_left], before[c, :, at]),
            jnp.where(final, after[c, :, at_right], after[c, :, at]),
            centre[c, :, at],
        )
        for c in range(3)
    ]


def mixed(values, e):
    s = [None] * 6
    for n, (a, b) in enumerate(UPPER):
        for p, q in ((a, b), (b, a))[: 1 if a == b else 2]:
            term = values[n] * e[q]
            s[p] = term if s[p] is None else s[p] + term
    return s


def product(left, right):
    return jnp.dot(left, right, preferred_element_type=jnp.float32)


def widened(x):
    return jnp.concatenate([x, jnp.zeros_like(x)], axis=0).astype(jnp.bfloat16)


def learn(x, w_first, w_mid, w_last, keep=None):
    h = jnp.tanh(product(w_first[...], x)).astype(jnp.bfloat16)
    if keep is not None:
        keep(0, h)
    for k in range(w_mid.shape[0]):
        h = jnp.tanh(product(w_mid[k], h)).astype(jnp.bfloat16)
        if keep is not None:
            keep(k + 1, h)
    return product(w_last[...], h)[:FIELDS]


def pieces_of(cols):
    step = cols
    while step > 1024 and step % 256 == 0:
        step //= 2
    return [(at, step) for at in range(0, cols, step)]


def gathered(array, row, spread, at, size):
    tiles = range(at // LANES, (at + size) // LANES)
    return jnp.concatenate(
        [array[t, pl.ds(row, FIELDS, stride=spread), :] for t in tiles], axis=1
    )


def learn_line(row, line, strain, learned, spread, cols, weights, hidden, inputs):
    for at, size in pieces_of(cols):
        x = widened(gathered(strain, row, spread, at, size))
        keep = None
        if line is not None:
            where = line * cols + at
            if not isinstance(where, int):
                where = pl.multiple_of(where, LANES)
            inputs[:, pl.ds(where, size)] = x

            def keep(k, h, where=where, size=size):
                hidden[k, :, pl.ds(where, size)] = h

        out = learn(x, *weights, keep)
        for n in range(size // LANES):
            piece = out[:, n * LANES : (n + 1) * LANES]
            learned[at // LANES + n, pl.ds(row, FIELDS, stride=spread), :] = piece


def learn_rims(rows, strain, learned, spread, cols, weights):
    rim = cols // LANES
    x = [strain[rim, pl.ds(row, FIELDS, stride=spread), :] for row in rows]
    out = learn(widened(jnp.concatenate(x, axis=1)), *weights)
    for n, row in enumerate(rows):
        learned[rim, pl.ds(row, FIELDS, stride=spread), :] = out[:, n * LANES : (n + 1) * LANES]


def inner_kernel(
    fields, w_first, w_mid, w_last, learned, hidden, inputs, before, after, strain
):
    rows, wide = fields.shape[1], fields.shape[2]
    tiles = wide // LANES
    cols = wide - LANES
    lane = lax.broadcasted_iota(jnp.int32, (rows, LANES), 1)
    first, final = lane == 0, lane == LANES - 1

    def set_up(tile, carry):
        at = lanes_of(tile)
        for c in range(3):
            value = fields[c, :, at]
            before[c, :, at] = pltpu.roll(value, 1, 1)
            after[c, :, at] = pltpu.roll(value, LANES - 1, 1)
        return carry

    lax.fori_loop(0, tiles, set_up, 0)

    def strains(tile, carry):
        at = lanes_of(tile)
        e = spread_strains(*triples_of(fields.at[0:3], before, after, tile, tiles, first, final))
        for n in range(FIELDS):
            value = HALVING[n] * e[n] if n < 6 else jnp.zeros((rows, LANES), jnp.float32)
            strain[tile, n * rows : (n + 1) * rows] = value
        return carry

    lax.fori_loop(0, tiles, strains, 0)
    weights = (w_first, w_mid, w_last)

    def line(row, carry):
        learn_line(row, row - 1, strain, learned, rows, cols, weights, hidden, inputs)
        return carry

    lax.fori_loop(1, rows - 1, line, 0)
    learn_rims(range(1, rows - 1), strain, learned, rows, cols, weights)


def outer_kernel(
    table, fields, up, down, fl_up, fl_down, inner, w_first, w_mid, w_last,
    residual, own_residual, stiff, support, hidden, inputs,
    centre, before, after, ahead, behind, middle, strain, learned,
):
    layups = table.shape[0] // 36
    rows, wide = fields.shape[1], fields.shape[2]
    tiles = wide // LANES
    cols = wide - LANES
    tall = 3 * rows
    halo = fl_up.shape[1]
    lane = lax.broadcasted_iota(jnp.int32, (tall, LANES), 1)
    first, final = lane == 0, lane == LANES - 1
    depth = 1
    while (1 << depth) < layups:
        depth += 1
    rim = jnp.zeros((rows - MARGIN, LANES), jnp.float32)
    edge = jnp.zeros((rows - halo, LANES), jnp.float32)

    def set_up(tile, carry):
        at = lanes_of(tile)
        for c in range(3):
            value = jnp.concatenate(
                [rim, up[c, :, at], fields[c, :, at], down[c, :, at], rim], axis=0
            )
            centre[c, :, at] = value
            before[c, :, at] = pltpu.roll(value, 1, 1)
            after[c, :, at] = pltpu.roll(value, LANES - 1, 1)
        around = [
            jnp.concatenate(
                [edge, fl_up[c, :, at], fields[3 + c, :, at], fl_down[c, :, at], edge], axis=0
            )
            for c in range(4)
        ]
        for c in range(3):
            support[c, :, at] = around[c]
        ids = around[3].astype(jnp.int32)
        bits = [(ids & (1 << k)) != 0 for k in range(depth)]
        for n, (a, b) in enumerate(UPPER):
            layers = [table[min(l, layups - 1) * 36 + a * 6 + b] for l in range(1 << depth)]
            stiff[n, :, at] = jnp.broadcast_to(chosen(layers, bits), (tall, LANES))
        return carry

    lax.fori_loop(0, tiles, set_up, 0)

    def strains(tile, carry):
        at = lanes_of(tile)
        e = spread_strains(*triples_of(centre, before, after, tile, tiles, first, final))
        for n in range(FIELDS):
            value = HALVING[n] * e[n] if n < 6 else jnp.zeros((tall, LANES), jnp.float32)
            strain[tile, n * tall : (n + 1) * tall] = value
        for n in range(6):
            learned[tile, n * tall + rows + 1 : n * tall + 2 * rows - 1] = inner[
                tile, n * rows + 1 : (n + 1) * rows - 1
            ]
        return carry

    lax.fori_loop(0, tiles, strains, 0)
    weights = (w_first, w_mid, w_last)
    rim_rows = (rows - 1, rows, 2 * rows - 1, 2 * rows)
    for row, line in zip(rim_rows, (None, 0, 1, None)):
        learn_line(row, line, strain, learned, tall, cols, weights, hidden, inputs)
    learn_rims(rim_rows, strain, learned, tall, cols, weights)

    def push(tile, carry):
        at = lanes_of(tile)
        e = [strain[tile, n * tall : (n + 1) * tall] * (1.0 / HALVING[n]) for n in range(6)]
        s = mixed([stiff[n, :, at] for n in range(len(UPPER))], e)
        s = [s[n] + HALVING[n] * learned[tile, n * tall : (n + 1) * tall] for n in range(6)]
        for c, (alpha, beta, gamma) in enumerate(spread_forces(s)):
            ahead[c, :, at] = pltpu.roll(alpha, 1, 1)
            behind[c, :, at] = pltpu.roll(beta, LANES - 1, 1)
            middle[c, :, at] = gamma
        return carry

    lax.fori_loop(0, tiles, push, 0)
    own = slice(rows, 2 * rows)

    def finish(tile, carry):
        at = lanes_of(tile)
        left, right = beside(tile, tiles)
        at_left, at_right = lanes_of(left), lanes_of(right)
        for c in range(3):
            value = (
                middle[c, own, at]
                + jnp.where(first[:rows], ahead[c, own, at_left], ahead[c, own, at])
                + jnp.where(final[:rows], behind[c, own, at_right], behind[c, own, at])
            )
            value = value + fields[3 + c, :, at] * fields[c, :, at] - fields[7 + c, :, at]
            residual[c, :, at] = value
            if carry is not None:
                own_residual[c, :, at] = value
        return carry

    lax.fori_loop(0, tiles - 1, finish, 0)
    finish(tiles - 1, None)


def outer(left, right):
    return lax.dot_general(
        left, right, (((1,), (1,)), ((), ())), preferred_element_type=jnp.float32
    )


def slope_of(signal, h):
    h = h.astype(jnp.float32)
    return (signal * (1.0 - h * h)).astype(jnp.bfloat16)


def backward_kernel(
    upstream, inner_hidden, inner_inputs, outer_hidden, outer_inputs, w_mid_t, w_last_t,
    packed, grads,
):
    layers = w_mid_t.shape[0]
    hid = w_mid_t.shape[1]
    cols = upstream.shape[0] * LANES
    rows = upstream.shape[1] // FIELDS
    last_at = layers * hid
    first_at = last_at + FIELDS
    grads[...] = jnp.zeros_like(grads)

    def line(row, at_line, hidden, inputs):
        for at, size in pieces_of(cols):
            where = at_line * cols + at
            if not isinstance(where, int):
                where = pl.multiple_of(where, LANES)
            here = pl.ds(where, size)
            signal = widened(gathered(upstream, row, rows, at, size))
            h = hidden[layers, :, here]
            grads[last_at : last_at + FIELDS] += outer(signal, h)[:FIELDS]
            d = slope_of(product(w_last_t[...], signal), h)
            for k in range(layers - 1, -1, -1):
                h = hidden[k, :, here]
                grads[k * hid : (k + 1) * hid] += outer(d, h)
                d = slope_of(product(w_mid_t[k], d), h)
            grads[first_at : first_at + FIELDS] += outer(inputs[:, here], d)[:FIELDS]

    def inside(row, carry):
        line(row, row - 1, inner_hidden, inner_inputs)
        return carry

    lax.fori_loop(1, rows - 1, inside, 0)
    line(0, 0, outer_hidden, outer_inputs)
    line(rows - 1, 1, outer_hidden, outer_inputs)
    chunk = packed.shape[1]
    for n in range(packed.shape[0]):
        packed[n] = grads[n * chunk : (n + 1) * chunk]


def gather_kernel(parts, total):
    total[...] = jnp.broadcast_to(jnp.sum(parts[...], axis=0, keepdims=True), total.shape)


def deliver_kernel(parts, grad_first, grad_mid, grad_last, flat):
    chunk = parts.shape[1]
    for n in range(parts.shape[0]):
        flat[n * chunk : (n + 1) * chunk] = parts[n]
    layers, hid = grad_mid.shape[0], grad_mid.shape[1]
    for k in range(layers):
        grad_mid[k] = flat[k * hid : (k + 1) * hid]
    at = layers * hid
    grad_last[...] = flat[at : at + FIELDS][: grad_last.shape[0]]
    grad_first[...] = flat[at + FIELDS : at + 2 * FIELDS].T[:, : grad_first.shape[1]]


def krylov_kernel(
    numbers, r_mid, r_up, r_down, stiff, support, basis, sums,
    before, after, ahead, behind, middle,
):
    rows = r_mid.shape[1]
    wide = r_mid.shape[2]
    tiles = wide // LANES
    own_tiles = tiles - 1
    tall = 3 * rows
    lane = lax.broadcasted_iota(jnp.int32, (tall, LANES), 1)
    first, final = lane == 0, lane == LANES - 1
    def place(k, c, at, value):
        basis[k, c, :, at] = value
        before[c, :, at] = pltpu.roll(value, 1, 1)
        after[c, :, at] = pltpu.roll(value, LANES - 1, 1)

    def set_up(tile, carry):
        at = lanes_of(tile)
        for c in range(3):
            value = jnp.concatenate([r_up[c, :, at], r_mid[c, :, at], r_down[c, :, at]], axis=0)
            place(0, c, at, value)
        return carry

    lax.fori_loop(0, tiles, set_up, 0)

    def strain_of(k, tile):
        return spread_strains(*triples_of(basis.at[k], before, after, tile, tiles, first, final))

    def stress_of(e, at):
        return mixed([stiff[n, :, at] for n in range(len(UPPER))], e)

    def mine(value):
        return value[rows : 2 * rows]

    zero = jnp.zeros((rows, LANES), jnp.float32)
    totals = [None] * SUMS

    for k in range(DEGREE):
        def push(tile, carry, k=k):
            at = lanes_of(tile)
            for c, (alpha, beta, gamma) in enumerate(
                spread_forces(stress_of(strain_of(k, tile), at))
            ):
                ahead[c, :, at] = pltpu.roll(alpha, 1, 1)
                behind[c, :, at] = pltpu.roll(beta, LANES - 1, 1)
                middle[c, :, at] = gamma
            return carry

        lax.fori_loop(0, tiles, push, 0)

        centre, width, inverse = numbers[k], numbers[3 + k], numbers[6 + k]
        former = numbers[2 + k]

        def advance(tile, carry, k=k):
            at = lanes_of(tile)
            left, right = beside(tile, tiles)
            at_left, at_right = lanes_of(left), lanes_of(right)
            image, here, following = [], [], []
            for c in range(3):
                vector = basis[k, c, :, at]
                value = (
                    middle[c, :, at]
                    + jnp.where(first, ahead[c, :, at_left], ahead[c, :, at])
                    + jnp.where(final, behind[c, :, at_right], behind[c, :, at])
                    + support[c, :, at] * vector
                )
                step = value - centre * vector
                if k:
                    step = step - former * basis[k - 1, c, :, at]
                step = step * inverse
                place(k + 1, c, at, step)
                image.append(mine(value))
                here.append(mine(vector))
                following.append(mine(step))
            if carry is None:
                return None

            def dot(left_side, right_side):
                return (
                    left_side[0] * right_side[0]
                    + left_side[1] * right_side[1]
                    + left_side[2] * right_side[2]
                )

            def old(m):
                return [basis[m, c, rows : 2 * rows, at] for c in range(3)]

            fresh = []
            origin = here if k == 0 else old(0)
            if k == 0:
                fresh.append(dot(here, here))
            fresh.append(dot(origin, following))
            for j in range(k + 1):
                fresh.append(dot(here if j == k else (origin if j == 0 else old(j)), image))
            if k == DEGREE - 1:
                fresh.append(dot(old(1), following))
                fresh.append(dot(here, following))
                fresh.append(dot(following, following))
            return tuple(p + q for p, q in zip(carry, fresh))

        names = ([0] if k == 0 else []) + [k + 1] + [4 + k * (k + 1) // 2 + j for j in range(k + 1)]
        if k == DEGREE - 1:
            names += [10, 11, 12]
        found = lax.fori_loop(0, own_tiles, advance, (zero,) * len(names))
        advance(own_tiles, None)
        for name, value in zip(names, found):
            totals[name] = value

    def energy(tile, running):
        at = lanes_of(tile)
        e = strain_of(DEGREE, tile)
        e = [mine(value) for value in e]
        for n, (a, b) in enumerate(UPPER):
            term = stiff[n, rows : 2 * rows, at] * e[b] * e[a]
            running = running + (term if a == b else 2.0 * term)
        for c in range(3):
            vector = basis[DEGREE, c, rows : 2 * rows, at]
            running = running + support[c, rows : 2 * rows, at] * vector * vector
        return running

    totals[13] = lax.fori_loop(0, own_tiles, energy, zero)
    place_of = lax.broadcasted_iota(jnp.int32, (1, LANES), 1)
    line = jnp.zeros((1, LANES), jnp.float32)
    for n in range(SUMS):
        total = jnp.sum(jnp.sum(totals[n], axis=0, keepdims=True), axis=1, keepdims=True)
        line = jnp.where(place_of == n, jnp.broadcast_to(total, (1, LANES)), line)
    sums[...] = jnp.broadcast_to(line[None], sums.shape)


def solve_kernel(numbers, sums, basis, adjoint, upstream, combined):
    rows = adjoint.shape[1]
    wide = basis.shape[3]
    tiles = wide // LANES
    own_tiles = tiles - 1
    tall = 3 * rows
    line = jnp.sum(sums[...], axis=0)
    picks = [jnp.broadcast_to(line[:, n : n + 1], (1, LANES)) for n in range(SUMS)]
    centre = [numbers[k] for k in range(3)]
    width = [numbers[3 + k] for k in range(3)]
    matrix = [[None] * 4 for _ in range(4)]
    for k in range(3):
        for j in range(k + 1):
            matrix[j][k] = picks[4 + k * (k + 1) // 2 + j]
    cross = [picks[3], picks[10], picks[11], picks[12]]
    for j in range(3):
        value = width[j] * cross[j + 1] + centre[j] * cross[j]
        matrix[j][3] = value + width[j - 1] * cross[j - 1] if j else value
    matrix[3][3] = picks[13]
    weights = [jnp.broadcast_to(x, (tall, LANES)) for x in galerkin(matrix, picks[:4])]

    def combine(tile, carry):
        at = lanes_of(tile)
        for c in range(3):
            value = weights[0] * basis[0, c, :, at]
            for k in range(1, DEGREE + 1):
                value = value + weights[k] * basis[k, c, :, at]
            combined[c, :, at] = value
            combined[3 + c, :, at] = pltpu.roll(value, 1, 1)
            combined[6 + c, :, at] = pltpu.roll(value, LANES - 1, 1)
        return carry

    lax.fori_loop(0, tiles, combine, 0)
    lane = lax.broadcasted_iota(jnp.int32, (tall, LANES), 1)
    first, final = lane == 0, lane == LANES - 1

    def strain(tile, carry):
        at = lanes_of(tile)
        triples = triples_of(
            combined.at[0:3], combined.at[3:6], combined.at[6:9], tile, tiles, first, final
        )
        for c in range(3):
            adjoint[c, :, at] = combined[c, rows : 2 * rows, at]
        for n, value in enumerate(spread_strains(*triples)):
            upstream[tile, n * rows : (n + 1) * rows] = HALVING[n] * value[rows : 2 * rows]
        for n in range(6, FIELDS):
            upstream[tile, n * rows : (n + 1) * rows] = jnp.zeros((rows, LANES), jnp.float32)
        return carry

    lax.fori_loop(0, own_tiles, strain, 0)


def basis_constants(layup_stiffness):
    bending = 0.5 * (jnp.mean(layup_stiffness[:, 3, 3]) + jnp.mean(layup_stiffness[:, 4, 4]))
    centres = [11.5 * bending + 1.1, 9.8 * bending + 1.1, 8.4 * bending + 1.1]
    widths = [3.9 * bending + 0.4, 5.6 * bending + 0.4, 4.8 * bending + 0.4]
    return centres, widths


ON_CHIP = pl.BlockSpec(memory_space=pltpu.VMEM)
SCALARS = pl.BlockSpec(memory_space=pltpu.SMEM)


def kernel_call(body, name, scalars, outs, scratch, *operands):
    return pl.pallas_call(
        body,
        name=name,
        in_specs=[SCALARS] * scalars + [ON_CHIP] * (len(operands) - scalars),
        out_specs=[ON_CHIP] * len(outs),
        out_shape=[jax.ShapeDtypeStruct(*out) for out in outs],
        scratch_shapes=[pltpu.VMEM(*s) for s in scratch],
        compiler_params=pltpu.CompilerParams(vmem_limit_bytes=LIMITS[name] << 20),
    )(*operands)


LIMITS = {"inner": 8, "outer": 14, "krylov": 10, "solve": 10, "backward": 8, "gather": 4, "deliver": 4}


def per_device(displacement, load, foundation, layup, layup_stiffness, w_first, w_mid, w_last):
    f32, bf16 = jnp.float32, jnp.bfloat16
    rows, cols = layup.shape
    layers, hid = w_mid.shape[0], w_mid.shape[1]
    devices = lax.axis_size("patch") * lax.axis_size("sub")
    wide = cols + LANES
    tall = 3 * rows
    tiles = wide // LANES
    fields = jnp.concatenate([displacement, foundation, layup.astype(f32)[None], load])
    before, after = from_both(fields, "sub", 2, HY)
    gap = jnp.zeros(fields.shape[:2] + (LANES - 2 * HY,), f32)
    fields = jnp.concatenate([fields, after, gap, before], axis=2)
    up, down = from_both(fields[:3], "patch", 1, MARGIN)
    fl_up, fl_down = from_both(fields[3:7], "patch", 1, 6)

    halving = jnp.array(HALVING, f32)
    table = (layup_stiffness * halving[:, None] * halving[None, :]).reshape(-1)
    centres, widths = basis_constants(layup_stiffness)
    numbers = jnp.stack(centres + widths + [1.0 / x for x in widths])
    thin = w_first.shape[1]
    first_pad = jnp.pad(w_first, ((0, 0), (0, PADDED - thin)))
    last_pad = jnp.pad(w_last, ((0, PADDED - thin), (0, 0)))
    mid_t, last_t = jnp.swapaxes(w_mid, 1, 2), last_pad.T

    learned, inner_hidden, inner_inputs = kernel_call(
        inner_kernel, "inner", 0,
        [((tiles, FIELDS * rows, LANES), f32), ((layers + 1, hid, (rows - 2) * cols), bf16),
         ((PADDED, (rows - 2) * cols), bf16)],
        [((3, rows, wide), f32)] * 2 + [((tiles, FIELDS * rows, LANES), f32)],
        fields, first_pad, w_mid, last_pad,
    )
    wide_residual, residual, stiff, support, outer_hidden, outer_inputs = kernel_call(
        outer_kernel, "outer", 1,
        [((3, rows, wide), f32), ((3, rows, cols), f32), ((len(UPPER), tall, wide), f32),
         ((3, tall, wide), f32), ((layers + 1, hid, 2 * cols), bf16), ((PADDED, 2 * cols), bf16)],
        [((3, tall, wide), f32)] * 6 + [((tiles, FIELDS * tall, LANES), f32)] * 2,
        table, fields, up, down, fl_up, fl_down, learned, first_pad, w_mid, last_pad,
    )
    up, down = from_both(wide_residual, "patch", 1, rows)
    basis, sums = kernel_call(
        krylov_kernel, "krylov", 1,
        [((DEGREE + 1, 3, tall, wide), f32), ((devices, 1, LANES), f32)],
        [((3, tall, wide), f32)] * 5,
        numbers, wide_residual, up, down, stiff, support,
    )
    sums = everyone(sums)
    adjoint, upstream = kernel_call(
        solve_kernel, "solve", 1,
        [((3, rows, cols), f32), ((tiles - 1, FIELDS * rows, LANES), f32)],
        [((9, tall, wide), f32)],
        numbers, sums, basis,
    )
    count = layers * hid + 2 * FIELDS
    chunk = -(-count // devices)
    (packed,) = kernel_call(
        backward_kernel, "backward", 0,
        [((devices, chunk, LANES), f32)],
        [((devices * chunk, LANES), f32)],
        upstream, inner_hidden, inner_inputs, outer_hidden, outer_inputs, mid_t, last_t,
    )
    (total,) = kernel_call(
        gather_kernel, "gather", 0, [(packed.shape, f32)], [], everyone(packed)
    )
    grad_first, grad_mid, grad_last = kernel_call(
        deliver_kernel, "deliver", 0,
        [(w_first.shape, f32), (w_mid.shape, f32), (w_last.shape, f32)],
        [((devices * chunk, LANES), f32)],
        everyone(total),
    )
    return residual, adjoint, grad_first, grad_mid, grad_last


def solution(mesh):
    field = P(None, "patch", "sub")
    return jax.shard_map(
        per_device,
        mesh=mesh,
        in_specs=(field, field, field, P("patch", "sub"), P(), P(), P(), P()),
        out_specs=(field, field, P(), P(), P()),
        check_vma=False,
    )
```

time: 142 us -> 149 us (1.049)
  Pallas kernels: 18.8 us -> 59.1 us
  matrix products: 31.6 us -> 0 us
  waiting for transfers between devices: 17.9 us -> 12.8 us
  other arithmetic: 6.81 us -> 2.79 us
  local copies, waits for them, and re-layouts: 22.2 us -> 25.7 us
  blocking collectives: 22 us -> 25 us
  starting transfers between devices: 19.1 us -> 20.8 us
    pallas_call x2 -> x7, Pallas kernels: 18.8 us -> 59.1 us  [kernel_call(): pl.pallas_call(body, name=name, in_specs=[SCALARS] * scalars + [ON_CHIP]...]
    dot_general x17 -> x0, matrix products: 31.6 us -> none  [the longest x5 10.8 us: outer_product(): lax.dot_general(left, right, (((1,), (1,)), ((), ())), preferred_element_...]
    unnamed x45 -> x43, local copies, waits for them, and re-layouts: 10.1 us -> 25.2 us
    slice x14 -> x2, local copies, waits for them, and re-layouts: 6.38 us -> 0.07 us  [from_both(): head = lax.slice_in_dim(array, 0, width, axis=dim)]
    ppermute x4, waiting for transfers between devices: 7.23 us -> 3.22 us  [from_both(): before = lax.ppermute(tail, axis, ring(axis, 1))]
    all_to_all x2, blocking collectives: 22 us -> 25 us  [everyone(): return lax.all_to_all(rows, AXES, 0, 0, tiled=True)]
    all_to_all x1, waiting for transfers between devices: 8.73 us -> 6.95 us  [everyone(): return lax.all_to_all(rows, AXES, 0, 0, tiled=True)]
    concatenate x34 -> x1, local copies, waits for them, and re-layouts: 1.78 us -> 0.1 us  [per_device(): fields = jnp.concatenate([fields, after, gap, before], axis=2)]
  transfers between devices with their start and end apart: 9 -> 9, of which waited for: 5 -> 5; matrix products, arithmetic and copies ran while one was open for 15% -> 1% of each run, Pallas kernels for 0% -> 8%
where the time goes in v1:
time: 149 us; the launch traced here: 148 us
  Pallas kernels  59.1 us (40%)
  local copies, waits for them, and re-layouts  25.7 us (17%)
  blocking collectives  25 us (17%)
  starting transfers between devices  20.8 us (14%)
  waiting for transfers between devices  12.8 us (9%)
  other arithmetic  2.79 us (2%)
  between operations  2.23 us (1%)
    pallas_call x7, Pallas kernels, kernel_call(): pl.pallas_call(body, name=name, in_specs=[SCALARS] * scalars + [ON_CHIP]...  59.1 us
    unnamed x43, local copies, waits for them, and re-layouts  25.2 us
    all_to_all x2, blocking collectives, everyone(): return lax.all_to_all(rows, AXES, 0, 0, tiled=True)  25 us
    ppermute x4, starting transfers between devices, from_both(): after = lax.ppermute(head, axis, ring(axis, -1))  15.1 us
    all_to_all x1, waiting for transfers between devices, everyone(): return lax.all_to_all(rows, AXES, 0, 0, tiled=True)  6.95 us
    all_to_all x1, starting transfers between devices, everyone(): return lax.all_to_all(rows, AXES, 0, 0, tiled=True)  4.16 us
    ppermute x4, waiting for transfers between devices, from_both(): before = lax.ppermute(tail, axis, ring(axis, 1))  3.22 us
  transfers between devices with their start and end apart: 9, of which 5 were waited for; matrix products, arithmetic and copies ran while one was open for 1% of the time, Pallas kernels for 8%

profile of v1, /device:TPU:0, one launch (start us, length us, event | category | flops | bytes accessed | tf_op | source)
XLA Modules:
  0.0 148.4 jit_solution(9770009614343004045)
XLA Ops:
  0.6 0.0 copy-start.18
  0.6 0.0 copy-start.15
  0.7 0.0 copy-start.16
  0.7 0.0 copy-start.17
  0.7 0.0 copy-start.6
  0.7 0.9 convert_bitcast_fusion
  1.6 1.2 pad_maximum_fusion
  2.7 0.1 fusion.2
  2.8 2.4 %collective-permute-start = (f32[10,8,16]{2,1,0:T(8,128)S(1)}, f32[10,8,16]{2,1,0:T(8,128)S(1)}, u32[]{:S(2)}, u32[]{:S(2)}) collective-permute-start(f32[10,8,16]{2,1,0:T(8,128)S(1)} %get-tuple-element.54), channel_id=1, source_target_pairs={{0,3},{1,0},{2,1},{3,2},{4,7},{5,4},{6,5},{7,6},{8,11},{9,8},{10,9... | collective-permute-start | bytes 15368 | tf_op jit(solution)/shard_map/ppermute | solution.py:23
  5.3 0.0 collective-permute-start.1
  5.3 1.9 %collective-permute-done = f32[10,8,16]{2,1,0:T(8,128)S(1)} collective-permute-done((f32[10,8,16]{2,1,0:T(8,128)S(1)}, f32[10,8,16]{2,1,0:T(8,128)S(1)}, u32[]{:S(2)}, u32[]{:S(2)}) %collective-permute-start) | collective-permute-done | bytes 5152 | tf_op jit(solution)/shard_map/ppermute | solution.py:23
  7.2 1.5 %collective-permute-done.1 = f32[10,8,16]{2,1,0:T(8,128)S(1)} collective-permute-done((f32[10,8,16]{2,1,0:T(8,128)S(1)}, f32[10,8,16]{2,1,0:T(8,128)S(1)}, u32[]{:S(2)}, u32[]{:S(2)}) %collective-permute-start.1) | collective-permute-done | bytes 5152 | tf_op jit(solution)/shard_map/ppermute | solution.py:22
  8.7 0.1 concatenate.7.fields
  8.9 1.5 %collective-permute-start.4 = (f32[4,6,2176]{2,1,0:T(8,128)S(1)}, f32[4,6,2176]{2,1,0:T(8,128)S(1)}, u32[]{:S(2)}, u32[]{:S(2)}) collective-permute-start(f32[4,6,2176]{2,1,0:T(8,128)S(1)} %get-tuple-element.50), channel_id=1, source_target_pairs={{0,4},{4,8},{8,12},{12,16},{16,20},{20,24},{24,28},{28,0},{1,5},{5... | collective-permute-start | bytes 626696 | tf_op jit(solution)/shard_map/ppermute | solution.py:22
  10.4 3.2 %collective-permute-start.5 = (f32[4,6,2176]{2,1,0:T(8,128)S(1)}, f32[4,6,2176]{2,1,0:T(8,128)S(1)}, u32[]{:S(2)}, u32[]{:S(2)}) collective-permute-start(f32[4,6,2176]{2,1,0:T(8,128)S(1)} %get-tuple-element.49), channel_id=1, source_target_pairs={{0,28},{4,0},{8,4},{12,8},{16,12},{20,16},{24,20},{28,24},{1,29},{... | collective-permute-start | bytes 626696 | tf_op jit(solution)/shard_map/ppermute | solution.py:23
  13.6 0.0 collective-permute-start.2
  13.7 4.7 %collective-permute-start.3 = (f32[3,2,2176]{2,1,0:T(2,128)S(1)}, f32[3,2,2176]{2,1,0:T(2,128)S(1)}, u32[]{:S(2)}, u32[]{:S(2)}) collective-permute-start(f32[3,2,2176]{2,1,0:T(2,128)S(1)} %get-tuple-element.51), channel_id=1, source_target_pairs={{0,28},{4,0},{8,4},{12,8},{16,12},{20,16},{24,20},{28,24},{1,29},{... | collective-permute-start | bytes 156680 | tf_op jit(solution)/shard_map/ppermute | solution.py:23
  18.4 0.0 copy-done.18
  18.4 0.0 copy-done.15
  18.4 0.1 multiply_multiply_fusion
  18.5 0.0 copy-done.16
  18.5 0.1 copy.22
  18.6 0.1 copy.27
  18.7 0.0 copy-done.17
  18.7 0.2 copy.21
  18.9 0.1 reshape.15.table
  19.0 0.0 copy-done.6
  19.0 11.8 %inner.1 = (f32[17,64,128]{2,1,0:T(8,128)S(1)}, bf16[4,128,12288]{2,1,0:T(8,128)(2,1)S(1)}, bf16[16,12288]{1,0:T(8,128)(2,1)S(1)}) custom-call(f32[10,8,2176]{2,1,0:T(8,128)S(1)} %concatenate.7.fields, bf16[128,16]{1,0:T(8,128)(2,1)S(1)} %pad.8.w_first, bf16[3,128,128]{2,1,0:T(8,128)(2,1)S(1)} %copy-done.6, bf16[16,128]{1,0:T(8,128)(2,1)S(1)} %pad.9.clone.w_last), custom_call_target="tpu_custom_call" | custom-call | tf_op jit(solution)/shard_map/inner/pallas_call | solution.py:612
  30.8 4.5 %copy-done = bf16[4,128,12288]{2,1,0:T(8,128)(2,1)} copy-done((bf16[4,128,12288]{2,1,0:T(8,128)(2,1)}, bf16[4,128,12288]{2,1,0:T(8,128)(2,1)S(1)}, u32[]{:S(2)}) %copy-start) | copy-done | bytes 12582936
  35.3 0.8 copy-done.7
  36.1 0.0 collective-permute-done.2.up
  36.1 0.0 collective-permute-done.3.down
  36.1 0.0 collective-permute-done.4.fl_up
  36.1 0.0 collective-permute-done.5.fl_down
  36.1 14.0 %outer.1 = (f32[3,8,2176]{2,1,0:T(8,128)S(1)}, f32[3,8,2048]{2,1,0:T(8,128)}, f32[21,24,2176]{2,1,0:T(8,128)S(1)}, f32[3,24,2176]{2,1,0:T(8,128)S(1)}, bf16[4,12...) custom-call(f32[288]{0:T(512)S(1)} %reshape.15.table, f32[10,8,2176]{2,1,0:T(8,128)S(1)} %concatenate.7.fields, ...), custom_call_target="tpu_custom_call" | custom-call | tf_op jit(solution)/shard_map/outer/pallas_call | solution.py:612
  50.1 2.0 %copy-done.2 = f32[21,24,2176]{2,1,0:T(8,128)} copy-done((f32[21,24,2176]{2,1,0:T(8,128)}, f32[21,24,2176]{2,1,0:T(8,128)S(1)}, u32[]{:S(2)}) %copy-start.2) | copy-done | bytes 4386840
  52.1 2.0 %copy-done.4 = bf16[4,128,4096]{2,1,0:T(8,128)(2,1)} copy-done((bf16[4,128,4096]{2,1,0:T(8,128)(2,1)}, bf16[4,128,4096]{2,1,0:T(8,128)(2,1)S(1)}, u32[]{:S(2)}) %copy-start.4) | copy-done | bytes 4194328
  54.1 0.7 copy-done.13
  54.7 0.0 collective-permute-start.6
  54.7 4.7 %collective-permute-start.7 = (f32[3,8,2176]{2,1,0:T(8,128)S(1)}, f32[3,8,2176]{2,1,0:T(8,128)S(1)}, u32[]{:S(2)}, u32[]{:S(2)}) collective-permute-start(f32[3,8,2176]{2,1,0:T(8,128)S(1)} %get-tuple-element.23.r_mid), channel_id=1, source_target_pairs={{0,28},{4,0},{8,4},{12,8},{16,12},{20,16},{24,20},{28,24},{1,29},{... | collective-permute-start | bytes 626696 | tf_op jit(solution)/shard_map/ppermute | solution.py:23
  59.4 0.7 slice_reduce_fusion
  61.5 0.1 stack.39.numbers
  61.6 1.7 %collective-permute-done.6.r_up = f32[3,8,2176]{2,1,0:T(8,128)S(1)} collective-permute-done((f32[3,8,2176]{2,1,0:T(8,128)S(1)}, f32[3,8,2176]{2,1,0:T(8,128)S(1)}, u32[]{:S(2)}, u32[]{:S(2)}) %collective-permute-start.6) | collective-permute-done | bytes 208928 | tf_op jit(solution)/shard_map/ppermute | solution.py:22
  63.3 0.7 copy-done.9
  64.0 0.7 collective-permute-done.7.r_down
  64.7 0.7 copy-done.11
  65.4 2.2 %copy-done.3 = f32[21,24,2176]{2,1,0:T(8,128)S(1)} copy-done((f32[21,24,2176]{2,1,0:T(8,128)S(1)}, f32[21,24,2176]{2,1,0:T(8,128)}, u32[]{:S(2)}) %copy-start.3) | copy-done | bytes 4386840
  67.6 0.9 copy-done.10
  68.6 0.9 copy-done.12
  69.5 15.9 %krylov.1 = (f32[4,3,24,2176]{3,2,1,0:T(8,128)S(1)}, f32[32,1,128]{2,1,0:T(1,128)}) custom-call(f32[9]{0:T(128)S(1)} %stack.39.numbers, f32[3,8,2176]{2,1,0:T(8,128)S(1)} %get-tuple-element.23.r_mid, f32[3,8,2176]{2,1,0:T(8,128)S(1)} %copy-done.10, f32[3,8,2176]{2,1,0:T(8,128)S(1)} %copy-done.12, f32[21,24,2176]{2,1,0:T(8,128)S(1)} %copy-done.3, ...), custom_call_target="tpu_custom_call" | custom-call | tf_op jit(solution)/shard_map/krylov/pallas_call | solution.py:612
  85.4 4.2 %all-to-all-start = ((f32[32,1,128]{2,1,0:T(1,128)}), f32[32,1,128]{2,1,0:T(1,128)S(1)}, u32[]{:S(2)}, u32[]{:S(2)}) async-start(f32[32,1,128]{2,1,0:T(1,128)} %get-tuple-element.26), calls=%async_computation | async-start | bytes 32768 | tf_op jit(solution)/shard_map/all_to_all | solution.py:28
  89.5 0.1 copy.25
  89.7 7.0 %all-to-all-done.sums = f32[32,1,128]{2,1,0:T(1,128)S(1)} async-done(((f32[32,1,128]{2,1,0:T(1,128)}), f32[32,1,128]{2,1,0:T(1,128)S(1)}, u32[]{:S(2)}, u32[]{:S(2)}) %all-to-all-start) | async-done | bytes 16416 | tf_op jit(solution)/shard_map/all_to_all | solution.py:28
  96.6 3.3 %solve.1 = (f32[3,8,2048]{2,1,0:T(8,128)}, f32[16,64,128]{2,1,0:T(8,128)S(1)}) custom-call(f32[9]{0:T(128)S(1)} %stack.39.numbers, f32[32,1,128]{2,1,0:T(1,128)S(1)} %all-to-all-done.sums, f32[4,3,24,2176]{3,2,1,0:T(8,128)S(1)} %get-tuple-element.27.basis), custom_call_target="tpu_custom_call" | custom-call | tf_op jit(solution)/shard_map/solve/pallas_call | solution.py:612
  100.0 4.6 %copy-done.1 = bf16[4,128,12288]{2,1,0:T(8,128)(2,1)S(1)} copy-done((bf16[4,128,12288]{2,1,0:T(8,128)(2,1)S(1)}, bf16[4,128,12288]{2,1,0:T(8,128)(2,1)}, u32[]{:S(2)}) %copy-start.1) | copy-done | bytes 12582936
  104.5 2.2 %copy-done.5 = bf16[4,128,4096]{2,1,0:T(8,128)(2,1)S(1)} copy-done((bf16[4,128,4096]{2,1,0:T(8,128)(2,1)S(1)}, bf16[4,128,4096]{2,1,0:T(8,128)(2,1)}, u32[]{:S(2)}) %copy-start.5) | copy-done | bytes 4194328
  106.7 1.0 copy-done.8
  107.7 0.9 copy-done.14
  108.6 13.4 %backward.1 = f32[32,13,128]{2,1,0:T(8,128)S(1)} custom-call(f32[16,64,128]{2,1,0:T(8,128)S(1)} %get-tuple-element.29.upstream, bf16[4,128,12288]{2,1,0:T(8,128)(2,1)S(1)} %copy-done.1, bf16[16,12288]{1,0:T(8,128)(2,1)S(1)} %copy-done.8, bf16[4,128,4096]{2,1,0:T(8,128)(2,1)S(1)} %copy-done.5, bf16[16,4096]{1,0:T(8,128)(2,1)S(1)} %copy-done.14, ...), custom_call_target="tpu_custom_call" | custom-call | tf_op jit(solution)/shard_map/backward/pallas_call | solution.py:612
  122.0 12.3 %all_to_all.15.parts = f32[32,13,128]{2,1,0:T(8,128)S(1)} all-to-all(f32[32,13,128]{2,1,0:T(8,128)S(1)} %backward.1), channel_id=1, replica_groups=mesh['patch'=8,'sub'=4] {'patch','sub'}, dimensions={0} | all-to-all | bytes 425984 | tf_op jit(solution)/shard_map/all_to_all | solution.py:28
  134.3 0.1 gather.1
  134.3 12.7 %all_to_all.16.parts = f32[32,13,128]{2,1,0:T(8,128)S(1)} all-to-all(f32[32,13,128]{2,1,0:T(8,128)S(1)} %gather.1), channel_id=1, replica_groups=mesh['patch'=8,'sub'=4] {'patch','sub'}, dimensions={0} | all-to-all | bytes 425984 | tf_op jit(solution)/shard_map/all_to_all | solution.py:28
  147.0 0.7 deliver.1
  147.7 0.7 copy.26
  (21 shorter events, 0.1 us)
Async XLA Ops:
  0.6 17.7 %copy-start.18 = (f32[6]{0:T(128)S(1)}, f32[6]{0:T(128)}, u32[]{:S(2)}) copy-start(f32[6]{0:T(128)} %constant.42.clone) | copy-start | bytes 76
  0.6 17.7 %copy-start.15 = (f32[8,6,6]{2,0,1:T(8,128)S(1)}, f32[8,6,6]{2,0,1:T(8,128)}, u32[]{:S(2)}) copy-start(f32[8,6,6]{2,0,1:T(8,128)} %param.13) | copy-start | bytes 3460
  0.7 17.8 %copy-start.16 = (bf16[6,128]{1,0:T(8,128)(2,1)S(1)}, bf16[6,128]{1,0:T(8,128)(2,1)}, u32[]{:S(2)}) copy-start(bf16[6,128]{1,0:T(8,128)(2,1)} %param.16) | copy-start | bytes 4612
  0.7 18.0 %copy-start.17 = (bf16[128,6]{0,1:T(8,128)(2,1)S(1)}, bf16[128,6]{0,1:T(8,128)(2,1)}, u32[]{:S(2)}) copy-start(bf16[128,6]{0,1:T(8,128)(2,1)} %param.14) | copy-start | bytes 4612
  0.7 18.3 %copy-start.6 = (bf16[3,128,128]{2,1,0:T(8,128)(2,1)S(1)}, bf16[3,128,128]{2,1,0:T(8,128)(2,1)}, u32[]{:S(2)}) copy-start(bf16[3,128,128]{2,1,0:T(8,128)(2,1)} %w_mid.3) | copy-start | bytes 294916
  2.8 4.3 %collective-permute-start = (f32[10,8,16]{2,1,0:T(8,128)S(1)}, f32[10,8,16]{2,1,0:T(8,128)S(1)}, u32[]{:S(2)}, u32[]{:S(2)}) collective-permute-start(f32[10,8,16]{2,1,0:T(8,128)S(1)} %get-tuple-element.54), channel_id=1, source_target_pairs={{0,3},{1,0},{2,1},{3,2},{4,7},{5,4},{6,5},{7,6},{8,11},{9,8},{10,9... | collective-permute-start | bytes 15368 | tf_op jit(solution)/shard_map/ppermute | solution.py:23
  5.3 3.4 %collective-permute-start.1 = (f32[10,8,16]{2,1,0:T(8,128)S(1)}, f32[10,8,16]{2,1,0:T(8,128)S(1)}, u32[]{:S(2)}, u32[]{:S(2)}) collective-permute-start(f32[10,8,16]{2,1,0:T(8,128)S(1)} %get-tuple-element.53), channel_id=1, source_target_pairs={{0,1},{1,2},{2,3},{3,0},{4,5},{5,6},{6,7},{7,4},{8,9},{9,10},{10,1... | collective-permute-start | bytes 15368 | tf_op jit(solution)/shard_map/ppermute | solution.py:22
  8.9 27.2 %collective-permute-start.4 = (f32[4,6,2176]{2,1,0:T(8,128)S(1)}, f32[4,6,2176]{2,1,0:T(8,128)S(1)}, u32[]{:S(2)}, u32[]{:S(2)}) collective-permute-start(f32[4,6,2176]{2,1,0:T(8,128)S(1)} %get-tuple-element.50), channel_id=1, source_target_pairs={{0,4},{4,8},{8,12},{12,16},{16,20},{20,24},{24,28},{28,0},{1,5},{5... | collective-permute-start | bytes 626696 | tf_op jit(solution)/shard_map/ppermute | solution.py:22
  10.4 25.7 %collective-permute-start.5 = (f32[4,6,2176]{2,1,0:T(8,128)S(1)}, f32[4,6,2176]{2,1,0:T(8,128)S(1)}, u32[]{:S(2)}, u32[]{:S(2)}) collective-permute-start(f32[4,6,2176]{2,1,0:T(8,128)S(1)} %get-tuple-element.49), channel_id=1, source_target_pairs={{0,28},{4,0},{8,4},{12,8},{16,12},{20,16},{24,20},{28,24},{1,29},{... | collective-permute-start | bytes 626696 | tf_op jit(solution)/shard_map/ppermute | solution.py:23
  13.6 22.4 %collective-permute-start.2 = (f32[3,2,2176]{2,1,0:T(2,128)S(1)}, f32[3,2,2176]{2,1,0:T(2,128)S(1)}, u32[]{:S(2)}, u32[]{:S(2)}) collective-permute-start(f32[3,2,2176]{2,1,0:T(2,128)S(1)} %get-tuple-element.52), channel_id=1, source_target_pairs={{0,4},{4,8},{8,12},{12,16},{16,20},{20,24},{24,28},{28,0},{1,5},{5... | collective-permute-start | bytes 156680 | tf_op jit(solution)/shard_map/ppermute | solution.py:22
  13.7 22.4 %collective-permute-start.3 = (f32[3,2,2176]{2,1,0:T(2,128)S(1)}, f32[3,2,2176]{2,1,0:T(2,128)S(1)}, u32[]{:S(2)}, u32[]{:S(2)}) collective-permute-start(f32[3,2,2176]{2,1,0:T(2,128)S(1)} %get-tuple-element.51), channel_id=1, source_target_pairs={{0,28},{4,0},{8,4},{12,8},{16,12},{20,16},{24,20},{28,24},{1,29},{... | collective-permute-start | bytes 156680 | tf_op jit(solution)/shard_map/ppermute | solution.py:23
  30.8 4.5 %copy-start = (bf16[4,128,12288]{2,1,0:T(8,128)(2,1)}, bf16[4,128,12288]{2,1,0:T(8,128)(2,1)S(1)}, u32[]{:S(2)}) copy-start(bf16[4,128,12288]{2,1,0:T(8,128)(2,1)S(1)} %get-tuple-element.30.inner_hidden) | copy-start | bytes 37748740
  35.3 0.8 copy-start.7
  50.1 2.0 %copy-start.2 = (f32[21,24,2176]{2,1,0:T(8,128)}, f32[21,24,2176]{2,1,0:T(8,128)S(1)}, u32[]{:S(2)}) copy-start(f32[21,24,2176]{2,1,0:T(8,128)S(1)} %get-tuple-element.24.stiff) | copy-start | bytes 13160452
  52.1 2.0 %copy-start.4 = (bf16[4,128,4096]{2,1,0:T(8,128)(2,1)}, bf16[4,128,4096]{2,1,0:T(8,128)(2,1)S(1)}, u32[]{:S(2)}) copy-start(bf16[4,128,4096]{2,1,0:T(8,128)(2,1)S(1)} %get-tuple-element.32.outer_hidden) | copy-start | bytes 12582916
  54.1 0.7 copy-start.13
  54.7 8.6 %collective-permute-start.6 = (f32[3,8,2176]{2,1,0:T(8,128)S(1)}, f32[3,8,2176]{2,1,0:T(8,128)S(1)}, u32[]{:S(2)}, u32[]{:S(2)}) collective-permute-start(f32[3,8,2176]{2,1,0:T(8,128)S(1)} %get-tuple-element.23.r_mid), channel_id=1, source_target_pairs={{0,4},{4,8},{8,12},{12,16},{16,20},{20,24},{24,28},{28,0},{1,5},{5... | collective-permute-start | bytes 626696 | tf_op jit(solution)/shard_map/ppermute | solution.py:22
  54.7 10.0 %collective-permute-start.7 = (f32[3,8,2176]{2,1,0:T(8,128)S(1)}, f32[3,8,2176]{2,1,0:T(8,128)S(1)}, u32[]{:S(2)}, u32[]{:S(2)}) collective-permute-start(f32[3,8,2176]{2,1,0:T(8,128)S(1)} %get-tuple-element.23.r_mid), channel_id=1, source_target_pairs={{0,28},{4,0},{8,4},{12,8},{16,12},{20,16},{24,20},{28,24},{1,29},{... | collective-permute-start | bytes 626696 | tf_op jit(solution)/shard_map/ppermute | solution.py:23
  63.3 0.7 copy-start.9
  64.7 0.7 copy-start.11
  65.4 2.2 %copy-start.3 = (f32[21,24,2176]{2,1,0:T(8,128)S(1)}, f32[21,24,2176]{2,1,0:T(8,128)}, u32[]{:S(2)}) copy-start(f32[21,24,2176]{2,1,0:T(8,128)} %copy-done.2) | copy-start | bytes 13160452
  67.6 0.9 copy-start.10
  68.6 0.9 copy-start.12
  85.4 11.3 %all-to-all-start = ((f32[32,1,128]{2,1,0:T(1,128)}), f32[32,1,128]{2,1,0:T(1,128)S(1)}, u32[]{:S(2)}, u32[]{:S(2)}) async-start(f32[32,1,128]{2,1,0:T(1,128)} %get-tuple-element.26), calls=%async_computation | async-start | bytes 32768 | tf_op jit(solution)/shard_map/all_to_all | solution.py:28
  100.0 4.6 %copy-start.1 = (bf16[4,128,12288]{2,1,0:T(8,128)(2,1)S(1)}, bf16[4,128,12288]{2,1,0:T(8,128)(2,1)}, u32[]{:S(2)}) copy-start(bf16[4,128,12288]{2,1,0:T(8,128)(2,1)} %copy-done) | copy-start | bytes 37748740
  104.5 2.2 %copy-start.5 = (bf16[4,128,4096]{2,1,0:T(8,128)(2,1)S(1)}, bf16[4,128,4096]{2,1,0:T(8,128)(2,1)}, u32[]{:S(2)}) copy-start(bf16[4,128,4096]{2,1,0:T(8,128)(2,1)} %copy-done.4) | copy-start | bytes 12582916
  106.7 1.0 copy-start.8
  107.7 0.9 copy-start.14

commit v2 on v1

--- a/solution.py
+++ b/solution.py
@@ -153,8 +153,10 @@
     return s
 
 
-def product(left, right):
-    return jnp.dot(left, right, preferred_element_type=jnp.float32)
+def contract(left, right, left_dim, right_dim):
+    return lax.dot_general(
+        left, right, (((left_dim,), (right_dim,)), ((), ())), preferred_element_type=jnp.float32
+    )
 
 
 def widened(x):
@@ -162,19 +164,19 @@
 
 
 def learn(x, w_first, w_mid, w_last, keep=None):
-    h = jnp.tanh(product(w_first[...], x)).astype(jnp.bfloat16)
+    h = jnp.tanh(contract(x, w_first[...], 0, 1)).astype(jnp.bfloat16)
     if keep is not None:
         keep(0, h)
     for k in range(w_mid.shape[0]):
-        h = jnp.tanh(product(w_mid[k], h)).astype(jnp.bfloat16)
+        h = jnp.tanh(contract(h, w_mid[k], 1, 1)).astype(jnp.bfloat16)
         if keep is not None:
             keep(k + 1, h)
-    return product(w_last[...], h)[:FIELDS]
+    return contract(w_last[...], h, 1, 1)[:FIELDS]
 
 
 def pieces_of(cols):
     step = cols
-    while step > 1024 and step % 256 == 0:
+    while step > 2048 and step % 256 == 0:
         step //= 2
     return [(at, step) for at in range(0, cols, step)]
 
@@ -197,7 +199,7 @@
             inputs[:, pl.ds(where, size)] = x
 
             def keep(k, h, where=where, size=size):
-                hidden[k, :, pl.ds(where, size)] = h
+                hidden[k, pl.ds(where, size), :] = h
 
         out = learn(x, *weights, keep)
         for n in range(size // LANES):
@@ -213,8 +215,16 @@
         learned[rim, pl.ds(row, FIELDS, stride=spread), :] = out[:, n * LANES : (n + 1) * LANES]
 
 
+def line_copy(line, cols, source, target, flags):
+    where = line * cols
+    if not isinstance(where, int):
+        where = pl.multiple_of(where, LANES)
+    here = pl.ds(where, cols)
+    return pltpu.make_async_copy(source.at[:, here, :], target.at[:, here, :], flags.at[line])
+
+
 def inner_kernel(
-    fields, w_first, w_mid, w_last, learned, hidden, inputs, before, after, strain
+    fields, w_first, w_mid, w_last, learned, stored, inputs, before, after, strain, hidden, flags
 ):
     rows, wide = fields.shape[1], fields.shape[2]
     tiles = wide // LANES
@@ -245,40 +255,37 @@
 
     def line(row, carry):
         learn_line(row, row - 1, strain, learned, rows, cols, weights, hidden, inputs)
+        line_copy(row - 1, cols, hidden, stored, flags).start()
         return carry
 
     lax.fori_loop(1, rows - 1, line, 0)
     learn_rims(range(1, rows - 1), strain, learned, rows, cols, weights)
-
-
-def outer_kernel(
-    table, fields, up, down, fl_up, fl_down, inner, w_first, w_mid, w_last,
-    residual, own_residual, stiff, support, hidden, inputs,
-    centre, before, after, ahead, behind, middle, strain, learned,
-):
+    for n in range(rows - 2):
+        line_copy(n, cols, hidden, stored, flags).wait()
+
+
+def stiffness_of(table, ids, depth, target, at):
     layups = table.shape[0] // 36
+    bits = [(ids & (1 << k)) != 0 for k in range(depth)]
+    for n, (a, b) in enumerate(UPPER):
+        layers = [table[min(l, layups - 1) * 36 + a * 6 + b] for l in range(1 << depth)]
+        target[n, :, at] = jnp.broadcast_to(chosen(layers, bits), ids.shape)
+
+
+def depth_of(table):
+    depth = 1
+    while (1 << depth) < table.shape[0] // 36:
+        depth += 1
+    return depth
+
+
+def prepare_kernel(table, fields, fl_up, fl_down, stiff, support):
     rows, wide = fields.shape[1], fields.shape[2]
-    tiles = wide // LANES
-    cols = wide - LANES
-    tall = 3 * rows
     halo = fl_up.shape[1]
-    lane = lax.broadcasted_iota(jnp.int32, (tall, LANES), 1)
-    first, final = lane == 0, lane == LANES - 1
-    depth = 1
-    while (1 << depth) < layups:
-        depth += 1
-    rim = jnp.zeros((rows - MARGIN, LANES), jnp.float32)
     edge = jnp.zeros((rows - halo, LANES), jnp.float32)
 
-    def set_up(tile, carry):
-        at = lanes_of(tile)
-        for c in range(3):
-            value = jnp.concatenate(
-                [rim, up[c, :, at], fields[c, :, at], down[c, :, at], rim], axis=0
-            )
-            centre[c, :, at] = value
-            before[c, :, at] = pltpu.roll(value, 1, 1)
-            after[c, :, at] = pltpu.roll(value, LANES - 1, 1)
+    def fill(tile, carry):
+        at = lanes_of(tile)
         around = [
             jnp.concatenate(
                 [edge, fl_up[c, :, at], fields[3 + c, :, at], fl_down[c, :, at], edge], axis=0
@@ -287,11 +294,40 @@
         ]
         for c in range(3):
             support[c, :, at] = around[c]
-        ids = around[3].astype(jnp.int32)
-        bits = [(ids & (1 << k)) != 0 for k in range(depth)]
-        for n, (a, b) in enumerate(UPPER):
-            layers = [table[min(l, layups - 1) * 36 + a * 6 + b] for l in range(1 << depth)]
-            stiff[n, :, at] = jnp.broadcast_to(chosen(layers, bits), (tall, LANES))
+        stiffness_of(table, around[3].astype(jnp.int32), depth_of(table), stiff, at)
+        return carry
+
+    lax.fori_loop(0, wide // LANES, fill, 0)
+
+
+def outer_kernel(
+    table, fields, up, down, inner, w_first, w_mid, w_last,
+    residual, own_residual, stored, inputs,
+    centre, before, after, ahead, behind, middle, strain, learned, stiff, hidden, flags,
+):
+    rows, wide = fields.shape[1], fields.shape[2]
+    tiles = wide // LANES
+    cols = wide - LANES
+    tall = 3 * rows
+    lane = lax.broadcasted_iota(jnp.int32, (tall, LANES), 1)
+    first, final = lane == 0, lane == LANES - 1
+    rim = jnp.zeros((rows - MARGIN, LANES), jnp.float32)
+    last = 3 * MARGIN
+
+    def set_up(tile, carry):
+        at = lanes_of(tile)
+        for c in range(3):
+            above, below = up[MARGIN * c : MARGIN * (c + 1), at], down[MARGIN * c : MARGIN * (c + 1), at]
+            value = jnp.concatenate([rim, above, fields[c, :, at], below, rim], axis=0)
+            centre[c, :, at] = value
+            before[c, :, at] = pltpu.roll(value, 1, 1)
+            after[c, :, at] = pltpu.roll(value, LANES - 1, 1)
+        wall = jnp.zeros((rows - 1, LANES), jnp.float32)
+        ids = jnp.concatenate(
+            [wall, up[last : last + 1, at], fields[6, :, at], down[last : last + 1, at], wall],
+            axis=0,
+        ).astype(jnp.int32)
+        stiffness_of(table, ids, depth_of(table), stiff, at)
         return carry
 
     lax.fori_loop(0, tiles, set_up, 0)
@@ -313,6 +349,8 @@
     rim_rows = (rows - 1, rows, 2 * rows - 1, 2 * rows)
     for row, line in zip(rim_rows, (None, 0, 1, None)):
         learn_line(row, line, strain, learned, tall, cols, weights, hidden, inputs)
+        if line is not None:
+            line_copy(line, cols, hidden, stored, flags).start()
     learn_rims(rim_rows, strain, learned, tall, cols, weights)
 
     def push(tile, carry):
@@ -347,12 +385,60 @@
 
     lax.fori_loop(0, tiles - 1, finish, 0)
     finish(tiles - 1, None)
-
-
-def outer(left, right):
-    return lax.dot_general(
-        left, right, (((1,), (1,)), ((), ())), preferred_element_type=jnp.float32
-    )
+    for n in range(2):
+        line_copy(n, cols, hidden, stored, flags).wait()
+
+
+def solve(numbers, sums, basis, adjoint, upstream, combined):
+    rows = adjoint.shape[1]
+    wide = basis.shape[3]
+    tiles = wide // LANES
+    own_tiles = tiles - 1
+    tall = 3 * rows
+    line = jnp.sum(sums[...], axis=0)
+    picks = [jnp.broadcast_to(line[:, n : n + 1], (1, LANES)) for n in range(SUMS)]
+    centre = [numbers[k] for k in range(3)]
+    width = [numbers[3 + k] for k in range(3)]
+    matrix = [[None] * 4 for _ in range(4)]
+    for k in range(3):
+        for j in range(k + 1):
+            matrix[j][k] = picks[4 + k * (k + 1) // 2 + j]
+    cross = [picks[3], picks[10], picks[11], picks[12]]
+    for j in range(3):
+        value = width[j] * cross[j + 1] + centre[j] * cross[j]
+        matrix[j][3] = value + width[j - 1] * cross[j - 1] if j else value
+    matrix[3][3] = picks[13]
+    weights = [jnp.broadcast_to(x, (tall, LANES)) for x in galerkin(matrix, picks[:4])]
+
+    def combine(tile, carry):
+        at = lanes_of(tile)
+        for c in range(3):
+            value = weights[0] * basis[0, c, :, at]
+            for k in range(1, DEGREE + 1):
+                value = value + weights[k] * basis[k, c, :, at]
+            combined[c, :, at] = value
+            combined[3 + c, :, at] = pltpu.roll(value, 1, 1)
+            combined[6 + c, :, at] = pltpu.roll(value, LANES - 1, 1)
+        return carry
+
+    lax.fori_loop(0, tiles, combine, 0)
+    lane = lax.broadcasted_iota(jnp.int32, (tall, LANES), 1)
+    first, final = lane == 0, lane == LANES - 1
+
+    def strain(tile, carry):
+        at = lanes_of(tile)
+        triples = triples_of(
+            combined.at[0:3], combined.at[3:6], combined.at[6:9], tile, tiles, first, final
+        )
+        for c in range(3):
+            adjoint[c, :, at] = combined[c, rows : 2 * rows, at]
+        for n, value in enumerate(spread_strains(*triples)):
+            upstream[tile, n * rows : (n + 1) * rows] = HALVING[n] * value[rows : 2 * rows]
+        for n in range(6, FIELDS):
+            upstream[tile, n * rows : (n + 1) * rows] = jnp.zeros((rows, LANES), jnp.float32)
+        return carry
+
+    lax.fori_loop(0, own_tiles, strain, 0)
 
 
 def slope_of(signal, h):
@@ -361,16 +447,22 @@
 
 
 def backward_kernel(
-    upstream, inner_hidden, inner_inputs, outer_hidden, outer_inputs, w_mid_t, w_last_t,
-    packed, grads,
+    numbers, sums, basis, inner_hidden, inner_inputs, outer_hidden, outer_inputs, w_mid, w_last,
+    adjoint, packed,
+    combined, upstream, grads, near_hidden, far_hidden, near_flags, far_flags,
 ):
-    layers = w_mid_t.shape[0]
-    hid = w_mid_t.shape[1]
+    layers = w_mid.shape[0]
+    hid = w_mid.shape[1]
     cols = upstream.shape[0] * LANES
     rows = upstream.shape[1] // FIELDS
     last_at = layers * hid
     first_at = last_at + FIELDS
+    for n in range(rows - 2):
+        line_copy(n, cols, inner_hidden, near_hidden, near_flags).start()
+    for n in range(2):
+        line_copy(n, cols, outer_hidden, far_hidden, far_flags).start()
     grads[...] = jnp.zeros_like(grads)
+    solve(numbers, sums, basis, adjoint, upstream, combined)
 
     def line(row, at_line, hidden, inputs):
         for at, size in pieces_of(cols):
@@ -379,22 +471,24 @@
                 where = pl.multiple_of(where, LANES)
             here = pl.ds(where, size)
             signal = widened(gathered(upstream, row, rows, at, size))
-            h = hidden[layers, :, here]
-            grads[last_at : last_at + FIELDS] += outer(signal, h)[:FIELDS]
-            d = slope_of(product(w_last_t[...], signal), h)
+            h = hidden[layers, here, :]
+            grads[last_at : last_at + FIELDS] += contract(signal, h, 1, 0)[:FIELDS]
+            d = slope_of(contract(signal, w_last[...], 0, 0), h)
             for k in range(layers - 1, -1, -1):
-                h = hidden[k, :, here]
-                grads[k * hid : (k + 1) * hid] += outer(d, h)
-                d = slope_of(product(w_mid_t[k], d), h)
-            grads[first_at : first_at + FIELDS] += outer(inputs[:, here], d)[:FIELDS]
+                h = hidden[k, here, :]
+                grads[k * hid : (k + 1) * hid] += contract(d, h, 0, 0)
+                d = slope_of(contract(d, w_mid[k], 1, 0), h)
+            grads[first_at : first_at + FIELDS] += contract(inputs[:, here], d, 1, 0)[:FIELDS]
 
     def inside(row, carry):
-        line(row, row - 1, inner_hidden, inner_inputs)
+        line_copy(row - 1, cols, inner_hidden, near_hidden, near_flags).wait()
+        line(row, row - 1, near_hidden, inner_inputs)
         return carry
 
     lax.fori_loop(1, rows - 1, inside, 0)
-    line(0, 0, outer_hidden, outer_inputs)
-    line(rows - 1, 1, outer_hidden, outer_inputs)
+    for n, row in enumerate((0, rows - 1)):
+        line_copy(n, cols, outer_hidden, far_hidden, far_flags).wait()
+        line(row, n, far_hidden, outer_inputs)
     chunk = packed.shape[1]
     for n in range(packed.shape[0]):
         packed[n] = grads[n * chunk : (n + 1) * chunk]
@@ -545,58 +639,6 @@
     sums[...] = jnp.broadcast_to(line[None], sums.shape)
 
 
-def solve_kernel(numbers, sums, basis, adjoint, upstream, combined):
-    rows = adjoint.shape[1]
-    wide = basis.shape[3]
-    tiles = wide // LANES
-    own_tiles = tiles - 1
-    tall = 3 * rows
-    line = jnp.sum(sums[...], axis=0)
-    picks = [jnp.broadcast_to(line[:, n : n + 1], (1, LANES)) for n in range(SUMS)]
-    centre = [numbers[k] for k in range(3)]
-    width = [numbers[3 + k] for k in range(3)]
-    matrix = [[None] * 4 for _ in range(4)]
-    for k in range(3):
-        for j in range(k + 1):
-            matrix[j][k] = picks[4 + k * (k + 1) // 2 + j]
-    cross = [picks[3], picks[10], picks[11], picks[12]]
-    for j in range(3):
-        value = width[j] * cross[j + 1] + centre[j] * cross[j]
-        matrix[j][3] = value + width[j - 1] * cross[j - 1] if j else value
-    matrix[3][3] = picks[13]
-    weights = [jnp.broadcast_to(x, (tall, LANES)) for x in galerkin(matrix, picks[:4])]
-
-    def combine(tile, carry):
-        at = lanes_of(tile)
-        for c in range(3):
-            value = weights[0] * basis[0, c, :, at]
-            for k in range(1, DEGREE + 1):
-                value = value + weights[k] * basis[k, c, :, at]
-            combined[c, :, at] = value
-            combined[3 + c, :, at] = pltpu.roll(value, 1, 1)
-            combined[6 + c, :, at] = pltpu.roll(value, LANES - 1, 1)
-        return carry
-
-    lax.fori_loop(0, tiles, combine, 0)
-    lane = lax.broadcasted_iota(jnp.int32, (tall, LANES), 1)
-    first, final = lane == 0, lane == LANES - 1
-
-    def strain(tile, carry):
-        at = lanes_of(tile)
-        triples = triples_of(
-            combined.at[0:3], combined.at[3:6], combined.at[6:9], tile, tiles, first, final
-        )
-        for c in range(3):
-            adjoint[c, :, at] = combined[c, rows : 2 * rows, at]
-        for n, value in enumerate(spread_strains(*triples)):
-            upstream[tile, n * rows : (n + 1) * rows] = HALVING[n] * value[rows : 2 * rows]
-        for n in range(6, FIELDS):
-            upstream[tile, n * rows : (n + 1) * rows] = jnp.zeros((rows, LANES), jnp.float32)
-        return carry
-
-    lax.fori_loop(0, own_tiles, strain, 0)
-
-
 def basis_constants(layup_stiffness):
     bending = 0.5 * (jnp.mean(layup_stiffness[:, 3, 3]) + jnp.mean(layup_stiffness[:, 4, 4]))
     centres = [11.5 * bending + 1.1, 9.8 * bending + 1.1, 8.4 * bending + 1.1]
@@ -608,19 +650,30 @@
 SCALARS = pl.BlockSpec(memory_space=pltpu.SMEM)
 
 
-def kernel_call(body, name, scalars, outs, scratch, *operands):
+IN_PLACE = pl.BlockSpec(memory_space=pltpu.HBM)
+
+
+def kernel_call(body, name, scalars, outs, scratch, *operands, far=(), far_outs=()):
+    specs = [SCALARS] * scalars + [ON_CHIP] * (len(operands) - scalars)
+    for n in far:
+        specs[n] = IN_PLACE
     return pl.pallas_call(
         body,
         name=name,
-        in_specs=[SCALARS] * scalars + [ON_CHIP] * (len(operands) - scalars),
-        out_specs=[ON_CHIP] * len(outs),
+        in_specs=specs,
+        out_specs=[IN_PLACE if n in far_outs else ON_CHIP for n in range(len(outs))],
         out_shape=[jax.ShapeDtypeStruct(*out) for out in outs],
-        scratch_shapes=[pltpu.VMEM(*s) for s in scratch],
+        scratch_shapes=[
+            pltpu.VMEM(*s) if isinstance(s, tuple) else pltpu.SemaphoreType.DMA((s,))
+            for s in scratch
+        ],
         compiler_params=pltpu.CompilerParams(vmem_limit_bytes=LIMITS[name] << 20),
     )(*operands)
 
 
-LIMITS = {"inner": 8, "outer": 14, "krylov": 10, "solve": 10, "backward": 8, "gather": 4, "deliver": 4}
+LIMITS = {
+    "inner": 24, "outer": 24, "prepare": 8, "krylov": 10, "backward": 32, "gather": 4, "deliver": 4,
+}
 
 
 def per_device(displacement, load, foundation, layup, layup_stiffness, w_first, w_mid, w_last):
@@ -635,8 +688,12 @@
     before, after = from_both(fields, "sub", 2, HY)
     gap = jnp.zeros(fields.shape[:2] + (LANES - 2 * HY,), f32)
     fields = jnp.concatenate([fields, after, gap, before], axis=2)
-    up, down = from_both(fields[:3], "patch", 1, MARGIN)
-    fl_up, fl_down = from_both(fields[3:7], "patch", 1, 6)
+    sends = [
+        jnp.concatenate([*[fields[c, edge] for c in range(3)], fields[6, edge][near]])
+        for edge, near in ((slice(rows - MARGIN, rows), slice(1, 2)), (slice(0, MARGIN), slice(0, 1)))
+    ]
+    up = lax.ppermute(sends[0], "patch", ring("patch", 1))
+    down = lax.ppermute(sends[1], "patch", ring("patch", -1))
 
     halving = jnp.array(HALVING, f32)
     table = (layup_stiffness * halving[:, None] * halving[None, :]).reshape(-1)
@@ -645,21 +702,31 @@
     thin = w_first.shape[1]
     first_pad = jnp.pad(w_first, ((0, 0), (0, PADDED - thin)))
     last_pad = jnp.pad(w_last, ((0, PADDED - thin), (0, 0)))
-    mid_t, last_t = jnp.swapaxes(w_mid, 1, 2), last_pad.T
 
     learned, inner_hidden, inner_inputs = kernel_call(
         inner_kernel, "inner", 0,
-        [((tiles, FIELDS * rows, LANES), f32), ((layers + 1, hid, (rows - 2) * cols), bf16),
+        [((tiles, FIELDS * rows, LANES), f32), ((layers + 1, (rows - 2) * cols, hid), bf16),
          ((PADDED, (rows - 2) * cols), bf16)],
-        [((3, rows, wide), f32)] * 2 + [((tiles, FIELDS * rows, LANES), f32)],
-        fields, first_pad, w_mid, last_pad,
-    )
-    wide_residual, residual, stiff, support, outer_hidden, outer_inputs = kernel_call(
+        [((3, rows, wide), f32)] * 2
+        + [((tiles, FIELDS * rows, LANES), f32), ((layers + 1, (rows - 2) * cols, hid), bf16),
+           rows - 2],
+        fields, first_pad, w_mid, last_pad, far_outs=(1,),
+    )
+    learned, distant = lax.optimization_barrier((learned, fields[3:7]))
+    fl_up, fl_down = from_both(distant, "patch", 1, 6)
+    wide_residual, residual, outer_hidden, outer_inputs = kernel_call(
         outer_kernel, "outer", 1,
-        [((3, rows, wide), f32), ((3, rows, cols), f32), ((len(UPPER), tall, wide), f32),
-         ((3, tall, wide), f32), ((layers + 1, hid, 2 * cols), bf16), ((PADDED, 2 * cols), bf16)],
-        [((3, tall, wide), f32)] * 6 + [((tiles, FIELDS * tall, LANES), f32)] * 2,
-        table, fields, up, down, fl_up, fl_down, learned, first_pad, w_mid, last_pad,
+        [((3, rows, wide), f32), ((3, rows, cols), f32),
+         ((layers + 1, 2 * cols, hid), bf16), ((PADDED, 2 * cols), bf16)],
+        [((3, tall, wide), f32)] * 6
+        + [((tiles, FIELDS * tall, LANES), f32)] * 2
+        + [((len(UPPER), tall, wide), f32), ((layers + 1, 2 * cols, hid), bf16), 2],
+        table, fields, up, down, learned, first_pad, w_mid, last_pad, far_outs=(2,),
+    )
+    stiff, support = kernel_call(
+        prepare_kernel, "prepare", 1,
+        [((len(UPPER), tall, wide), f32), ((3, tall, wide), f32)], [],
+        table, fields, fl_up, fl_down,
     )
     up, down = from_both(wide_residual, "patch", 1, rows)
     basis, sums = kernel_call(
@@ -669,19 +736,16 @@
         numbers, wide_residual, up, down, stiff, support,
     )
     sums = everyone(sums)
-    adjoint, upstream = kernel_call(
-        solve_kernel, "solve", 1,
-        [((3, rows, cols), f32), ((tiles - 1, FIELDS * rows, LANES), f32)],
-        [((9, tall, wide), f32)],
-        numbers, sums, basis,
-    )
     count = layers * hid + 2 * FIELDS
     chunk = -(-count // devices)
-    (packed,) = kernel_call(
-        backward_kernel, "backward", 0,
-        [((devices, chunk, LANES), f32)],
-        [((devices * chunk, LANES), f32)],
-        upstream, inner_hidden, inner_inputs, outer_hidden, outer_inputs, mid_t, last_t,
+    adjoint, packed = kernel_call(
+        backward_kernel, "backward", 1,
+        [((3, rows, cols), f32), ((devices, chunk, LANES), f32)],
+        [((9, tall, wide), f32), ((tiles - 1, FIELDS * rows, LANES), f32),
+         ((devices * chunk, LANES), f32), ((layers + 1, (rows - 2) * cols, hid), bf16),
+         ((layers + 1, 2 * cols, hid), bf16), rows - 2, 2],
+        numbers, sums, basis, inner_hidden, inner_inputs, outer_hidden, outer_inputs,
+        w_mid, last_pad, far=(3, 5),
     )
     (total,) = kernel_call(
         gather_kernel, "gather", 0, [(packed.shape, f32)], [], everyone(packed)

time: 149 us -> 128 us (0.86)
  local copies, waits for them, and re-layouts: 25.7 us -> 13.7 us
  blocking collectives: 25 us -> 34.4 us
  waiting for transfers between devices: 12.8 us -> 4.17 us
  starting transfers between devices: 20.8 us -> 14.7 us
  Pallas kernels: 59.1 us -> 54.4 us
  other arithmetic: 2.79 us -> 4.32 us
    unnamed x43 -> x12, local copies, waits for them, and re-layouts: 25.2 us -> 12.5 us
    all_to_all x2 -> x3, blocking collectives: 25 us -> 34.4 us  [everyone(): return lax.all_to_all(rows, AXES, 0, 0, tiled=True)]
    all_to_all x1 -> x0, waiting for transfers between devices: 6.95 us -> none  [everyone(): return lax.all_to_all(rows, AXES, 0, 0, tiled=True)]
    ppermute x4 -> x3, starting transfers between devices: 15.1 us -> 8.76 us  [from_both(): after = lax.ppermute(head, axis, ring(axis, -1))]
    ppermute x0 -> x2, starting transfers between devices: none -> 5.38 us  [the longest x1 3.11 us: per_device(): down = lax.ppermute(sends[1], 'patch', ring('patch', -1))]
    pallas_call x7, Pallas kernels: 59.1 us -> 54.4 us  [kernel_call(): pl.pallas_call(body, name=name, in_specs=specs, out_specs=[IN_PLACE if n...]
    all_to_all x1 -> x0, starting transfers between devices: 4.16 us -> none  [everyone(): return lax.all_to_all(rows, AXES, 0, 0, tiled=True)]
    ppermute x4 -> x3, waiting for transfers between devices: 2.59 us -> 0.01 us  [from_both(): after = lax.ppermute(head, axis, ring(axis, -1))]
  transfers between devices with their start and end apart: 9 -> 8, of which waited for: 5 -> 1; matrix products, arithmetic and copies ran while one was open for 1% -> 3% of each run, Pallas kernels for 8% -> 18%
where the time goes in v2:
time: 128 us
  Pallas kernels  54.4 us (42%)
  blocking collectives  34.4 us (27%)
  starting transfers between devices  14.7 us (11%)
  local copies, waits for them, and re-layouts  13.7 us (11%)
  other arithmetic  4.32 us (3%)
  waiting for transfers between devices  4.17 us (3%)
  between operations  2.23 us (2%)
    pallas_call x7, Pallas kernels, kernel_call(): pl.pallas_call(body, name=name, in_specs=specs, out_specs=[IN_PLACE if n...  54.4 us
    all_to_all x3, blocking collectives, everyone(): return lax.all_to_all(rows, AXES, 0, 0, tiled=True)  34.4 us
    unnamed x12, local copies, waits for them, and re-layouts  12.5 us
    ppermute x3, starting transfers between devices, from_both(): after = lax.ppermute(head, axis, ring(axis, -1))  8.76 us
    ppermute x3, waiting for transfers between devices, from_both(): before = lax.ppermute(tail, axis, ring(axis, 1))  4.16 us
    ppermute x1, starting transfers between devices, per_device(): down = lax.ppermute(sends[1], 'patch', ring('patch', -1))  3.11 us
  transfers between devices with their start and end apart: 8, of which 1 were waited for; matrix products, arithmetic and copies ran while one was open for 3% of the time, Pallas kernels for 18%

profile of v2, /device:TPU:0, one launch (start us, length us, event | category | flops | bytes accessed | tf_op | source)
XLA Modules:
  0.0 127.8 jit_solution(11239677110369343755)
XLA Ops:
  0.6 0.0 copy-start.4
  0.6 0.9 convert_bitcast_fusion
  1.5 1.2 pad_maximum_fusion
  2.7 0.1 fusion
  2.8 0.5 collective-permute-start.1
  3.3 2.0 %collective-permute-start = (f32[10,8,16]{2,1,0:T(8,128)S(1)}, f32[10,8,16]{2,1,0:T(8,128)S(1)}, u32[]{:S(2)}, u32[]{:S(2)}) collective-permute-start(f32[10,8,16]{2,1,0:T(8,128)S(1)} %get-tuple-element.62), channel_id=1, source_target_pairs={{0,3},{1,0},{2,1},{3,2},{4,7},{5,4},{6,5},{7,6},{8,11},{9,8},{10,9... | collective-permute-start | bytes 15368 | tf_op jit(solution)/shard_map/ppermute | solution.py:23
  5.3 0.8 multiply_multiply_fusion
  6.1 0.1 reshape.17.table
  6.2 0.8 copy.17
  7.0 0.7 pad.9.w_last
  7.7 0.0 collective-permute-done.1
  7.8 0.0 collective-permute-done
  7.8 0.1 concatenate.13.fields
  8.0 2.3 %collective-permute-start.2 = (f32[7,2176]{1,0:T(8,128)S(1)}, f32[7,2176]{1,0:T(8,128)S(1)}, u32[]{:S(2)}, u32[]{:S(2)}) collective-permute-start(f32[7,2176]{1,0:T(8,128)S(1)} %pad_maximum_fusion.1), channel_id=1, source_target_pairs={{0,4},{4,8},{8,12},{12,16},{16,20},{20,24},{24,28},{28,0},{1,5},{5... | collective-permute-start | bytes 182792 | tf_op jit(solution)/shard_map/ppermute | solution.py:695
  10.3 3.1 %collective-permute-start.3 = (f32[7,2176]{1,0:T(8,128)S(1)}, f32[7,2176]{1,0:T(8,128)S(1)}, u32[]{:S(2)}, u32[]{:S(2)}) collective-permute-start(f32[7,2176]{1,0:T(8,128)S(1)} %pad_maximum_fusion.2), channel_id=1, source_target_pairs={{0,28},{4,0},{8,4},{12,8},{16,12},{20,16},{24,20},{28,24},{1,29},{... | collective-permute-start | bytes 182792 | tf_op jit(solution)/shard_map/ppermute | solution.py:696
  13.4 0.0 copy-done.4
  13.4 9.2 %inner.1 = (f32[17,64,128]{2,1,0:T(8,128)S(1)}, bf16[4,12288,128]{2,1,0:T(8,128)(2,1)S(1)}, bf16[16,12288]{1,0:T(8,128)(2,1)S(1)}) custom-call(f32[10,8,2176]{2,1,0:T(8,128)S(1)} %concatenate.13.fields, bf16[128,16]{1,0:T(8,128)(2,1)S(1)} %pad.8.w_first, bf16[3,128,128]{2,1,0:T(8,128)(2,1)S(1)} %copy-done.4, bf16[16,128]{1,0:T(8,128)(2,1)S(1)} %pad.9.w_last), custom_call_target="tpu_custom_call" | custom-call | tf_op jit(solution)/shard_map/inner/pallas_call | solution.py:660
  22.6 0.0 copy-start
  22.7 4.5 %copy-done = bf16[4,12288,128]{2,1,0:T(8,128)(2,1)} copy-done((bf16[4,12288,128]{2,1,0:T(8,128)(2,1)}, bf16[4,12288,128]{2,1,0:T(8,128)(2,1)S(1)}, u32[]{:S(2)}) %copy-start) | copy-done | bytes 12582936
  27.2 2.1 %collective-permute-start.7 = (f32[4,6,2176]{2,1,0:T(8,128)S(1)}, f32[4,6,2176]{2,1,0:T(8,128)S(1)}, u32[]{:S(2)}, u32[]{:S(2)}) collective-permute-start(f32[4,6,2176]{2,1,0:T(8,128)S(1)} %get-tuple-element.63), channel_id=1, source_target_pairs={{0,28},{4,0},{8,4},{12,8},{16,12},{20,16},{24,20},{28,24},{1,29},{... | collective-permute-start | bytes 626696 | tf_op jit(solution)/shard_map/ppermute | solution.py:23
  29.3 0.0 collective-permute-start.6
  29.3 0.0 collective-permute-done.2.up
  29.3 0.0 collective-permute-done.3.down
  29.3 11.6 %outer.1 = (f32[3,8,2176]{2,1,0:T(8,128)S(1)}, f32[3,8,2048]{2,1,0:T(8,128)}, bf16[4,4096,128]{2,1,0:T(8,128)(2,1)S(1)}, bf16[16,4096]{1,0:T(8,128)(2,1)S(1)}) custom-call(f32[288]{0:T(512)S(1)} %reshape.17.table, f32[10,8,2176]{2,1,0:T(8,128)S(1)} %concatenate.13.fields, f32[7,2176]{1,0:T(8,128)S(1)} %collective-permute-done.2.up, ...), custom_call_target="tpu_custom_call" | custom-call | tf_op jit(solution)/shard_map/outer/pallas_call | solution.py:660
  40.9 0.0 copy-start.2
  40.9 1.9 %copy-done.2 = bf16[4,4096,128]{2,1,0:T(8,128)(2,1)} copy-done((bf16[4,4096,128]{2,1,0:T(8,128)(2,1)}, bf16[4,4096,128]{2,1,0:T(8,128)(2,1)S(1)}, u32[]{:S(2)}) %copy-start.2) | copy-done | bytes 4194328
  42.9 4.7 %collective-permute-start.5 = (f32[3,8,2176]{2,1,0:T(8,128)S(1)}, f32[3,8,2176]{2,1,0:T(8,128)S(1)}, u32[]{:S(2)}, u32[]{:S(2)}) collective-permute-start(f32[3,8,2176]{2,1,0:T(8,128)S(1)} %get-tuple-element.26.r_mid), channel_id=1, source_target_pairs={{0,28},{4,0},{8,4},{12,8},{16,12},{20,16},{24,20},{28,24},{1,29},{... | collective-permute-start | bytes 626696 | tf_op jit(solution)/shard_map/ppermute | solution.py:23
  47.6 0.0 collective-permute-start.4
  47.6 1.4 %slice_reduce_fusion = (f32[]{:T(128)}, f32[]{:T(128)}) fusion(f32[8,6,6]{2,0,1:T(8,128)} %param.13), kind=kLoop, calls=%fused_computation.13 | loop fusion | flops 14 | bytes 72 | tf_op jit(solution)/shard_map/reduce_sum | solution.py:643
  50.4 0.1 stack.39.numbers
  50.5 0.0 copy-start.3
  50.5 0.0 collective-permute-done.7.fl_down
  50.5 0.0 collective-permute-done.6.fl_up
  50.5 2.1 %prepare.1 = (f32[21,24,2176]{2,1,0:T(8,128)S(1)}, f32[3,24,2176]{2,1,0:T(8,128)S(1)}) custom-call(f32[288]{0:T(512)S(1)} %reshape.17.table, f32[10,8,2176]{2,1,0:T(8,128)S(1)} %concatenate.13.fields, f32[4,6,2176]{2,1,0:T(8,128)S(1)} %collective-permute-done.6.fl_up, f32[4,6,2176]{2,1,0:T(8,128)S(1)} %collective-permute-done.7.fl_down), custom_call_target="tpu_custom_call" | custom-call | tf_op jit(solution)/shard_map/prepare/pallas_call | solution.py:660
  52.6 0.0 collective-permute-done.5.r_down
  52.6 4.2 %collective-permute-done.4.r_up = f32[3,8,2176]{2,1,0:T(8,128)S(1)} collective-permute-done((f32[3,8,2176]{2,1,0:T(8,128)S(1)}, f32[3,8,2176]{2,1,0:T(8,128)S(1)}, u32[]{:S(2)}, u32[]{:S(2)}) %collective-permute-start.4) | collective-permute-done | bytes 208928 | tf_op jit(solution)/shard_map/ppermute | solution.py:22
  56.7 15.3 %krylov.1 = (f32[4,3,24,2176]{3,2,1,0:T(8,128)S(1)}, f32[32,1,128]{2,1,0:T(1,128)S(1)}) custom-call(f32[9]{0:T(128)S(1)} %stack.39.numbers, f32[3,8,2176]{2,1,0:T(8,128)S(1)} %get-tuple-element.26.r_mid, f32[3,8,2176]{2,1,0:T(8,128)S(1)} %collective-permute-done.4.r_up, f32[3,8,2176]{2,1,0:T(8,128)S(1)} %collective-permute-done.5.r_down, ...), custom_call_target="tpu_custom_call" | custom-call | tf_op jit(solution)/shard_map/krylov/pallas_call | solution.py:660
  72.1 9.4 %all_to_all.15.sums = f32[32,1,128]{2,1,0:T(1,128)S(1)} all-to-all(f32[32,1,128]{2,1,0:T(1,128)S(1)} %get-tuple-element.30), channel_id=1, replica_groups=mesh['patch'=8,'sub'=4] {'patch','sub'}, dimensions={0} | all-to-all | bytes 32768 | tf_op jit(solution)/shard_map/all_to_all | solution.py:28
  81.5 0.0 copy-done.3
  81.5 0.0 copy-start.1
  81.5 4.6 %copy-done.1 = bf16[4,12288,128]{2,1,0:T(8,128)(2,1)S(1)} copy-done((bf16[4,12288,128]{2,1,0:T(8,128)(2,1)S(1)}, bf16[4,12288,128]{2,1,0:T(8,128)(2,1)}, u32[]{:S(2)}) %copy-start.1) | copy-done | bytes 12582936
  86.1 15.4 %backward.1 = (f32[3,8,2048]{2,1,0:T(8,128)}, f32[32,13,128]{2,1,0:T(8,128)S(1)}) custom-call(f32[9]{0:T(128)S(1)} %stack.39.numbers, f32[32,1,128]{2,1,0:T(1,128)S(1)} %all_to_all.15.sums, f32[4,3,24,2176]{3,2,1,0:T(8,128)S(1)} %get-tuple-element.31.basis, bf16[4,12288,128]{2,1,0:T(8,128)(2,1)S(1)} %copy-done.1, ...), custom_call_target="tpu_custom_call" | custom-call | tf_op jit(solution)/shard_map/backward/pallas_call | solution.py:660
  101.4 12.3 %all_to_all.16.parts = f32[32,13,128]{2,1,0:T(8,128)S(1)} all-to-all(f32[32,13,128]{2,1,0:T(8,128)S(1)} %get-tuple-element.37), channel_id=1, replica_groups=mesh['patch'=8,'sub'=4] {'patch','sub'}, dimensions={0} | all-to-all | bytes 425984 | tf_op jit(solution)/shard_map/all_to_all | solution.py:28
  113.7 0.1 gather.1
  113.8 12.7 %all_to_all.17.parts = f32[32,13,128]{2,1,0:T(8,128)S(1)} all-to-all(f32[32,13,128]{2,1,0:T(8,128)S(1)} %gather.1), channel_id=1, replica_groups=mesh['patch'=8,'sub'=4] {'patch','sub'}, dimensions={0} | all-to-all | bytes 425984 | tf_op jit(solution)/shard_map/all_to_all | solution.py:28
  126.5 0.7 deliver.1
  127.2 0.7 copy.18
  (9 shorter events, 0.2 us)
Async XLA Ops:
  0.6 12.8 %copy-start.4 = (bf16[3,128,128]{2,1,0:T(8,128)(2,1)S(1)}, bf16[3,128,128]{2,1,0:T(8,128)(2,1)}, u32[]{:S(2)}) copy-start(bf16[3,128,128]{2,1,0:T(8,128)(2,1)} %w_mid.5) | copy-start | bytes 294916
  2.8 5.0 %collective-permute-start.1 = (f32[10,8,16]{2,1,0:T(8,128)S(1)}, f32[10,8,16]{2,1,0:T(8,128)S(1)}, u32[]{:S(2)}, u32[]{:S(2)}) collective-permute-start(f32[10,8,16]{2,1,0:T(8,128)S(1)} %get-tuple-element.61), channel_id=1, source_target_pairs={{0,1},{1,2},{2,3},{3,0},{4,5},{5,6},{6,7},{7,4},{8,9},{9,10},{10,1... | collective-permute-start | bytes 15368 | tf_op jit(solution)/shard_map/ppermute | solution.py:22
  3.3 4.5 %collective-permute-start = (f32[10,8,16]{2,1,0:T(8,128)S(1)}, f32[10,8,16]{2,1,0:T(8,128)S(1)}, u32[]{:S(2)}, u32[]{:S(2)}) collective-permute-start(f32[10,8,16]{2,1,0:T(8,128)S(1)} %get-tuple-element.62), channel_id=1, source_target_pairs={{0,3},{1,0},{2,1},{3,2},{4,7},{5,4},{6,5},{7,6},{8,11},{9,8},{10,9... | collective-permute-start | bytes 15368 | tf_op jit(solution)/shard_map/ppermute | solution.py:23
  8.0 21.3 %collective-permute-start.2 = (f32[7,2176]{1,0:T(8,128)S(1)}, f32[7,2176]{1,0:T(8,128)S(1)}, u32[]{:S(2)}, u32[]{:S(2)}) collective-permute-start(f32[7,2176]{1,0:T(8,128)S(1)} %pad_maximum_fusion.1), channel_id=1, source_target_pairs={{0,4},{4,8},{8,12},{12,16},{16,20},{20,24},{24,28},{28,0},{1,5},{5... | collective-permute-start | bytes 182792 | tf_op jit(solution)/shard_map/ppermute | solution.py:695
  10.3 19.0 %collective-permute-start.3 = (f32[7,2176]{1,0:T(8,128)S(1)}, f32[7,2176]{1,0:T(8,128)S(1)}, u32[]{:S(2)}, u32[]{:S(2)}) collective-permute-start(f32[7,2176]{1,0:T(8,128)S(1)} %pad_maximum_fusion.2), channel_id=1, source_target_pairs={{0,28},{4,0},{8,4},{12,8},{16,12},{20,16},{24,20},{28,24},{1,29},{... | collective-permute-start | bytes 182792 | tf_op jit(solution)/shard_map/ppermute | solution.py:696
  22.6 4.5 %copy-start = (bf16[4,12288,128]{2,1,0:T(8,128)(2,1)}, bf16[4,12288,128]{2,1,0:T(8,128)(2,1)S(1)}, u32[]{:S(2)}) copy-start(bf16[4,12288,128]{2,1,0:T(8,128)(2,1)S(1)} %get-tuple-element.32.inner_hidden) | copy-start | bytes 37748740
  27.2 23.2 %collective-permute-start.7 = (f32[4,6,2176]{2,1,0:T(8,128)S(1)}, f32[4,6,2176]{2,1,0:T(8,128)S(1)}, u32[]{:S(2)}, u32[]{:S(2)}) collective-permute-start(f32[4,6,2176]{2,1,0:T(8,128)S(1)} %get-tuple-element.63), channel_id=1, source_target_pairs={{0,28},{4,0},{8,4},{12,8},{16,12},{20,16},{24,20},{28,24},{1,29},{... | collective-permute-start | bytes 626696 | tf_op jit(solution)/shard_map/ppermute | solution.py:23
  29.3 21.2 %collective-permute-start.6 = (f32[4,6,2176]{2,1,0:T(8,128)S(1)}, f32[4,6,2176]{2,1,0:T(8,128)S(1)}, u32[]{:S(2)}, u32[]{:S(2)}) collective-permute-start(f32[4,6,2176]{2,1,0:T(8,128)S(1)} %get-tuple-element.64), channel_id=1, source_target_pairs={{0,4},{4,8},{8,12},{12,16},{16,20},{20,24},{24,28},{28,0},{1,5},{5... | collective-permute-start | bytes 626696 | tf_op jit(solution)/shard_map/ppermute | solution.py:22
  40.9 1.9 %copy-start.2 = (bf16[4,4096,128]{2,1,0:T(8,128)(2,1)}, bf16[4,4096,128]{2,1,0:T(8,128)(2,1)S(1)}, u32[]{:S(2)}) copy-start(bf16[4,4096,128]{2,1,0:T(8,128)(2,1)S(1)} %get-tuple-element.34.outer_hidden) | copy-start | bytes 12582916
  42.9 9.7 %collective-permute-start.5 = (f32[3,8,2176]{2,1,0:T(8,128)S(1)}, f32[3,8,2176]{2,1,0:T(8,128)S(1)}, u32[]{:S(2)}, u32[]{:S(2)}) collective-permute-start(f32[3,8,2176]{2,1,0:T(8,128)S(1)} %get-tuple-element.26.r_mid), channel_id=1, source_target_pairs={{0,28},{4,0},{8,4},{12,8},{16,12},{20,16},{24,20},{28,24},{1,29},{... | collective-permute-start | bytes 626696 | tf_op jit(solution)/shard_map/ppermute | solution.py:23
  47.6 9.2 %collective-permute-start.4 = (f32[3,8,2176]{2,1,0:T(8,128)S(1)}, f32[3,8,2176]{2,1,0:T(8,128)S(1)}, u32[]{:S(2)}, u32[]{:S(2)}) collective-permute-start(f32[3,8,2176]{2,1,0:T(8,128)S(1)} %get-tuple-element.26.r_mid), channel_id=1, source_target_pairs={{0,4},{4,8},{8,12},{12,16},{16,20},{20,24},{24,28},{28,0},{1,5},{5... | collective-permute-start | bytes 626696 | tf_op jit(solution)/shard_map/ppermute | solution.py:22
  50.5 31.0 %copy-start.3 = (bf16[4,4096,128]{2,1,0:T(8,128)(2,1)S(1)}, bf16[4,4096,128]{2,1,0:T(8,128)(2,1)}, u32[]{:S(2)}) copy-start(bf16[4,4096,128]{2,1,0:T(8,128)(2,1)} %copy-done.2) | copy-start | bytes 12582916
  81.5 4.6 %copy-start.1 = (bf16[4,12288,128]{2,1,0:T(8,128)(2,1)S(1)}, bf16[4,12288,128]{2,1,0:T(8,128)(2,1)}, u32[]{:S(2)}) copy-start(bf16[4,12288,128]{2,1,0:T(8,128)(2,1)} %copy-done) | copy-start | bytes 37748740

commit v3 on v2

--- a/solution.py
+++ b/solution.py
@@ -164,7 +164,7 @@
 
 
 def learn(x, w_first, w_mid, w_last, keep=None):
-    h = jnp.tanh(contract(x, w_first[...], 0, 1)).astype(jnp.bfloat16)
+    h = jnp.tanh(contract(x, w_first[...], 0, 0)).astype(jnp.bfloat16)
     if keep is not None:
         keep(0, h)
     for k in range(w_mid.shape[0]):
@@ -507,7 +507,7 @@
         grad_mid[k] = flat[k * hid : (k + 1) * hid]
     at = layers * hid
     grad_last[...] = flat[at : at + FIELDS][: grad_last.shape[0]]
-    grad_first[...] = flat[at + FIELDS : at + 2 * FIELDS].T[:, : grad_first.shape[1]]
+    grad_first[...] = flat[at + FIELDS : at + 2 * FIELDS][: grad_first.shape[0]]
 
 
 def krylov_kernel(
@@ -662,13 +662,19 @@
         name=name,
         in_specs=specs,
         out_specs=[IN_PLACE if n in far_outs else ON_CHIP for n in range(len(outs))],
-        out_shape=[jax.ShapeDtypeStruct(*out) for out in outs],
+        out_shape=[
+            pltpu.HBM(*out) if n in far_outs else jax.ShapeDtypeStruct(*out)
+            for n, out in enumerate(outs)
+        ],
         scratch_shapes=[
             pltpu.VMEM(*s) if isinstance(s, tuple) else pltpu.SemaphoreType.DMA((s,))
             for s in scratch
         ],
         compiler_params=pltpu.CompilerParams(vmem_limit_bytes=LIMITS[name] << 20),
-    )(*operands)
+    )(*[
+        pltpu.with_memory_space_constraint(x, pltpu.HBM) if n in far else x
+        for n, x in enumerate(operands)
+    ])
 
 
 LIMITS = {
@@ -700,7 +706,7 @@
     centres, widths = basis_constants(layup_stiffness)
     numbers = jnp.stack(centres + widths + [1.0 / x for x in widths])
     thin = w_first.shape[1]
-    first_pad = jnp.pad(w_first, ((0, 0), (0, PADDED - thin)))
+    first_pad = jnp.pad(w_first.T, ((0, PADDED - thin), (0, 0)))
     last_pad = jnp.pad(w_last, ((0, PADDED - thin), (0, 0)))
 
     learned, inner_hidden, inner_inputs = kernel_call(
@@ -752,11 +758,11 @@
     )
     grad_first, grad_mid, grad_last = kernel_call(
         deliver_kernel, "deliver", 0,
-        [(w_first.shape, f32), (w_mid.shape, f32), (w_last.shape, f32)],
+        [((thin, hid), f32), (w_mid.shape, f32), (w_last.shape, f32)],
         [((devices * chunk, LANES), f32)],
         everyone(total),
     )
-    return residual, adjoint, grad_first, grad_mid, grad_last
+    return residual, adjoint, grad_first.T, grad_mid, grad_last
 
 
 def solution(mesh):

time: 128 us -> 114 us (0.89)
  local copies, waits for them, and re-layouts: 13.7 us -> 1.88 us
  Pallas kernels: 54.4 us -> 52.1 us
    unnamed x12 -> x2, local copies, waits for them, and re-layouts: 12.5 us -> 0.01 us
    pallas_call x7, Pallas kernels: 54.4 us -> 52.1 us  [kernel_call(): pl.pallas_call(body, name=name, in_specs=specs, out_specs=[IN_PLACE if n...]
  transfers between devices with their start and end apart: 8 -> 8, of which waited for: 1 -> 1; matrix products, arithmetic and copies ran while one was open for 3% -> 3% of each run, Pallas kernels for 18% -> 19%
where the time goes in v3:
time: 114 us
  Pallas kernels  52.1 us (46%)
  blocking collectives  34.4 us (30%)
  starting transfers between devices  14.7 us (13%)
  other arithmetic  4.32 us (4%)
  waiting for transfers between devices  4.32 us (4%)
  between operations  2.21 us (2%)
  local copies, waits for them, and re-layouts  1.88 us (2%)
    pallas_call x7, Pallas kernels, kernel_call(): pl.pallas_call(body, name=name, in_specs=specs, out_specs=[IN_PLACE if n...  52.1 us
    all_to_all x3, blocking collectives, everyone(): return lax.all_to_all(rows, AXES, 0, 0, tiled=True)  34.4 us
    ppermute x3, starting transfers between devices, from_both(): after = lax.ppermute(head, axis, ring(axis, -1))  8.82 us
    ppermute x3, waiting for transfers between devices, from_both(): before = lax.ppermute(tail, axis, ring(axis, 1))  4.31 us
    ppermute x1, starting transfers between devices, per_device(): down = lax.ppermute(sends[1], 'patch', ring('patch', -1))  3.11 us
  transfers between devices with their start and end apart: 8, of which 1 were waited for; matrix products, arithmetic and copies ran while one was open for 3% of the time, Pallas kernels for 19%

profile of v3, /device:TPU:0, one launch (start us, length us, event | category | flops | bytes accessed | tf_op | source)
XLA Modules:
  0.0 114.0 jit_solution(4187757337671066337)
XLA Ops:
  0.6 0.0 copy-start
  0.6 0.9 convert_bitcast_fusion
  1.5 1.2 %pad_maximum_fusion = f32[10,8,2048]{2,1,0:T(8,128)S(1)} fusion(f32[3,8,2048]{2,1,0:T(8,128)} %param.10, f32[1,8,2048]{2,1,0:T(8,128)S(1)} %convert_bitcast_fusion, f32[3,8,2048]{2,1,0:T(8,128)} %param.11, f32[3,8,2048]{2,1,0:T(8,128)} %param.9), kind=kLoop, calls=%fused_computation | loop fusion | flops 491520 | bytes 1310720 | tf_op jit(solution)/shard_map/concatenate | solution.py:693
  2.7 0.1 fusion
  2.8 0.5 collective-permute-start.1
  3.3 2.0 %collective-permute-start = (f32[10,8,16]{2,1,0:T(8,128)S(1)}, f32[10,8,16]{2,1,0:T(8,128)S(1)}, u32[]{:S(2)}, u32[]{:S(2)}) collective-permute-start(f32[10,8,16]{2,1,0:T(8,128)S(1)} %get-tuple-element.52), channel_id=1, source_target_pairs={{0,3},{1,0},{2,1},{3,2},{4,7},{5,4},{6,5},{7,6},{8,11},{9,8},{10,9... | collective-permute-start | bytes 15368 | tf_op jit(solution)/shard_map/ppermute | solution.py:23
  5.3 0.8 multiply_multiply_fusion
  6.1 0.7 pad.8.w_last
  6.8 0.7 pad.7.w_first
  7.5 0.1 reshape.17.table
  7.6 0.0 collective-permute-done.1
  7.6 0.0 collective-permute-done
  7.6 0.1 concatenate.13.fields
  7.9 2.3 %collective-permute-start.2 = (f32[7,2176]{1,0:T(8,128)S(1)}, f32[7,2176]{1,0:T(8,128)S(1)}, u32[]{:S(2)}, u32[]{:S(2)}) collective-permute-start(f32[7,2176]{1,0:T(8,128)S(1)} %pad_maximum_fusion.1), channel_id=1, source_target_pairs={{0,4},{4,8},{8,12},{12,16},{16,20},{20,24},{24,28},{28,0},{1,5},{5... | collective-permute-start | bytes 182792 | tf_op jit(solution)/shard_map/ppermute | solution.py:701
  10.2 3.1 %collective-permute-start.3 = (f32[7,2176]{1,0:T(8,128)S(1)}, f32[7,2176]{1,0:T(8,128)S(1)}, u32[]{:S(2)}, u32[]{:S(2)}) collective-permute-start(f32[7,2176]{1,0:T(8,128)S(1)} %pad_maximum_fusion.2), channel_id=1, source_target_pairs={{0,28},{4,0},{8,4},{12,8},{16,12},{20,16},{24,20},{28,24},{1,29},{... | collective-permute-start | bytes 182792 | tf_op jit(solution)/shard_map/ppermute | solution.py:702
  13.3 0.0 copy-done
  13.3 8.8 %inner.1 = (f32[17,64,128]{2,1,0:T(8,128)S(1)}, bf16[4,12288,128]{2,1,0:T(8,128)(2,1)}, bf16[16,12288]{1,0:T(8,128)(2,1)S(1)}) custom-call(f32[10,8,2176]{2,1,0:T(8,128)S(1)} %concatenate.13.fields, bf16[16,128]{1,0:T(8,128)(2,1)S(1)} %pad.7.w_first, bf16[3,128,128]{2,1,0:T(8,128)(2,1)S(1)} %copy-done, bf16[16,128]{1,0:T(8,128)(2,1)S(1)} %pad.8.w_last), custom_call_target="tpu_custom_call" | custom-call | tf_op jit(solution)/shard_map/inner/pallas_call | solution.py:660
  22.2 2.1 %collective-permute-start.7 = (f32[4,6,2176]{2,1,0:T(8,128)S(1)}, f32[4,6,2176]{2,1,0:T(8,128)S(1)}, u32[]{:S(2)}, u32[]{:S(2)}) collective-permute-start(f32[4,6,2176]{2,1,0:T(8,128)S(1)} %get-tuple-element.53), channel_id=1, source_target_pairs={{0,28},{4,0},{8,4},{12,8},{16,12},{20,16},{24,20},{28,24},{1,29},{... | collective-permute-start | bytes 626696 | tf_op jit(solution)/shard_map/ppermute | solution.py:23
  24.2 0.0 collective-permute-start.6
  24.2 0.0 collective-permute-done.2.up
  24.2 0.0 collective-permute-done.3.down
  24.2 10.8 %outer.1 = (f32[3,8,2176]{2,1,0:T(8,128)S(1)}, f32[3,8,2048]{2,1,0:T(8,128)}, bf16[4,4096,128]{2,1,0:T(8,128)(2,1)}, bf16[16,4096]{1,0:T(8,128)(2,1)S(1)}) custom-call(f32[288]{0:T(512)S(1)} %reshape.17.table, f32[10,8,2176]{2,1,0:T(8,128)S(1)} %concatenate.13.fields, f32[7,2176]{1,0:T(8,128)S(1)} %collective-permute-done.2.up, ...), custom_call_target="tpu_custom_call" | custom-call | tf_op jit(solution)/shard_map/outer/pallas_call | solution.py:660
  35.1 4.8 %collective-permute-start.5 = (f32[3,8,2176]{2,1,0:T(8,128)S(1)}, f32[3,8,2176]{2,1,0:T(8,128)S(1)}, u32[]{:S(2)}, u32[]{:S(2)}) collective-permute-start(f32[3,8,2176]{2,1,0:T(8,128)S(1)} %get-tuple-element.26.r_mid), channel_id=1, source_target_pairs={{0,28},{4,0},{8,4},{12,8},{16,12},{20,16},{24,20},{28,24},{1,29},{... | collective-permute-start | bytes 626696 | tf_op jit(solution)/shard_map/ppermute | solution.py:23
  39.9 0.0 collective-permute-start.4
  39.9 1.4 %slice_reduce_fusion = (f32[]{:T(128)}, f32[]{:T(128)}) fusion(f32[8,6,6]{2,0,1:T(8,128)} %param.13), kind=kLoop, calls=%fused_computation.13 | loop fusion | flops 14 | bytes 72 | tf_op jit(solution)/shard_map/reduce_sum | solution.py:643
  42.7 0.1 stack.39.numbers
  42.7 0.0 collective-permute-done.7.fl_down
  42.7 0.0 collective-permute-done.6.fl_up
  42.8 2.1 %prepare.1 = (f32[21,24,2176]{2,1,0:T(8,128)S(1)}, f32[3,24,2176]{2,1,0:T(8,128)S(1)}) custom-call(f32[288]{0:T(512)S(1)} %reshape.17.table, f32[10,8,2176]{2,1,0:T(8,128)S(1)} %concatenate.13.fields, f32[4,6,2176]{2,1,0:T(8,128)S(1)} %collective-permute-done.6.fl_up, f32[4,6,2176]{2,1,0:T(8,128)S(1)} %collective-permute-done.7.fl_down), custom_call_target="tpu_custom_call" | custom-call | tf_op jit(solution)/shard_map/prepare/pallas_call | solution.py:660
  44.9 0.0 collective-permute-done.5.r_down
  44.9 4.3 %collective-permute-done.4.r_up = f32[3,8,2176]{2,1,0:T(8,128)S(1)} collective-permute-done((f32[3,8,2176]{2,1,0:T(8,128)S(1)}, f32[3,8,2176]{2,1,0:T(8,128)S(1)}, u32[]{:S(2)}, u32[]{:S(2)}) %collective-permute-start.4) | collective-permute-done | bytes 208928 | tf_op jit(solution)/shard_map/ppermute | solution.py:22
  49.2 15.3 %krylov.1 = (f32[4,3,24,2176]{3,2,1,0:T(8,128)S(1)}, f32[32,1,128]{2,1,0:T(1,128)S(1)}) custom-call(f32[9]{0:T(128)S(1)} %stack.39.numbers, f32[3,8,2176]{2,1,0:T(8,128)S(1)} %get-tuple-element.26.r_mid, f32[3,8,2176]{2,1,0:T(8,128)S(1)} %collective-permute-done.4.r_up, f32[3,8,2176]{2,1,0:T(8,128)S(1)} %collective-permute-done.5.r_down, ...), custom_call_target="tpu_custom_call" | custom-call | tf_op jit(solution)/shard_map/krylov/pallas_call | solution.py:660
  64.5 9.5 %all_to_all.15.sums = f32[32,1,128]{2,1,0:T(1,128)S(1)} all-to-all(f32[32,1,128]{2,1,0:T(1,128)S(1)} %get-tuple-element.30), channel_id=1, replica_groups=mesh['patch'=8,'sub'=4] {'patch','sub'}, dimensions={0} | all-to-all | bytes 32768 | tf_op jit(solution)/shard_map/all_to_all | solution.py:28
  74.0 14.2 %backward.1 = (f32[3,8,2048]{2,1,0:T(8,128)}, f32[32,13,128]{2,1,0:T(8,128)S(1)}) custom-call(f32[9]{0:T(128)S(1)} %stack.39.numbers, f32[32,1,128]{2,1,0:T(1,128)S(1)} %all_to_all.15.sums, f32[4,3,24,2176]{3,2,1,0:T(8,128)S(1)} %get-tuple-element.31.basis, bf16[4,12288,128]{2,1,0:T(8,128)(2,1)} %get-tuple-element.32.inner_hidden, ...), custom_call_target="tpu_custom_call" | custom-call | tf_op jit(solution)/shard_map/backward/pallas_call | solution.py:660
  88.2 12.3 %all_to_all.16.parts = f32[32,13,128]{2,1,0:T(8,128)S(1)} all-to-all(f32[32,13,128]{2,1,0:T(8,128)S(1)} %get-tuple-element.37), channel_id=1, replica_groups=mesh['patch'=8,'sub'=4] {'patch','sub'}, dimensions={0} | all-to-all | bytes 425984 | tf_op jit(solution)/shard_map/all_to_all | solution.py:28
  100.5 0.1 gather.1
  100.6 12.7 %all_to_all.17.parts = f32[32,13,128]{2,1,0:T(8,128)S(1)} all-to-all(f32[32,13,128]{2,1,0:T(8,128)S(1)} %gather.1), channel_id=1, replica_groups=mesh['patch'=8,'sub'=4] {'patch','sub'}, dimensions={0} | all-to-all | bytes 425984 | tf_op jit(solution)/shard_map/all_to_all | solution.py:28
  113.3 0.7 deliver.1
  (8 shorter events, 0.2 us)
Async XLA Ops:
  0.6 12.7 %copy-start = (bf16[3,128,128]{2,1,0:T(8,128)(2,1)S(1)}, bf16[3,128,128]{2,1,0:T(8,128)(2,1)}, u32[]{:S(2)}) copy-start(bf16[3,128,128]{2,1,0:T(8,128)(2,1)} %w_mid.5) | copy-start | bytes 294916
  2.8 4.8 %collective-permute-start.1 = (f32[10,8,16]{2,1,0:T(8,128)S(1)}, f32[10,8,16]{2,1,0:T(8,128)S(1)}, u32[]{:S(2)}, u32[]{:S(2)}) collective-permute-start(f32[10,8,16]{2,1,0:T(8,128)S(1)} %get-tuple-element.51), channel_id=1, source_target_pairs={{0,1},{1,2},{2,3},{3,0},{4,5},{5,6},{6,7},{7,4},{8,9},{9,10},{10,1... | collective-permute-start | bytes 15368 | tf_op jit(solution)/shard_map/ppermute | solution.py:22
  3.3 4.4 %collective-permute-start = (f32[10,8,16]{2,1,0:T(8,128)S(1)}, f32[10,8,16]{2,1,0:T(8,128)S(1)}, u32[]{:S(2)}, u32[]{:S(2)}) collective-permute-start(f32[10,8,16]{2,1,0:T(8,128)S(1)} %get-tuple-element.52), channel_id=1, source_target_pairs={{0,3},{1,0},{2,1},{3,2},{4,7},{5,4},{6,5},{7,6},{8,11},{9,8},{10,9... | collective-permute-start | bytes 15368 | tf_op jit(solution)/shard_map/ppermute | solution.py:23
  7.9 16.4 %collective-permute-start.2 = (f32[7,2176]{1,0:T(8,128)S(1)}, f32[7,2176]{1,0:T(8,128)S(1)}, u32[]{:S(2)}, u32[]{:S(2)}) collective-permute-start(f32[7,2176]{1,0:T(8,128)S(1)} %pad_maximum_fusion.1), channel_id=1, source_target_pairs={{0,4},{4,8},{8,12},{12,16},{16,20},{20,24},{24,28},{28,0},{1,5},{5... | collective-permute-start | bytes 182792 | tf_op jit(solution)/shard_map/ppermute | solution.py:701
  10.2 14.1 %collective-permute-start.3 = (f32[7,2176]{1,0:T(8,128)S(1)}, f32[7,2176]{1,0:T(8,128)S(1)}, u32[]{:S(2)}, u32[]{:S(2)}) collective-permute-start(f32[7,2176]{1,0:T(8,128)S(1)} %pad_maximum_fusion.2), channel_id=1, source_target_pairs={{0,28},{4,0},{8,4},{12,8},{16,12},{20,16},{24,20},{28,24},{1,29},{... | collective-permute-start | bytes 182792 | tf_op jit(solution)/shard_map/ppermute | solution.py:702
  22.2 20.6 %collective-permute-start.7 = (f32[4,6,2176]{2,1,0:T(8,128)S(1)}, f32[4,6,2176]{2,1,0:T(8,128)S(1)}, u32[]{:S(2)}, u32[]{:S(2)}) collective-permute-start(f32[4,6,2176]{2,1,0:T(8,128)S(1)} %get-tuple-element.53), channel_id=1, source_target_pairs={{0,28},{4,0},{8,4},{12,8},{16,12},{20,16},{24,20},{28,24},{1,29},{... | collective-permute-start | bytes 626696 | tf_op jit(solution)/shard_map/ppermute | solution.py:23
  24.2 18.5 %collective-permute-start.6 = (f32[4,6,2176]{2,1,0:T(8,128)S(1)}, f32[4,6,2176]{2,1,0:T(8,128)S(1)}, u32[]{:S(2)}, u32[]{:S(2)}) collective-permute-start(f32[4,6,2176]{2,1,0:T(8,128)S(1)} %get-tuple-element.54), channel_id=1, source_target_pairs={{0,4},{4,8},{8,12},{12,16},{16,20},{20,24},{24,28},{28,0},{1,5},{5... | collective-permute-start | bytes 626696 | tf_op jit(solution)/shard_map/ppermute | solution.py:22
  35.1 9.8 %collective-permute-start.5 = (f32[3,8,2176]{2,1,0:T(8,128)S(1)}, f32[3,8,2176]{2,1,0:T(8,128)S(1)}, u32[]{:S(2)}, u32[]{:S(2)}) collective-permute-start(f32[3,8,2176]{2,1,0:T(8,128)S(1)} %get-tuple-element.26.r_mid), channel_id=1, source_target_pairs={{0,28},{4,0},{8,4},{12,8},{16,12},{20,16},{24,20},{28,24},{1,29},{... | collective-permute-start | bytes 626696 | tf_op jit(solution)/shard_map/ppermute | solution.py:23
  39.9 9.3 %collective-permute-start.4 = (f32[3,8,2176]{2,1,0:T(8,128)S(1)}, f32[3,8,2176]{2,1,0:T(8,128)S(1)}, u32[]{:S(2)}, u32[]{:S(2)}) collective-permute-start(f32[3,8,2176]{2,1,0:T(8,128)S(1)} %get-tuple-element.26.r_mid), channel_id=1, source_target_pairs={{0,4},{4,8},{8,12},{12,16},{16,20},{20,24},{24,28},{28,0},{1,5},{5... | collective-permute-start | bytes 626696 | tf_op jit(solution)/shard_map/ppermute | solution.py:22

commit v4 on v3

--- a/solution.py
+++ b/solution.py
@@ -4,6 +4,7 @@
 from jax.experimental import pallas as pl
 from jax.experimental.pallas import tpu as pltpu
 from jax.sharding import PartitionSpec as P
+
 
 HY = 16
 LANES = 128
@@ -224,7 +225,7 @@
 
 
 def inner_kernel(
-    fields, w_first, w_mid, w_last, learned, stored, inputs, before, after, strain, hidden, flags
+    fields, ends, w_mid, learned, stored, inputs, before, after, strain, hidden, flags
 ):
     rows, wide = fields.shape[1], fields.shape[2]
     tiles = wide // LANES
@@ -251,7 +252,7 @@
         return carry
 
     lax.fori_loop(0, tiles, strains, 0)
-    weights = (w_first, w_mid, w_last)
+    weights = (ends.at[0:PADDED], w_mid, ends.at[PADDED : 2 * PADDED])
 
     def line(row, carry):
         learn_line(row, row - 1, strain, learned, rows, cols, weights, hidden, inputs)
@@ -301,7 +302,7 @@
 
 
 def outer_kernel(
-    table, fields, up, down, inner, w_first, w_mid, w_last,
+    table, fields, up, down, inner, ends, w_mid,
     residual, own_residual, stored, inputs,
     centre, before, after, ahead, behind, middle, strain, learned, stiff, hidden, flags,
 ):
@@ -345,7 +346,7 @@
         return carry
 
     lax.fori_loop(0, tiles, strains, 0)
-    weights = (w_first, w_mid, w_last)
+    weights = (ends.at[0:PADDED], w_mid, ends.at[PADDED : 2 * PADDED])
     rim_rows = (rows - 1, rows, 2 * rows - 1, 2 * rows)
     for row, line in zip(rim_rows, (None, 0, 1, None)):
         learn_line(row, line, strain, learned, tall, cols, weights, hidden, inputs)
@@ -389,12 +390,9 @@
         line_copy(n, cols, hidden, stored, flags).wait()
 
 
-def solve(numbers, sums, basis, adjoint, upstream, combined):
+def solve(numbers, sums, kept, bends, adjoint, upstream):
     rows = adjoint.shape[1]
-    wide = basis.shape[3]
-    tiles = wide // LANES
-    own_tiles = tiles - 1
-    tall = 3 * rows
+    own_tiles = upstream.shape[0]
     line = jnp.sum(sums[...], axis=0)
     picks = [jnp.broadcast_to(line[:, n : n + 1], (1, LANES)) for n in range(SUMS)]
     centre = [numbers[k] for k in range(3)]
@@ -408,37 +406,27 @@
         value = width[j] * cross[j + 1] + centre[j] * cross[j]
         matrix[j][3] = value + width[j - 1] * cross[j - 1] if j else value
     matrix[3][3] = picks[13]
-    weights = [jnp.broadcast_to(x, (tall, LANES)) for x in galerkin(matrix, picks[:4])]
+    weights = [jnp.broadcast_to(x, (rows, LANES)) for x in galerkin(matrix, picks[:4])]
+
+    def weighted(parts):
+        total = weights[0] * parts[0]
+        for weight, part in zip(weights[1:], parts[1:]):
+            total = total + weight * part
+        return total
+
+    levels = range(DEGREE + 1)
 
     def combine(tile, carry):
         at = lanes_of(tile)
         for c in range(3):
-            value = weights[0] * basis[0, c, :, at]
-            for k in range(1, DEGREE + 1):
-                value = value + weights[k] * basis[k, c, :, at]
-            combined[c, :, at] = value
-            combined[3 + c, :, at] = pltpu.roll(value, 1, 1)
-            combined[6 + c, :, at] = pltpu.roll(value, LANES - 1, 1)
-        return carry
-
-    lax.fori_loop(0, tiles, combine, 0)
-    lane = lax.broadcasted_iota(jnp.int32, (tall, LANES), 1)
-    first, final = lane == 0, lane == LANES - 1
-
-    def strain(tile, carry):
-        at = lanes_of(tile)
-        triples = triples_of(
-            combined.at[0:3], combined.at[3:6], combined.at[6:9], tile, tiles, first, final
-        )
-        for c in range(3):
-            adjoint[c, :, at] = combined[c, rows : 2 * rows, at]
-        for n, value in enumerate(spread_strains(*triples)):
-            upstream[tile, n * rows : (n + 1) * rows] = HALVING[n] * value[rows : 2 * rows]
-        for n in range(6, FIELDS):
-            upstream[tile, n * rows : (n + 1) * rows] = jnp.zeros((rows, LANES), jnp.float32)
-        return carry
-
-    lax.fori_loop(0, own_tiles, strain, 0)
+            adjoint[c, :, at] = weighted([kept[k, c, :, at] for k in levels])
+        for n in range(6):
+            here = slice(n * rows, (n + 1) * rows)
+            upstream[tile, here] = HALVING[n] * weighted([bends[k, tile, here] for k in levels])
+        upstream[tile, 6 * rows :] = jnp.zeros(((FIELDS - 6) * rows, LANES), jnp.float32)
+        return carry
+
+    lax.fori_loop(0, own_tiles, combine, 0)
 
 
 def slope_of(signal, h):
@@ -447,9 +435,9 @@
 
 
 def backward_kernel(
-    numbers, sums, basis, inner_hidden, inner_inputs, outer_hidden, outer_inputs, w_mid, w_last,
-    adjoint, packed,
-    combined, upstream, grads, near_hidden, far_hidden, near_flags, far_flags,
+    numbers, sums, kept, bends, inner_hidden, inner_inputs, outer_hidden, outer_inputs, w_mid,
+    ends, adjoint, packed,
+    upstream, grads, near_hidden, far_hidden, near_flags, far_flags,
 ):
     layers = w_mid.shape[0]
     hid = w_mid.shape[1]
@@ -462,7 +450,7 @@
     for n in range(2):
         line_copy(n, cols, outer_hidden, far_hidden, far_flags).start()
     grads[...] = jnp.zeros_like(grads)
-    solve(numbers, sums, basis, adjoint, upstream, combined)
+    solve(numbers, sums, kept, bends, adjoint, upstream)
 
     def line(row, at_line, hidden, inputs):
         for at, size in pieces_of(cols):
@@ -473,7 +461,7 @@
             signal = widened(gathered(upstream, row, rows, at, size))
             h = hidden[layers, here, :]
             grads[last_at : last_at + FIELDS] += contract(signal, h, 1, 0)[:FIELDS]
-            d = slope_of(contract(signal, w_last[...], 0, 0), h)
+            d = slope_of(contract(signal, ends[PADDED : 2 * PADDED], 0, 0), h)
             for k in range(layers - 1, -1, -1):
                 h = hidden[k, here, :]
                 grads[k * hid : (k + 1) * hid] += contract(d, h, 0, 0)
@@ -491,7 +479,8 @@
         line(row, n, far_hidden, outer_inputs)
     chunk = packed.shape[1]
     for n in range(packed.shape[0]):
-        packed[n] = grads[n * chunk : (n + 1) * chunk]
+        for r in range(chunk):
+            packed[n, r] = grads[n * chunk + r : n * chunk + r + 1]
 
 
 def gather_kernel(parts, total):
@@ -501,7 +490,8 @@
 def deliver_kernel(parts, grad_first, grad_mid, grad_last, flat):
     chunk = parts.shape[1]
     for n in range(parts.shape[0]):
-        flat[n * chunk : (n + 1) * chunk] = parts[n]
+        for r in range(chunk):
+            flat[n * chunk + r : n * chunk + r + 1] = parts[n, r]
     layers, hid = grad_mid.shape[0], grad_mid.shape[1]
     for k in range(layers):
         grad_mid[k] = flat[k * hid : (k + 1) * hid]
@@ -511,8 +501,8 @@
 
 
 def krylov_kernel(
-    numbers, r_mid, r_up, r_down, stiff, support, basis, sums,
-    before, after, ahead, behind, middle,
+    numbers, r_mid, r_up, r_down, stiff, support, kept, bends, sums,
+    basis, before, after, ahead, behind, middle,
 ):
     rows = r_mid.shape[1]
     wide = r_mid.shape[2]
@@ -521,8 +511,10 @@
     tall = 3 * rows
     lane = lax.broadcasted_iota(jnp.int32, (tall, LANES), 1)
     first, final = lane == 0, lane == LANES - 1
+
     def place(k, c, at, value):
         basis[k, c, :, at] = value
+        kept[k, c, :, at] = value[rows : 2 * rows]
         before[c, :, at] = pltpu.roll(value, 1, 1)
         after[c, :, at] = pltpu.roll(value, LANES - 1, 1)
 
@@ -536,7 +528,10 @@
     lax.fori_loop(0, tiles, set_up, 0)
 
     def strain_of(k, tile):
-        return spread_strains(*triples_of(basis.at[k], before, after, tile, tiles, first, final))
+        e = spread_strains(*triples_of(basis.at[k], before, after, tile, tiles, first, final))
+        for n in range(6):
+            bends[k, tile, n * rows : (n + 1) * rows] = e[n][rows : 2 * rows]
+        return e
 
     def stress_of(e, at):
         return mixed([stiff[n, :, at] for n in range(len(UPPER))], e)
@@ -560,7 +555,7 @@
 
         lax.fori_loop(0, tiles, push, 0)
 
-        centre, width, inverse = numbers[k], numbers[3 + k], numbers[6 + k]
+        centre, inverse = numbers[k], numbers[6 + k]
         former = numbers[2 + k]
 
         def advance(tile, carry, k=k):
@@ -659,7 +654,6 @@
         specs[n] = IN_PLACE
     return pl.pallas_call(
         body,
-        name=name,
         in_specs=specs,
         out_specs=[IN_PLACE if n in far_outs else ON_CHIP for n in range(len(outs))],
         out_shape=[
@@ -700,14 +694,15 @@
     ]
     up = lax.ppermute(sends[0], "patch", ring("patch", 1))
     down = lax.ppermute(sends[1], "patch", ring("patch", -1))
+    fl_up, fl_down = from_both(fields[3:7], "patch", 1, 6)
 
     halving = jnp.array(HALVING, f32)
     table = (layup_stiffness * halving[:, None] * halving[None, :]).reshape(-1)
     centres, widths = basis_constants(layup_stiffness)
     numbers = jnp.stack(centres + widths + [1.0 / x for x in widths])
     thin = w_first.shape[1]
-    first_pad = jnp.pad(w_first.T, ((0, PADDED - thin), (0, 0)))
-    last_pad = jnp.pad(w_last, ((0, PADDED - thin), (0, 0)))
+    blank = jnp.zeros((PADDED - thin, hid), bf16)
+    ends = jnp.concatenate([w_first.T, blank, w_last, blank])
 
     learned, inner_hidden, inner_inputs = kernel_call(
         inner_kernel, "inner", 0,
@@ -716,10 +711,8 @@
         [((3, rows, wide), f32)] * 2
         + [((tiles, FIELDS * rows, LANES), f32), ((layers + 1, (rows - 2) * cols, hid), bf16),
            rows - 2],
-        fields, first_pad, w_mid, last_pad, far_outs=(1,),
-    )
-    learned, distant = lax.optimization_barrier((learned, fields[3:7]))
-    fl_up, fl_down = from_both(distant, "patch", 1, 6)
+        fields, ends, w_mid, far_outs=(1,),
+    )
     wide_residual, residual, outer_hidden, outer_inputs = kernel_call(
         outer_kernel, "outer", 1,
         [((3, rows, wide), f32), ((3, rows, cols), f32),
@@ -727,7 +720,7 @@
         [((3, tall, wide), f32)] * 6
         + [((tiles, FIELDS * tall, LANES), f32)] * 2
         + [((len(UPPER), tall, wide), f32), ((layers + 1, 2 * cols, hid), bf16), 2],
-        table, fields, up, down, learned, first_pad, w_mid, last_pad, far_outs=(2,),
+        table, fields, up, down, learned, ends, w_mid, far_outs=(2,),
     )
     stiff, support = kernel_call(
         prepare_kernel, "prepare", 1,
@@ -735,10 +728,11 @@
         table, fields, fl_up, fl_down,
     )
     up, down = from_both(wide_residual, "patch", 1, rows)
-    basis, sums = kernel_call(
+    kept, bends, sums = kernel_call(
         krylov_kernel, "krylov", 1,
-        [((DEGREE + 1, 3, tall, wide), f32), ((devices, 1, LANES), f32)],
-        [((3, tall, wide), f32)] * 5,
+        [((DEGREE + 1, 3, rows, wide), f32), ((DEGREE + 1, tiles, 6 * rows, LANES), f32),
+         ((devices, 1, LANES), f32)],
+        [((DEGREE + 1, 3, tall, wide), f32)] + [((3, tall, wide), f32)] * 5,
         numbers, wide_residual, up, down, stiff, support,
     )
     sums = everyone(sums)
@@ -746,12 +740,12 @@
     chunk = -(-count // devices)
     adjoint, packed = kernel_call(
         backward_kernel, "backward", 1,
-        [((3, rows, cols), f32), ((devices, chunk, LANES), f32)],
-        [((9, tall, wide), f32), ((tiles - 1, FIELDS * rows, LANES), f32),
+        [((3, rows, cols), f32), ((devices, chunk, 1, LANES), f32)],
+        [((tiles - 1, FIELDS * rows, LANES), f32),
          ((devices * chunk, LANES), f32), ((layers + 1, (rows - 2) * cols, hid), bf16),
          ((layers + 1, 2 * cols, hid), bf16), rows - 2, 2],
-        numbers, sums, basis, inner_hidden, inner_inputs, outer_hidden, outer_inputs,
-        w_mid, last_pad, far=(3, 5),
+        numbers, sums, kept, bends, inner_hidden, inner_inputs, outer_hidden, outer_inputs,
+        w_mid, ends, far=(4, 6),
     )
     (total,) = kernel_call(
         gather_kernel, "gather", 0, [(packed.shape, f32)], [], everyone(packed)

time: 114 us -> 112 us (0.982)
  blocking collectives: 34.4 us -> 32.2 us
  local copies, waits for them, and re-layouts: 1.88 us -> 0.49 us
    all_to_all x3, blocking collectives: 34.4 us -> 32.2 us  [everyone(): return lax.all_to_all(rows, AXES, 0, 0, tiled=True)]
    pad x2 -> x0, local copies, waits for them, and re-layouts: 1.38 us -> none  [the longest x1 0.69 us: per_device(): last_pad = jnp.pad(w_last, ((0, PADDED - thin), (0, 0)))]
  transfers between devices with their start and end apart: 8 -> 8, of which waited for: 1 -> 3; matrix products, arithmetic and copies ran while one was open for 3% -> 3% of each run, Pallas kernels for 19% -> 20%
where the time goes in v4:
time: 112 us; the launch traced here: 111 us
  Pallas kernels  51.5 us (46%)
  blocking collectives  32.2 us (29%)
  starting transfers between devices  14.5 us (13%)
  waiting for transfers between devices  5.21 us (5%)
  other arithmetic  5.03 us (4%)
  between operations  2.19 us (2%)
    pallas_call x7, Pallas kernels, kernel_call(): pl.pallas_call(body, in_specs=specs, out_specs=[IN_PLACE if n in far_outs...  51.5 us
    all_to_all x3, blocking collectives, everyone(): return lax.all_to_all(rows, AXES, 0, 0, tiled=True)  32.2 us
    ppermute x3, starting transfers between devices, from_both(): after = lax.ppermute(head, axis, ring(axis, -1))  8.82 us
    ppermute x3, waiting for transfers between devices, from_both(): before = lax.ppermute(tail, axis, ring(axis, 1))  4.9 us
    ppermute x1, starting transfers between devices, per_device(): down = lax.ppermute(sends[1], 'patch', ring('patch', -1))  3.11 us
  transfers between devices with their start and end apart: 8, of which 3 were waited for; matrix products, arithmetic and copies ran while one was open for 3% of the time, Pallas kernels for 20%

profile of v4, /device:TPU:0, one launch (start us, length us, event | category | flops | bytes accessed | tf_op | source)
XLA Modules:
  0.0 111.2 jit_solution(3746770662888295283)
XLA Ops:
  0.6 0.0 copy-start
  0.6 0.9 convert_bitcast_fusion
  1.5 1.2 %pad_maximum_fusion = f32[10,8,2048]{2,1,0:T(8,128)S(1)} fusion(f32[3,8,2048]{2,1,0:T(8,128)} %param.10, f32[1,8,2048]{2,1,0:T(8,128)S(1)} %convert_bitcast_fusion, f32[3,8,2048]{2,1,0:T(8,128)} %param.11, f32[3,8,2048]{2,1,0:T(8,128)} %param.9), kind=kLoop, calls=%fused_computation | loop fusion | flops 491520 | bytes 1310720 | tf_op jit(solution)/shard_map/concatenate | solution.py:687
  2.7 0.1 fusion.1
  2.8 0.5 collective-permute-start.1
  3.3 2.0 %collective-permute-start = (f32[10,8,16]{2,1,0:T(8,128)S(1)}, f32[10,8,16]{2,1,0:T(8,128)S(1)}, u32[]{:S(2)}, u32[]{:S(2)}) collective-permute-start(f32[10,8,16]{2,1,0:T(8,128)S(1)} %get-tuple-element.52), channel_id=1, source_target_pairs={{0,3},{1,0},{2,1},{3,2},{4,7},{5,4},{6,5},{7,6},{8,11},{9,8},{10,9... | collective-permute-start | bytes 15368 | tf_op jit(solution)/shard_map/ppermute | solution.py:24
  5.3 0.8 multiply_multiply_fusion
  6.1 0.7 pad_maximum_fusion.3.ends
  6.8 0.1 reshape.17.table
  6.9 0.0 collective-permute-done.1
  6.9 0.2 collective-permute-done
  7.2 0.1 concatenate.16.fields
  7.4 2.1 %collective-permute-start.2 = (f32[7,2176]{1,0:T(8,128)S(1)}, f32[7,2176]{1,0:T(8,128)S(1)}, u32[]{:S(2)}, u32[]{:S(2)}) collective-permute-start(f32[7,2176]{1,0:T(8,128)S(1)} %pad_maximum_fusion.1), channel_id=1, source_target_pairs={{0,4},{4,8},{8,12},{12,16},{16,20},{20,24},{24,28},{28,0},{1,5},{5... | collective-permute-start | bytes 182792 | tf_op jit(solution)/shard_map/ppermute | solution.py:695
  9.5 3.1 %collective-permute-start.3 = (f32[7,2176]{1,0:T(8,128)S(1)}, f32[7,2176]{1,0:T(8,128)S(1)}, u32[]{:S(2)}, u32[]{:S(2)}) collective-permute-start(f32[7,2176]{1,0:T(8,128)S(1)} %pad_maximum_fusion.2), channel_id=1, source_target_pairs={{0,28},{4,0},{8,4},{12,8},{16,12},{20,16},{24,20},{28,24},{1,29},{... | collective-permute-start | bytes 182792 | tf_op jit(solution)/shard_map/ppermute | solution.py:696
  12.6 2.1 %collective-permute-start.7 = (f32[4,6,2176]{2,1,0:T(8,128)S(1)}, f32[4,6,2176]{2,1,0:T(8,128)S(1)}, u32[]{:S(2)}, u32[]{:S(2)}) collective-permute-start(f32[4,6,2176]{2,1,0:T(8,128)S(1)} %get-tuple-element.41), channel_id=1, source_target_pairs={{0,28},{4,0},{8,4},{12,8},{16,12},{20,16},{24,20},{28,24},{1,29},{... | collective-permute-start | bytes 626696 | tf_op jit(solution)/shard_map/ppermute | solution.py:24
  14.7 0.0 collective-permute-start.6
  14.7 0.0 copy-done
  14.7 8.8 %shard_map.128 = (f32[17,64,128]{2,1,0:T(8,128)S(1)}, bf16[4,12288,128]{2,1,0:T(8,128)(2,1)}, bf16[16,12288]{1,0:T(8,128)(2,1)S(1)}) custom-call(f32[10,8,2176]{2,1,0:T(8,128)S(1)} %concatenate.16.fields, bf16[32,128]{1,0:T(8,128)(2,1)S(1)} %pad_maximum_fusion.3.ends, bf16[3,128,128]{2,1,0:T(8,128)(2,1)S(1)} %copy-done), custom_call_target="tpu_custom_call" | custom-call | tf_op jit(solution)/shard_map/pallas_call | solution.py:655
  23.5 0.0 collective-permute-done.2.up
  23.5 0.0 collective-permute-done.3.down
  23.6 10.8 %shard_map.129 = (f32[3,8,2176]{2,1,0:T(8,128)S(1)}, f32[3,8,2048]{2,1,0:T(8,128)}, bf16[4,4096,128]{2,1,0:T(8,128)(2,1)}, bf16[16,4096]{1,0:T(8,128)(2,1)S(1)}) custom-call(f32[288]{0:T(512)S(1)} %reshape.17.table, f32[10,8,2176]{2,1,0:T(8,128)S(1)} %concatenate.16.fields, f32[7,2176]{1,0:T(8,128)S(1)} %collective-permute-done.2.up, ...), custom_call_target="tpu_custom_call" | custom-call | tf_op jit(solution)/shard_map/pallas_call | solution.py:655
  34.4 4.8 %collective-permute-start.5 = (f32[3,8,2176]{2,1,0:T(8,128)S(1)}, f32[3,8,2176]{2,1,0:T(8,128)S(1)}, u32[]{:S(2)}, u32[]{:S(2)}) collective-permute-start(f32[3,8,2176]{2,1,0:T(8,128)S(1)} %get-tuple-element.24.r_mid), channel_id=1, source_target_pairs={{0,28},{4,0},{8,4},{12,8},{16,12},{20,16},{24,20},{28,24},{1,29},{... | collective-permute-start | bytes 626696 | tf_op jit(solution)/shard_map/ppermute | solution.py:24
  39.2 0.0 collective-permute-start.4
  39.2 1.4 %slice_reduce_fusion = (f32[]{:T(128)}, f32[]{:T(128)}) fusion(f32[8,6,6]{2,0,1:T(8,128)} %param.13), kind=kLoop, calls=%fused_computation.14 | loop fusion | flops 14 | bytes 72 | tf_op jit(solution)/shard_map/reduce_sum | solution.py:638
  42.0 0.1 stack.39.numbers
  42.1 0.0 collective-permute-done.7.fl_down
  42.1 0.0 collective-permute-done.6.fl_up
  42.1 2.1 %shard_map.130 = (f32[21,24,2176]{2,1,0:T(8,128)S(1)}, f32[3,24,2176]{2,1,0:T(8,128)S(1)}) custom-call(f32[288]{0:T(512)S(1)} %reshape.17.table, f32[10,8,2176]{2,1,0:T(8,128)S(1)} %concatenate.16.fields, f32[4,6,2176]{2,1,0:T(8,128)S(1)} %collective-permute-done.6.fl_up, f32[4,6,2176]{2,1,0:T(8,128)S(1)} %collective-permute-done.7.fl_down), custom_call_target="tpu_custom_call" | custom-call | tf_op jit(solution)/shard_map/pallas_call | solution.py:655
  44.2 0.1 collective-permute-done.5.r_down
  44.2 4.9 %collective-permute-done.4.r_up = f32[3,8,2176]{2,1,0:T(8,128)S(1)} collective-permute-done((f32[3,8,2176]{2,1,0:T(8,128)S(1)}, f32[3,8,2176]{2,1,0:T(8,128)S(1)}, u32[]{:S(2)}, u32[]{:S(2)}) %collective-permute-start.4) | collective-permute-done | bytes 208928 | tf_op jit(solution)/shard_map/ppermute | solution.py:23
  49.1 15.3 %shard_map.131 = (f32[4,3,8,2176]{3,2,1,0:T(8,128)S(1)}, f32[4,17,48,128]{3,2,1,0:T(8,128)S(1)}, f32[32,1,128]{2,1,0:T(1,128)S(1)}) custom-call(f32[9]{0:T(128)S(1)} %stack.39.numbers, f32[3,8,2176]{2,1,0:T(8,128)S(1)} %get-tuple-element.24.r_mid, f32[3,8,2176]{2,1,0:T(8,128)S(1)} %collective-permute-done.4.r_up, ...), custom_call_target="tpu_custom_call" | custom-call | tf_op jit(solution)/shard_map/pallas_call | solution.py:655
  64.5 9.5 %all_to_all.15.sums = f32[32,1,128]{2,1,0:T(1,128)S(1)} all-to-all(f32[32,1,128]{2,1,0:T(1,128)S(1)} %get-tuple-element.27), channel_id=1, replica_groups=mesh['patch'=8,'sub'=4] {'patch','sub'}, dimensions={0} | all-to-all | bytes 32768 | tf_op jit(solution)/shard_map/all_to_all | solution.py:29
  73.9 13.6 %shard_map.132 = (f32[3,8,2048]{2,1,0:T(8,128)}, f32[32,13,1,128]{3,2,1,0:T(1,128)S(1)}) custom-call(f32[9]{0:T(128)S(1)} %stack.39.numbers, f32[32,1,128]{2,1,0:T(1,128)S(1)} %all_to_all.15.sums, f32[4,3,8,2176]{3,2,1,0:T(8,128)S(1)} %get-tuple-element.28.kept, f32[4,17,48,128]{3,2,1,0:T(8,128)S(1)} %get-tuple-element.29.bends, ...), custom_call_target="tpu_custom_call" | custom-call | tf_op jit(solution)/shard_map/pallas_call | solution.py:655
  87.5 11.1 %all_to_all.16.parts = f32[32,13,1,128]{3,2,1,0:T(1,128)S(1)} all-to-all(f32[32,13,1,128]{3,2,1,0:T(1,128)S(1)} %get-tuple-element.35), channel_id=1, replica_groups=mesh['patch'=8,'sub'=4] {'patch','sub'}, dimensions={0} | all-to-all | bytes 425984 | tf_op jit(solution)/shard_map/all_to_all | solution.py:29
  98.7 0.2 shard_map.133
  98.9 11.6 %all_to_all.17.parts = f32[32,13,1,128]{3,2,1,0:T(1,128)S(1)} all-to-all(f32[32,13,1,128]{3,2,1,0:T(1,128)S(1)} %shard_map.133), channel_id=1, replica_groups=mesh['patch'=8,'sub'=4] {'patch','sub'}, dimensions={0} | all-to-all | bytes 425984 | tf_op jit(solution)/shard_map/all_to_all | solution.py:29
  110.5 0.7 shard_map.134
  (8 shorter events, 0.2 us)
Async XLA Ops:
  0.6 14.1 %copy-start = (bf16[3,128,128]{2,1,0:T(8,128)(2,1)S(1)}, bf16[3,128,128]{2,1,0:T(8,128)(2,1)}, u32[]{:S(2)}) copy-start(bf16[3,128,128]{2,1,0:T(8,128)(2,1)} %w_mid.5) | copy-start | bytes 294916
  2.8 4.2 %collective-permute-start.1 = (f32[10,8,16]{2,1,0:T(8,128)S(1)}, f32[10,8,16]{2,1,0:T(8,128)S(1)}, u32[]{:S(2)}, u32[]{:S(2)}) collective-permute-start(f32[10,8,16]{2,1,0:T(8,128)S(1)} %get-tuple-element.51), channel_id=1, source_target_pairs={{0,1},{1,2},{2,3},{3,0},{4,5},{5,6},{6,7},{7,4},{8,9},{9,10},{10,1... | collective-permute-start | bytes 15368 | tf_op jit(solution)/shard_map/ppermute | solution.py:23
  3.3 3.9 %collective-permute-start = (f32[10,8,16]{2,1,0:T(8,128)S(1)}, f32[10,8,16]{2,1,0:T(8,128)S(1)}, u32[]{:S(2)}, u32[]{:S(2)}) collective-permute-start(f32[10,8,16]{2,1,0:T(8,128)S(1)} %get-tuple-element.52), channel_id=1, source_target_pairs={{0,3},{1,0},{2,1},{3,2},{4,7},{5,4},{6,5},{7,6},{8,11},{9,8},{10,9... | collective-permute-start | bytes 15368 | tf_op jit(solution)/shard_map/ppermute | solution.py:24
  7.4 16.2 %collective-permute-start.2 = (f32[7,2176]{1,0:T(8,128)S(1)}, f32[7,2176]{1,0:T(8,128)S(1)}, u32[]{:S(2)}, u32[]{:S(2)}) collective-permute-start(f32[7,2176]{1,0:T(8,128)S(1)} %pad_maximum_fusion.1), channel_id=1, source_target_pairs={{0,4},{4,8},{8,12},{12,16},{16,20},{20,24},{24,28},{28,0},{1,5},{5... | collective-permute-start | bytes 182792 | tf_op jit(solution)/shard_map/ppermute | solution.py:695
  9.5 14.1 %collective-permute-start.3 = (f32[7,2176]{1,0:T(8,128)S(1)}, f32[7,2176]{1,0:T(8,128)S(1)}, u32[]{:S(2)}, u32[]{:S(2)}) collective-permute-start(f32[7,2176]{1,0:T(8,128)S(1)} %pad_maximum_fusion.2), channel_id=1, source_target_pairs={{0,28},{4,0},{8,4},{12,8},{16,12},{20,16},{24,20},{28,24},{1,29},{... | collective-permute-start | bytes 182792 | tf_op jit(solution)/shard_map/ppermute | solution.py:696
  12.6 29.4 %collective-permute-start.7 = (f32[4,6,2176]{2,1,0:T(8,128)S(1)}, f32[4,6,2176]{2,1,0:T(8,128)S(1)}, u32[]{:S(2)}, u32[]{:S(2)}) collective-permute-start(f32[4,6,2176]{2,1,0:T(8,128)S(1)} %get-tuple-element.41), channel_id=1, source_target_pairs={{0,28},{4,0},{8,4},{12,8},{16,12},{20,16},{24,20},{28,24},{1,29},{... | collective-permute-start | bytes 626696 | tf_op jit(solution)/shard_map/ppermute | solution.py:24
  14.7 27.4 %collective-permute-start.6 = (f32[4,6,2176]{2,1,0:T(8,128)S(1)}, f32[4,6,2176]{2,1,0:T(8,128)S(1)}, u32[]{:S(2)}, u32[]{:S(2)}) collective-permute-start(f32[4,6,2176]{2,1,0:T(8,128)S(1)} %get-tuple-element.42), channel_id=1, source_target_pairs={{0,4},{4,8},{8,12},{12,16},{16,20},{20,24},{24,28},{28,0},{1,5},{5... | collective-permute-start | bytes 626696 | tf_op jit(solution)/shard_map/ppermute | solution.py:23
  34.4 9.8 %collective-permute-start.5 = (f32[3,8,2176]{2,1,0:T(8,128)S(1)}, f32[3,8,2176]{2,1,0:T(8,128)S(1)}, u32[]{:S(2)}, u32[]{:S(2)}) collective-permute-start(f32[3,8,2176]{2,1,0:T(8,128)S(1)} %get-tuple-element.24.r_mid), channel_id=1, source_target_pairs={{0,28},{4,0},{8,4},{12,8},{16,12},{20,16},{24,20},{28,24},{1,29},{... | collective-permute-start | bytes 626696 | tf_op jit(solution)/shard_map/ppermute | solution.py:24
  39.2 10.0 %collective-permute-start.4 = (f32[3,8,2176]{2,1,0:T(8,128)S(1)}, f32[3,8,2176]{2,1,0:T(8,128)S(1)}, u32[]{:S(2)}, u32[]{:S(2)}) collective-permute-start(f32[3,8,2176]{2,1,0:T(8,128)S(1)} %get-tuple-element.24.r_mid), channel_id=1, source_target_pairs={{0,4},{4,8},{8,12},{12,16},{16,20},{20,24},{24,28},{28,0},{1,5},{5... | collective-permute-start | bytes 626696 | tf_op jit(solution)/shard_map/ppermute | solution.py:23

commit v5 on v4

--- a/solution.py
+++ b/solution.py
@@ -129,6 +129,8 @@
 MARGIN = 2
 FIELDS = 8
 PADDED = 16
+PIECES = 3
+GROUP = 9
 
 
 def triples_of(centre, before, after, tile, tiles, first, final):
@@ -304,7 +306,7 @@
 def outer_kernel(
     table, fields, up, down, inner, ends, w_mid,
     residual, own_residual, stored, inputs,
-    centre, before, after, ahead, behind, middle, strain, learned, stiff, hidden, flags,
+    centre, before, after, ahead, behind, middle, strain, learned, stiff, shifts, hidden, flags,
 ):
     rows, wide = fields.shape[1], fields.shape[2]
     tiles = wide // LANES
@@ -321,8 +323,6 @@
             above, below = up[MARGIN * c : MARGIN * (c + 1), at], down[MARGIN * c : MARGIN * (c + 1), at]
             value = jnp.concatenate([rim, above, fields[c, :, at], below, rim], axis=0)
             centre[c, :, at] = value
-            before[c, :, at] = pltpu.roll(value, 1, 1)
-            after[c, :, at] = pltpu.roll(value, LANES - 1, 1)
         wall = jnp.zeros((rows - 1, LANES), jnp.float32)
         ids = jnp.concatenate(
             [wall, up[last : last + 1, at], fields[6, :, at], down[last : last + 1, at], wall],
@@ -331,7 +331,9 @@
         stiffness_of(table, ids, depth_of(table), stiff, at)
         return carry
 
+    fill_shifts(shifts)
     lax.fori_loop(0, tiles, set_up, 0)
+    shift_both(centre, before, after, shifts)
 
     def strains(tile, carry):
         at = lanes_of(tile)
@@ -360,12 +362,14 @@
         s = mixed([stiff[n, :, at] for n in range(len(UPPER))], e)
         s = [s[n] + HALVING[n] * learned[tile, n * tall : (n + 1) * tall] for n in range(6)]
         for c, (alpha, beta, gamma) in enumerate(spread_forces(s)):
-            ahead[c, :, at] = pltpu.roll(alpha, 1, 1)
-            behind[c, :, at] = pltpu.roll(beta, LANES - 1, 1)
+            ahead[c, :, at] = alpha
+            behind[c, :, at] = beta
             middle[c, :, at] = gamma
         return carry
 
     lax.fori_loop(0, tiles, push, 0)
+    shift_in_place(ahead, 0, shifts)
+    shift_in_place(behind, 1, shifts)
     own = slice(rows, 2 * rows)
 
     def finish(tile, carry):
@@ -500,9 +504,60 @@
     grad_first[...] = flat[at + FIELDS : at + 2 * FIELDS][: grad_first.shape[0]]
 
 
+def fill_shifts(shifts):
+    shape = (PIECES * LANES, LANES)
+    source = lax.broadcasted_iota(jnp.int32, shape, 0) % LANES
+    target = lax.broadcasted_iota(jnp.int32, shape, 1)
+    for n, step in enumerate((1, LANES - 1)):
+        hit = (source + step) % LANES == target
+        shifts[:, n * LANES : (n + 1) * LANES] = jnp.where(hit, 1.0, 0.0).astype(jnp.bfloat16)
+
+
+def pieces(x):
+    parts = []
+    for n in range(PIECES):
+        part = x.astype(jnp.bfloat16)
+        parts.append(part)
+        if n + 1 < PIECES:
+            x = x - part.astype(jnp.float32)
+    return jnp.concatenate(parts, axis=1)
+
+
+def groups_of(array):
+    tiles = array.shape[2] // LANES
+    return [range(t, min(t + GROUP, tiles)) for t in range(0, tiles, GROUP)]
+
+
+def stacked(source, group):
+    return pieces(
+        jnp.concatenate([source[c, :, lanes_of(t)] for t in group for c in range(3)], axis=0)
+    )
+
+
+def shift_both(source, before, after, shifts):
+    tall = source.shape[1]
+    for group in groups_of(source):
+        moved = contract(stacked(source, group), shifts[...], 1, 0)
+        for n, tile in enumerate(group):
+            for c in range(3):
+                at = (3 * n + c) * tall
+                before[c, :, lanes_of(tile)] = moved[at : at + tall, :LANES]
+                after[c, :, lanes_of(tile)] = moved[at : at + tall, LANES:]
+
+
+def shift_in_place(array, side, shifts):
+    tall = array.shape[1]
+    for group in groups_of(array):
+        moved = contract(stacked(array, group), shifts[:, side * LANES : (side + 1) * LANES], 1, 0)
+        for n, tile in enumerate(group):
+            for c in range(3):
+                at = (3 * n + c) * tall
+                array[c, :, lanes_of(tile)] = moved[at : at + tall]
+
+
 def krylov_kernel(
     numbers, r_mid, r_up, r_down, stiff, support, kept, bends, sums,
-    basis, before, after, ahead, behind, middle,
+    basis, before, after, ahead, behind, middle, shifts,
 ):
     rows = r_mid.shape[1]
     wide = r_mid.shape[2]
@@ -515,8 +570,6 @@
     def place(k, c, at, value):
         basis[k, c, :, at] = value
         kept[k, c, :, at] = value[rows : 2 * rows]
-        before[c, :, at] = pltpu.roll(value, 1, 1)
-        after[c, :, at] = pltpu.roll(value, LANES - 1, 1)
 
     def set_up(tile, carry):
         at = lanes_of(tile)
@@ -525,7 +578,9 @@
             place(0, c, at, value)
         return carry
 
+    fill_shifts(shifts)
     lax.fori_loop(0, tiles, set_up, 0)
+    shift_both(basis.at[0], before, after, shifts)
 
     def strain_of(k, tile):
         e = spread_strains(*triples_of(basis.at[k], before, after, tile, tiles, first, final))
@@ -548,12 +603,14 @@
             for c, (alpha, beta, gamma) in enumerate(
                 spread_forces(stress_of(strain_of(k, tile), at))
             ):
-                ahead[c, :, at] = pltpu.roll(alpha, 1, 1)
-                behind[c, :, at] = pltpu.roll(beta, LANES - 1, 1)
+                ahead[c, :, at] = alpha
+                behind[c, :, at] = beta
                 middle[c, :, at] = gamma
             return carry
 
         lax.fori_loop(0, tiles, push, 0)
+        shift_in_place(ahead, 0, shifts)
+        shift_in_place(behind, 1, shifts)
 
         centre, inverse = numbers[k], numbers[6 + k]
         former = numbers[2 + k]
@@ -610,6 +667,7 @@
             names += [10, 11, 12]
         found = lax.fori_loop(0, own_tiles, advance, (zero,) * len(names))
         advance(own_tiles, None)
+        shift_both(basis.at[k + 1], before, after, shifts)
         for name, value in zip(names, found):
             totals[name] = value
 
@@ -719,7 +777,8 @@
          ((layers + 1, 2 * cols, hid), bf16), ((PADDED, 2 * cols), bf16)],
         [((3, tall, wide), f32)] * 6
         + [((tiles, FIELDS * tall, LANES), f32)] * 2
-        + [((len(UPPER), tall, wide), f32), ((layers + 1, 2 * cols, hid), bf16), 2],
+        + [((len(UPPER), tall, wide), f32), ((PIECES * LANES, 2 * LANES), bf16),
+           ((layers + 1, 2 * cols, hid), bf16), 2],
         table, fields, up, down, learned, ends, w_mid, far_outs=(2,),
     )
     stiff, support = kernel_call(
@@ -732,7 +791,8 @@
         krylov_kernel, "krylov", 1,
         [((DEGREE + 1, 3, rows, wide), f32), ((DEGREE + 1, tiles, 6 * rows, LANES), f32),
          ((devices, 1, LANES), f32)],
-        [((DEGREE + 1, 3, tall, wide), f32)] + [((3, tall, wide), f32)] * 5,
+        [((DEGREE + 1, 3, tall, wide), f32)] + [((3, tall, wide), f32)] * 5
+        + [((PIECES * LANES, 2 * LANES), bf16)],
         numbers, wide_residual, up, down, stiff, support,
     )
     sums = everyone(sums)

time: 112 us -> 107 us (0.955)
  Pallas kernels: 51.5 us -> 46.9 us
    pallas_call x7, Pallas kernels: 51.5 us -> 46.9 us  [kernel_call(): pl.pallas_call(body, in_specs=specs, out_specs=[IN_PLACE if n in far_outs...]
where the time goes in v5:
time: 107 us
  Pallas kernels  46.9 us (44%)
  blocking collectives  32.4 us (30%)
  starting transfers between devices  14.5 us (14%)
  waiting for transfers between devices  5.2 us (5%)
  other arithmetic  5.03 us (5%)
  between operations  2.19 us (2%)
    pallas_call x7, Pallas kernels, kernel_call(): pl.pallas_call(body, in_specs=specs, out_specs=[IN_PLACE if n in far_outs...  46.9 us
    all_to_all x3, blocking collectives, everyone(): return lax.all_to_all(rows, AXES, 0, 0, tiled=True)  32.4 us
    ppermute x3, starting transfers between devices, from_both(): after = lax.ppermute(head, axis, ring(axis, -1))  8.81 us
    ppermute x3, waiting for transfers between devices, from_both(): before = lax.ppermute(tail, axis, ring(axis, 1))  4.9 us
    ppermute x1, starting transfers between devices, per_device(): down = lax.ppermute(sends[1], 'patch', ring('patch', -1))  3.11 us
  transfers between devices with their start and end apart: 8, of which 3 were waited for; matrix products, arithmetic and copies ran while one was open for 3% of the time, Pallas kernels for 20%

profile of v5, /device:TPU:0, one launch (start us, length us, event | category | flops | bytes accessed | tf_op | source)
XLA Modules:
  0.0 106.7 jit_solution(9542346934081521203)
XLA Ops:
  0.6 0.0 copy-start
  0.6 0.9 convert_bitcast_fusion
  1.5 1.2 %pad_maximum_fusion = f32[10,8,2048]{2,1,0:T(8,128)S(1)} fusion(f32[3,8,2048]{2,1,0:T(8,128)} %param.10, f32[1,8,2048]{2,1,0:T(8,128)S(1)} %convert_bitcast_fusion, f32[3,8,2048]{2,1,0:T(8,128)} %param.11, f32[3,8,2048]{2,1,0:T(8,128)} %param.9), kind=kLoop, calls=%fused_computation | loop fusion | flops 491520 | bytes 1310720 | tf_op jit(solution)/shard_map/concatenate | solution.py:745
  2.7 0.1 fusion.1
  2.8 0.5 collective-permute-start.1
  3.3 2.0 %collective-permute-start = (f32[10,8,16]{2,1,0:T(8,128)S(1)}, f32[10,8,16]{2,1,0:T(8,128)S(1)}, u32[]{:S(2)}, u32[]{:S(2)}) collective-permute-start(f32[10,8,16]{2,1,0:T(8,128)S(1)} %get-tuple-element.52), channel_id=1, source_target_pairs={{0,3},{1,0},{2,1},{3,2},{4,7},{5,4},{6,5},{7,6},{8,11},{9,8},{10,9... | collective-permute-start | bytes 15368 | tf_op jit(solution)/shard_map/ppermute | solution.py:24
  5.3 0.8 multiply_multiply_fusion
  6.1 0.7 pad_maximum_fusion.3.ends
  6.8 0.1 reshape.17.table
  6.9 0.0 collective-permute-done.1
  6.9 0.2 collective-permute-done
  7.2 0.1 concatenate.16.fields
  7.4 2.1 %collective-permute-start.2 = (f32[7,2176]{1,0:T(8,128)S(1)}, f32[7,2176]{1,0:T(8,128)S(1)}, u32[]{:S(2)}, u32[]{:S(2)}) collective-permute-start(f32[7,2176]{1,0:T(8,128)S(1)} %pad_maximum_fusion.1), channel_id=1, source_target_pairs={{0,4},{4,8},{8,12},{12,16},{16,20},{20,24},{24,28},{28,0},{1,5},{5... | collective-permute-start | bytes 182792 | tf_op jit(solution)/shard_map/ppermute | solution.py:753
  9.5 3.1 %collective-permute-start.3 = (f32[7,2176]{1,0:T(8,128)S(1)}, f32[7,2176]{1,0:T(8,128)S(1)}, u32[]{:S(2)}, u32[]{:S(2)}) collective-permute-start(f32[7,2176]{1,0:T(8,128)S(1)} %pad_maximum_fusion.2), channel_id=1, source_target_pairs={{0,28},{4,0},{8,4},{12,8},{16,12},{20,16},{24,20},{28,24},{1,29},{... | collective-permute-start | bytes 182792 | tf_op jit(solution)/shard_map/ppermute | solution.py:754
  12.6 2.1 %collective-permute-start.7 = (f32[4,6,2176]{2,1,0:T(8,128)S(1)}, f32[4,6,2176]{2,1,0:T(8,128)S(1)}, u32[]{:S(2)}, u32[]{:S(2)}) collective-permute-start(f32[4,6,2176]{2,1,0:T(8,128)S(1)} %get-tuple-element.41), channel_id=1, source_target_pairs={{0,28},{4,0},{8,4},{12,8},{16,12},{20,16},{24,20},{28,24},{1,29},{... | collective-permute-start | bytes 626696 | tf_op jit(solution)/shard_map/ppermute | solution.py:24
  14.7 0.0 collective-permute-start.6
  14.7 0.0 copy-done
  14.7 8.8 %shard_map.128 = (f32[17,64,128]{2,1,0:T(8,128)S(1)}, bf16[4,12288,128]{2,1,0:T(8,128)(2,1)}, bf16[16,12288]{1,0:T(8,128)(2,1)S(1)}) custom-call(f32[10,8,2176]{2,1,0:T(8,128)S(1)} %concatenate.16.fields, bf16[32,128]{1,0:T(8,128)(2,1)S(1)} %pad_maximum_fusion.3.ends, bf16[3,128,128]{2,1,0:T(8,128)(2,1)S(1)} %copy-done), custom_call_target="tpu_custom_call" | custom-call | tf_op jit(solution)/shard_map/pallas_call | solution.py:713
  23.5 0.0 collective-permute-done.2.up
  23.5 0.0 collective-permute-done.3.down
  23.6 10.0 %shard_map.129 = (f32[3,8,2176]{2,1,0:T(8,128)S(1)}, f32[3,8,2048]{2,1,0:T(8,128)}, bf16[4,4096,128]{2,1,0:T(8,128)(2,1)}, bf16[16,4096]{1,0:T(8,128)(2,1)S(1)}) custom-call(f32[288]{0:T(512)S(1)} %reshape.17.table, f32[10,8,2176]{2,1,0:T(8,128)S(1)} %concatenate.16.fields, f32[7,2176]{1,0:T(8,128)S(1)} %collective-permute-done.2.up, ...), custom_call_target="tpu_custom_call" | custom-call | tf_op jit(solution)/shard_map/pallas_call | solution.py:713
  33.5 4.8 %collective-permute-start.5 = (f32[3,8,2176]{2,1,0:T(8,128)S(1)}, f32[3,8,2176]{2,1,0:T(8,128)S(1)}, u32[]{:S(2)}, u32[]{:S(2)}) collective-permute-start(f32[3,8,2176]{2,1,0:T(8,128)S(1)} %get-tuple-element.24.r_mid), channel_id=1, source_target_pairs={{0,28},{4,0},{8,4},{12,8},{16,12},{20,16},{24,20},{28,24},{1,29},{... | collective-permute-start | bytes 626696 | tf_op jit(solution)/shard_map/ppermute | solution.py:24
  38.3 0.0 collective-permute-start.4
  38.3 1.4 %slice_reduce_fusion = (f32[]{:T(128)}, f32[]{:T(128)}) fusion(f32[8,6,6]{2,0,1:T(8,128)} %param.13), kind=kLoop, calls=%fused_computation.14 | loop fusion | flops 14 | bytes 72 | tf_op jit(solution)/shard_map/reduce_sum | solution.py:696
  41.1 0.1 stack.39.numbers
  41.2 0.0 collective-permute-done.7.fl_down
  41.2 0.0 collective-permute-done.6.fl_up
  41.2 2.1 %shard_map.130 = (f32[21,24,2176]{2,1,0:T(8,128)S(1)}, f32[3,24,2176]{2,1,0:T(8,128)S(1)}) custom-call(f32[288]{0:T(512)S(1)} %reshape.17.table, f32[10,8,2176]{2,1,0:T(8,128)S(1)} %concatenate.16.fields, f32[4,6,2176]{2,1,0:T(8,128)S(1)} %collective-permute-done.6.fl_up, f32[4,6,2176]{2,1,0:T(8,128)S(1)} %collective-permute-done.7.fl_down), custom_call_target="tpu_custom_call" | custom-call | tf_op jit(solution)/shard_map/pallas_call | solution.py:713
  43.3 0.1 collective-permute-done.5.r_down
  43.4 4.9 %collective-permute-done.4.r_up = f32[3,8,2176]{2,1,0:T(8,128)S(1)} collective-permute-done((f32[3,8,2176]{2,1,0:T(8,128)S(1)}, f32[3,8,2176]{2,1,0:T(8,128)S(1)}, u32[]{:S(2)}, u32[]{:S(2)}) %collective-permute-start.4) | collective-permute-done | bytes 208928 | tf_op jit(solution)/shard_map/ppermute | solution.py:23
  48.3 11.5 %shard_map.131 = (f32[4,3,8,2176]{3,2,1,0:T(8,128)S(1)}, f32[4,17,48,128]{3,2,1,0:T(8,128)S(1)}, f32[32,1,128]{2,1,0:T(1,128)S(1)}) custom-call(f32[9]{0:T(128)S(1)} %stack.39.numbers, f32[3,8,2176]{2,1,0:T(8,128)S(1)} %get-tuple-element.24.r_mid, f32[3,8,2176]{2,1,0:T(8,128)S(1)} %collective-permute-done.4.r_up, ...), custom_call_target="tpu_custom_call" | custom-call | tf_op jit(solution)/shard_map/pallas_call | solution.py:713
  59.8 9.7 %all_to_all.15.sums = f32[32,1,128]{2,1,0:T(1,128)S(1)} all-to-all(f32[32,1,128]{2,1,0:T(1,128)S(1)} %get-tuple-element.27), channel_id=1, replica_groups=mesh['patch'=8,'sub'=4] {'patch','sub'}, dimensions={0} | all-to-all | bytes 32768 | tf_op jit(solution)/shard_map/all_to_all | solution.py:29
  69.4 13.6 %shard_map.132 = (f32[3,8,2048]{2,1,0:T(8,128)}, f32[32,13,1,128]{3,2,1,0:T(1,128)S(1)}) custom-call(f32[9]{0:T(128)S(1)} %stack.39.numbers, f32[32,1,128]{2,1,0:T(1,128)S(1)} %all_to_all.15.sums, f32[4,3,8,2176]{3,2,1,0:T(8,128)S(1)} %get-tuple-element.28.kept, f32[4,17,48,128]{3,2,1,0:T(8,128)S(1)} %get-tuple-element.29.bends, ...), custom_call_target="tpu_custom_call" | custom-call | tf_op jit(solution)/shard_map/pallas_call | solution.py:713
  83.1 11.1 %all_to_all.16.parts = f32[32,13,1,128]{3,2,1,0:T(1,128)S(1)} all-to-all(f32[32,13,1,128]{3,2,1,0:T(1,128)S(1)} %get-tuple-element.35), channel_id=1, replica_groups=mesh['patch'=8,'sub'=4] {'patch','sub'}, dimensions={0} | all-to-all | bytes 425984 | tf_op jit(solution)/shard_map/all_to_all | solution.py:29
  94.2 0.2 shard_map.133
  94.4 11.6 %all_to_all.17.parts = f32[32,13,1,128]{3,2,1,0:T(1,128)S(1)} all-to-all(f32[32,13,1,128]{3,2,1,0:T(1,128)S(1)} %shard_map.133), channel_id=1, replica_groups=mesh['patch'=8,'sub'=4] {'patch','sub'}, dimensions={0} | all-to-all | bytes 425984 | tf_op jit(solution)/shard_map/all_to_all | solution.py:29
  106.0 0.7 shard_map.134
  (8 shorter events, 0.2 us)
Async XLA Ops:
  0.6 14.1 %copy-start = (bf16[3,128,128]{2,1,0:T(8,128)(2,1)S(1)}, bf16[3,128,128]{2,1,0:T(8,128)(2,1)}, u32[]{:S(2)}) copy-start(bf16[3,128,128]{2,1,0:T(8,128)(2,1)} %w_mid.5) | copy-start | bytes 294916
  2.8 4.2 %collective-permute-start.1 = (f32[10,8,16]{2,1,0:T(8,128)S(1)}, f32[10,8,16]{2,1,0:T(8,128)S(1)}, u32[]{:S(2)}, u32[]{:S(2)}) collective-permute-start(f32[10,8,16]{2,1,0:T(8,128)S(1)} %get-tuple-element.51), channel_id=1, source_target_pairs={{0,1},{1,2},{2,3},{3,0},{4,5},{5,6},{6,7},{7,4},{8,9},{9,10},{10,1... | collective-permute-start | bytes 15368 | tf_op jit(solution)/shard_map/ppermute | solution.py:23
  3.3 3.9 %collective-permute-start = (f32[10,8,16]{2,1,0:T(8,128)S(1)}, f32[10,8,16]{2,1,0:T(8,128)S(1)}, u32[]{:S(2)}, u32[]{:S(2)}) collective-permute-start(f32[10,8,16]{2,1,0:T(8,128)S(1)} %get-tuple-element.52), channel_id=1, source_target_pairs={{0,3},{1,0},{2,1},{3,2},{4,7},{5,4},{6,5},{7,6},{8,11},{9,8},{10,9... | collective-permute-start | bytes 15368 | tf_op jit(solution)/shard_map/ppermute | solution.py:24
  7.4 16.2 %collective-permute-start.2 = (f32[7,2176]{1,0:T(8,128)S(1)}, f32[7,2176]{1,0:T(8,128)S(1)}, u32[]{:S(2)}, u32[]{:S(2)}) collective-permute-start(f32[7,2176]{1,0:T(8,128)S(1)} %pad_maximum_fusion.1), channel_id=1, source_target_pairs={{0,4},{4,8},{8,12},{12,16},{16,20},{20,24},{24,28},{28,0},{1,5},{5... | collective-permute-start | bytes 182792 | tf_op jit(solution)/shard_map/ppermute | solution.py:753
  9.5 14.1 %collective-permute-start.3 = (f32[7,2176]{1,0:T(8,128)S(1)}, f32[7,2176]{1,0:T(8,128)S(1)}, u32[]{:S(2)}, u32[]{:S(2)}) collective-permute-start(f32[7,2176]{1,0:T(8,128)S(1)} %pad_maximum_fusion.2), channel_id=1, source_target_pairs={{0,28},{4,0},{8,4},{12,8},{16,12},{20,16},{24,20},{28,24},{1,29},{... | collective-permute-start | bytes 182792 | tf_op jit(solution)/shard_map/ppermute | solution.py:754
  12.6 28.5 %collective-permute-start.7 = (f32[4,6,2176]{2,1,0:T(8,128)S(1)}, f32[4,6,2176]{2,1,0:T(8,128)S(1)}, u32[]{:S(2)}, u32[]{:S(2)}) collective-permute-start(f32[4,6,2176]{2,1,0:T(8,128)S(1)} %get-tuple-element.41), channel_id=1, source_target_pairs={{0,28},{4,0},{8,4},{12,8},{16,12},{20,16},{24,20},{28,24},{1,29},{... | collective-permute-start | bytes 626696 | tf_op jit(solution)/shard_map/ppermute | solution.py:24
  14.7 26.5 %collective-permute-start.6 = (f32[4,6,2176]{2,1,0:T(8,128)S(1)}, f32[4,6,2176]{2,1,0:T(8,128)S(1)}, u32[]{:S(2)}, u32[]{:S(2)}) collective-permute-start(f32[4,6,2176]{2,1,0:T(8,128)S(1)} %get-tuple-element.42), channel_id=1, source_target_pairs={{0,4},{4,8},{8,12},{12,16},{16,20},{20,24},{24,28},{28,0},{1,5},{5... | collective-permute-start | bytes 626696 | tf_op jit(solution)/shard_map/ppermute | solution.py:23
  33.5 9.8 %collective-permute-start.5 = (f32[3,8,2176]{2,1,0:T(8,128)S(1)}, f32[3,8,2176]{2,1,0:T(8,128)S(1)}, u32[]{:S(2)}, u32[]{:S(2)}) collective-permute-start(f32[3,8,2176]{2,1,0:T(8,128)S(1)} %get-tuple-element.24.r_mid), channel_id=1, source_target_pairs={{0,28},{4,0},{8,4},{12,8},{16,12},{20,16},{24,20},{28,24},{1,29},{... | collective-permute-start | bytes 626696 | tf_op jit(solution)/shard_map/ppermute | solution.py:24
  38.3 10.0 %collective-permute-start.4 = (f32[3,8,2176]{2,1,0:T(8,128)S(1)}, f32[3,8,2176]{2,1,0:T(8,128)S(1)}, u32[]{:S(2)}, u32[]{:S(2)}) collective-permute-start(f32[3,8,2176]{2,1,0:T(8,128)S(1)} %get-tuple-element.24.r_mid), channel_id=1, source_target_pairs={{0,4},{4,8},{8,12},{12,16},{16,20},{20,24},{24,28},{28,0},{1,5},{5... | collective-permute-start | bytes 626696 | tf_op jit(solution)/shard_map/ppermute | solution.py:23

commit v6 on v5

--- a/solution.py
+++ b/solution.py
@@ -131,6 +131,7 @@
 PADDED = 16
 PIECES = 3
 GROUP = 9
+PARTS = 3
 
 
 def triples_of(centre, before, after, tile, tiles, first, final):
@@ -191,31 +192,36 @@
     )
 
 
-def learn_line(row, line, strain, learned, spread, cols, weights, hidden, inputs):
-    for at, size in pieces_of(cols):
-        x = widened(gathered(strain, row, spread, at, size))
-        keep = None
-        if line is not None:
-            where = line * cols + at
-            if not isinstance(where, int):
-                where = pl.multiple_of(where, LANES)
-            inputs[:, pl.ds(where, size)] = x
-
-            def keep(k, h, where=where, size=size):
-                hidden[k, pl.ds(where, size), :] = h
-
-        out = learn(x, *weights, keep)
-        for n in range(size // LANES):
-            piece = out[:, n * LANES : (n + 1) * LANES]
-            learned[at // LANES + n, pl.ds(row, FIELDS, stride=spread), :] = piece
-
-
-def learn_rims(rows, strain, learned, spread, cols, weights):
+def layer_copy(k, base, span, source, target, flag):
+    here = pl.ds(base, span)
+    return pltpu.make_async_copy(source.at[k, here, :], target.at[k, here, :], flag)
+
+
+def learn_lines(
+    rows, rims, kept, base, strain, learned, spread, cols, weights, hidden, stored, inputs, flags
+):
     rim = cols // LANES
-    x = [strain[rim, pl.ds(row, FIELDS, stride=spread), :] for row in rows]
-    out = learn(widened(jnp.concatenate(x, axis=1)), *weights)
+    parts = [gathered(strain, row, spread, 0, cols) for row in rows]
+    parts += [strain[rim, pl.ds(row, FIELDS, stride=spread), :] for row in rims]
+    x = widened(jnp.concatenate(parts, axis=1))
+    start, span = base * cols, kept * cols
+    inputs[:, pl.ds(start, span)] = x[:, :span]
+    copies = []
+
+    def keep(k, h):
+        hidden[k, pl.ds(start, span), :] = h[:span]
+        copies.append(layer_copy(k, start, span, hidden, stored, flags[k]))
+        copies[-1].start()
+
+    out = learn(x, *weights, keep)
     for n, row in enumerate(rows):
-        learned[rim, pl.ds(row, FIELDS, stride=spread), :] = out[:, n * LANES : (n + 1) * LANES]
+        for t in range(rim):
+            at = n * cols + t * LANES
+            learned[t, pl.ds(row, FIELDS, stride=spread), :] = out[:, at : at + LANES]
+    for n, row in enumerate(rims):
+        at = len(rows) * cols + n * LANES
+        learned[rim, pl.ds(row, FIELDS, stride=spread), :] = out[:, at : at + LANES]
+    return copies
 
 
 def line_copy(line, cols, source, target, flags):
@@ -255,16 +261,19 @@
 
     lax.fori_loop(0, tiles, strains, 0)
     weights = (ends.at[0:PADDED], w_mid, ends.at[PADDED : 2 * PADDED])
-
-    def line(row, carry):
-        learn_line(row, row - 1, strain, learned, rows, cols, weights, hidden, inputs)
-        line_copy(row - 1, cols, hidden, stored, flags).start()
-        return carry
-
-    lax.fori_loop(1, rows - 1, line, 0)
-    learn_rims(range(1, rows - 1), strain, learned, rows, cols, weights)
-    for n in range(rows - 2):
-        line_copy(n, cols, hidden, stored, flags).wait()
+    inside = list(range(1, rows - 1))
+    share = -(-len(inside) // PARTS)
+    levels = w_mid.shape[0] + 1
+    copies = []
+    for n in range(PARTS):
+        mine = inside[n * share : (n + 1) * share]
+        copies += learn_lines(
+            mine, inside if n == PARTS - 1 else [], len(mine), n * share,
+            strain, learned, rows, cols, weights, hidden, stored, inputs,
+            [flags.at[n * levels + k] for k in range(levels)],
+        )
+    for copy in copies:
+        copy.wait()
 
 
 def stiffness_of(table, ids, depth, target, at):
@@ -349,12 +358,11 @@
 
     lax.fori_loop(0, tiles, strains, 0)
     weights = (ends.at[0:PADDED], w_mid, ends.at[PADDED : 2 * PADDED])
-    rim_rows = (rows - 1, rows, 2 * rows - 1, 2 * rows)
-    for row, line in zip(rim_rows, (None, 0, 1, None)):
-        learn_line(row, line, strain, learned, tall, cols, weights, hidden, inputs)
-        if line is not None:
-            line_copy(line, cols, hidden, stored, flags).start()
-    learn_rims(rim_rows, strain, learned, tall, cols, weights)
+    lines = (rows, 2 * rows - 1, rows - 1, 2 * rows)
+    copies = learn_lines(
+        lines, lines, 2, 0, strain, learned, tall, cols, weights, hidden, stored, inputs,
+        [flags.at[k] for k in range(w_mid.shape[0] + 1)],
+    )
 
     def push(tile, carry):
         at = lanes_of(tile)
@@ -390,8 +398,8 @@
 
     lax.fori_loop(0, tiles - 1, finish, 0)
     finish(tiles - 1, None)
-    for n in range(2):
-        line_copy(n, cols, hidden, stored, flags).wait()
+    for copy in copies:
+        copy.wait()
 
 
 def solve(numbers, sums, kept, bends, adjoint, upstream):
@@ -730,7 +738,7 @@
 
 
 LIMITS = {
-    "inner": 24, "outer": 24, "prepare": 8, "krylov": 10, "backward": 32, "gather": 4, "deliver": 4,
+    "inner": 40, "outer": 40, "prepare": 8, "krylov": 10, "backward": 32, "gather": 4, "deliver": 4,
 }
 
 
@@ -768,7 +776,7 @@
          ((PADDED, (rows - 2) * cols), bf16)],
         [((3, rows, wide), f32)] * 2
         + [((tiles, FIELDS * rows, LANES), f32), ((layers + 1, (rows - 2) * cols, hid), bf16),
-           rows - 2],
+           PARTS * (layers + 1)],
         fields, ends, w_mid, far_outs=(1,),
     )
     wide_residual, residual, outer_hidden, outer_inputs = kernel_call(
@@ -778,7 +786,7 @@
         [((3, tall, wide), f32)] * 6
         + [((tiles, FIELDS * tall, LANES), f32)] * 2
         + [((len(UPPER), tall, wide), f32), ((PIECES * LANES, 2 * LANES), bf16),
-           ((layers + 1, 2 * cols, hid), bf16), 2],
+           ((layers + 1, 2 * cols, hid), bf16), layers + 1],
         table, fields, up, down, learned, ends, w_mid, far_outs=(2,),
     )
     stiff, support = kernel_call(

time: 107 us -> 105 us (0.981)
  Pallas kernels: 46.9 us -> 45.1 us
    pallas_call x7, Pallas kernels: 46.9 us -> 45.1 us  [kernel_call(): pl.pallas_call(body, in_specs=specs, out_specs=[IN_PLACE if n in far_outs...]
  transfers between devices with their start and end apart: 8 -> 8, of which waited for: 3 -> 3; matrix products, arithmetic and copies ran while one was open for 3% -> 3% of each run, Pallas kernels for 20% -> 18%
where the time goes in v6:
time: 105 us
  Pallas kernels  45.1 us (43%)
  blocking collectives  32.4 us (31%)
  starting transfers between devices  14.5 us (14%)
  waiting for transfers between devices  5.2 us (5%)
  other arithmetic  5.03 us (5%)
  between operations  2.19 us (2%)
    pallas_call x7, Pallas kernels, kernel_call(): pl.pallas_call(body, in_specs=specs, out_specs=[IN_PLACE if n in far_outs...  45.1 us
    all_to_all x3, blocking collectives, everyone(): return lax.all_to_all(rows, AXES, 0, 0, tiled=True)  32.4 us
    ppermute x3, starting transfers between devices, from_both(): after = lax.ppermute(head, axis, ring(axis, -1))  8.82 us
    ppermute x3, waiting for transfers between devices, from_both(): before = lax.ppermute(tail, axis, ring(axis, 1))  4.9 us
    ppermute x1, starting transfers between devices, per_device(): down = lax.ppermute(sends[1], 'patch', ring('patch', -1))  3.11 us
  transfers between devices with their start and end apart: 8, of which 3 were waited for; matrix products, arithmetic and copies ran while one was open for 3% of the time, Pallas kernels for 18%

profile of v6, /device:TPU:0, one launch (start us, length us, event | category | flops | bytes accessed | tf_op | source)
XLA Modules:
  0.0 105.0 jit_solution(1754908078607597719)
XLA Ops:
  0.6 0.0 copy-start
  0.6 0.9 convert_bitcast_fusion
  1.5 1.2 %pad_maximum_fusion = f32[10,8,2048]{2,1,0:T(8,128)S(1)} fusion(f32[3,8,2048]{2,1,0:T(8,128)} %param.10, f32[1,8,2048]{2,1,0:T(8,128)S(1)} %convert_bitcast_fusion, f32[3,8,2048]{2,1,0:T(8,128)} %param.11, f32[3,8,2048]{2,1,0:T(8,128)} %param.9), kind=kLoop, calls=%fused_computation | loop fusion | flops 491520 | bytes 1310720 | tf_op jit(solution)/shard_map/concatenate | solution.py:753
  2.7 0.1 fusion.1
  2.8 0.5 collective-permute-start.1
  3.3 2.0 %collective-permute-start = (f32[10,8,16]{2,1,0:T(8,128)S(1)}, f32[10,8,16]{2,1,0:T(8,128)S(1)}, u32[]{:S(2)}, u32[]{:S(2)}) collective-permute-start(f32[10,8,16]{2,1,0:T(8,128)S(1)} %get-tuple-element.52), channel_id=1, source_target_pairs={{0,3},{1,0},{2,1},{3,2},{4,7},{5,4},{6,5},{7,6},{8,11},{9,8},{10,9... | collective-permute-start | bytes 15368 | tf_op jit(solution)/shard_map/ppermute | solution.py:24
  5.3 0.8 multiply_multiply_fusion
  6.1 0.7 pad_maximum_fusion.3.ends
  6.8 0.1 reshape.17.table
  6.9 0.0 collective-permute-done.1
  6.9 0.2 collective-permute-done
  7.2 0.1 concatenate.16.fields
  7.4 2.1 %collective-permute-start.2 = (f32[7,2176]{1,0:T(8,128)S(1)}, f32[7,2176]{1,0:T(8,128)S(1)}, u32[]{:S(2)}, u32[]{:S(2)}) collective-permute-start(f32[7,2176]{1,0:T(8,128)S(1)} %pad_maximum_fusion.1), channel_id=1, source_target_pairs={{0,4},{4,8},{8,12},{12,16},{16,20},{20,24},{24,28},{28,0},{1,5},{5... | collective-permute-start | bytes 182792 | tf_op jit(solution)/shard_map/ppermute | solution.py:761
  9.5 3.1 %collective-permute-start.3 = (f32[7,2176]{1,0:T(8,128)S(1)}, f32[7,2176]{1,0:T(8,128)S(1)}, u32[]{:S(2)}, u32[]{:S(2)}) collective-permute-start(f32[7,2176]{1,0:T(8,128)S(1)} %pad_maximum_fusion.2), channel_id=1, source_target_pairs={{0,28},{4,0},{8,4},{12,8},{16,12},{20,16},{24,20},{28,24},{1,29},{... | collective-permute-start | bytes 182792 | tf_op jit(solution)/shard_map/ppermute | solution.py:762
  12.6 2.1 %collective-permute-start.7 = (f32[4,6,2176]{2,1,0:T(8,128)S(1)}, f32[4,6,2176]{2,1,0:T(8,128)S(1)}, u32[]{:S(2)}, u32[]{:S(2)}) collective-permute-start(f32[4,6,2176]{2,1,0:T(8,128)S(1)} %get-tuple-element.41), channel_id=1, source_target_pairs={{0,28},{4,0},{8,4},{12,8},{16,12},{20,16},{24,20},{28,24},{1,29},{... | collective-permute-start | bytes 626696 | tf_op jit(solution)/shard_map/ppermute | solution.py:24
  14.7 0.0 collective-permute-start.6
  14.7 0.0 copy-done
  14.7 7.6 %shard_map.128 = (f32[17,64,128]{2,1,0:T(8,128)S(1)}, bf16[4,12288,128]{2,1,0:T(8,128)(2,1)}, bf16[16,12288]{1,0:T(8,128)(2,1)S(1)}) custom-call(f32[10,8,2176]{2,1,0:T(8,128)S(1)} %concatenate.16.fields, bf16[32,128]{1,0:T(8,128)(2,1)S(1)} %pad_maximum_fusion.3.ends, bf16[3,128,128]{2,1,0:T(8,128)(2,1)S(1)} %copy-done), custom_call_target="tpu_custom_call" | custom-call | tf_op jit(solution)/shard_map/pallas_call | solution.py:721
  22.3 0.0 collective-permute-done.2.up
  22.3 0.0 collective-permute-done.3.down
  22.3 9.4 %shard_map.129 = (f32[3,8,2176]{2,1,0:T(8,128)S(1)}, f32[3,8,2048]{2,1,0:T(8,128)}, bf16[4,4096,128]{2,1,0:T(8,128)(2,1)}, bf16[16,4096]{1,0:T(8,128)(2,1)S(1)}) custom-call(f32[288]{0:T(512)S(1)} %reshape.17.table, f32[10,8,2176]{2,1,0:T(8,128)S(1)} %concatenate.16.fields, f32[7,2176]{1,0:T(8,128)S(1)} %collective-permute-done.2.up, ...), custom_call_target="tpu_custom_call" | custom-call | tf_op jit(solution)/shard_map/pallas_call | solution.py:721
  31.8 4.8 %collective-permute-start.5 = (f32[3,8,2176]{2,1,0:T(8,128)S(1)}, f32[3,8,2176]{2,1,0:T(8,128)S(1)}, u32[]{:S(2)}, u32[]{:S(2)}) collective-permute-start(f32[3,8,2176]{2,1,0:T(8,128)S(1)} %get-tuple-element.24.r_mid), channel_id=1, source_target_pairs={{0,28},{4,0},{8,4},{12,8},{16,12},{20,16},{24,20},{28,24},{1,29},{... | collective-permute-start | bytes 626696 | tf_op jit(solution)/shard_map/ppermute | solution.py:24
  36.5 0.0 collective-permute-start.4
  36.5 1.4 %slice_reduce_fusion = (f32[]{:T(128)}, f32[]{:T(128)}) fusion(f32[8,6,6]{2,0,1:T(8,128)} %param.13), kind=kLoop, calls=%fused_computation.14 | loop fusion | flops 14 | bytes 72 | tf_op jit(solution)/shard_map/reduce_sum | solution.py:704
  39.3 0.1 stack.39.numbers
  39.4 0.0 collective-permute-done.7.fl_down
  39.4 0.0 collective-permute-done.6.fl_up
  39.4 2.1 %shard_map.130 = (f32[21,24,2176]{2,1,0:T(8,128)S(1)}, f32[3,24,2176]{2,1,0:T(8,128)S(1)}) custom-call(f32[288]{0:T(512)S(1)} %reshape.17.table, f32[10,8,2176]{2,1,0:T(8,128)S(1)} %concatenate.16.fields, f32[4,6,2176]{2,1,0:T(8,128)S(1)} %collective-permute-done.6.fl_up, f32[4,6,2176]{2,1,0:T(8,128)S(1)} %collective-permute-done.7.fl_down), custom_call_target="tpu_custom_call" | custom-call | tf_op jit(solution)/shard_map/pallas_call | solution.py:721
  41.5 0.1 collective-permute-done.5.r_down
  41.6 4.9 %collective-permute-done.4.r_up = f32[3,8,2176]{2,1,0:T(8,128)S(1)} collective-permute-done((f32[3,8,2176]{2,1,0:T(8,128)S(1)}, f32[3,8,2176]{2,1,0:T(8,128)S(1)}, u32[]{:S(2)}, u32[]{:S(2)}) %collective-permute-start.4) | collective-permute-done | bytes 208928 | tf_op jit(solution)/shard_map/ppermute | solution.py:23
  46.5 11.5 %shard_map.131 = (f32[4,3,8,2176]{3,2,1,0:T(8,128)S(1)}, f32[4,17,48,128]{3,2,1,0:T(8,128)S(1)}, f32[32,1,128]{2,1,0:T(1,128)S(1)}) custom-call(f32[9]{0:T(128)S(1)} %stack.39.numbers, f32[3,8,2176]{2,1,0:T(8,128)S(1)} %get-tuple-element.24.r_mid, f32[3,8,2176]{2,1,0:T(8,128)S(1)} %collective-permute-done.4.r_up, ...), custom_call_target="tpu_custom_call" | custom-call | tf_op jit(solution)/shard_map/pallas_call | solution.py:721
  58.0 9.7 %all_to_all.15.sums = f32[32,1,128]{2,1,0:T(1,128)S(1)} all-to-all(f32[32,1,128]{2,1,0:T(1,128)S(1)} %get-tuple-element.27), channel_id=1, replica_groups=mesh['patch'=8,'sub'=4] {'patch','sub'}, dimensions={0} | all-to-all | bytes 32768 | tf_op jit(solution)/shard_map/all_to_all | solution.py:29
  67.7 13.6 %shard_map.132 = (f32[3,8,2048]{2,1,0:T(8,128)}, f32[32,13,1,128]{3,2,1,0:T(1,128)S(1)}) custom-call(f32[9]{0:T(128)S(1)} %stack.39.numbers, f32[32,1,128]{2,1,0:T(1,128)S(1)} %all_to_all.15.sums, f32[4,3,8,2176]{3,2,1,0:T(8,128)S(1)} %get-tuple-element.28.kept, f32[4,17,48,128]{3,2,1,0:T(8,128)S(1)} %get-tuple-element.29.bends, ...), custom_call_target="tpu_custom_call" | custom-call | tf_op jit(solution)/shard_map/pallas_call | solution.py:721
  81.3 11.1 %all_to_all.16.parts = f32[32,13,1,128]{3,2,1,0:T(1,128)S(1)} all-to-all(f32[32,13,1,128]{3,2,1,0:T(1,128)S(1)} %get-tuple-element.35), channel_id=1, replica_groups=mesh['patch'=8,'sub'=4] {'patch','sub'}, dimensions={0} | all-to-all | bytes 425984 | tf_op jit(solution)/shard_map/all_to_all | solution.py:29
  92.4 0.2 shard_map.133
  92.6 11.6 %all_to_all.17.parts = f32[32,13,1,128]{3,2,1,0:T(1,128)S(1)} all-to-all(f32[32,13,1,128]{3,2,1,0:T(1,128)S(1)} %shard_map.133), channel_id=1, replica_groups=mesh['patch'=8,'sub'=4] {'patch','sub'}, dimensions={0} | all-to-all | bytes 425984 | tf_op jit(solution)/shard_map/all_to_all | solution.py:29
  104.2 0.7 shard_map.134
  (8 shorter events, 0.2 us)
Async XLA Ops:
  0.6 14.1 %copy-start = (bf16[3,128,128]{2,1,0:T(8,128)(2,1)S(1)}, bf16[3,128,128]{2,1,0:T(8,128)(2,1)}, u32[]{:S(2)}) copy-start(bf16[3,128,128]{2,1,0:T(8,128)(2,1)} %w_mid.5) | copy-start | bytes 294916
  2.8 4.2 %collective-permute-start.1 = (f32[10,8,16]{2,1,0:T(8,128)S(1)}, f32[10,8,16]{2,1,0:T(8,128)S(1)}, u32[]{:S(2)}, u32[]{:S(2)}) collective-permute-start(f32[10,8,16]{2,1,0:T(8,128)S(1)} %get-tuple-element.51), channel_id=1, source_target_pairs={{0,1},{1,2},{2,3},{3,0},{4,5},{5,6},{6,7},{7,4},{8,9},{9,10},{10,1... | collective-permute-start | bytes 15368 | tf_op jit(solution)/shard_map/ppermute | solution.py:23
  3.3 3.9 %collective-permute-start = (f32[10,8,16]{2,1,0:T(8,128)S(1)}, f32[10,8,16]{2,1,0:T(8,128)S(1)}, u32[]{:S(2)}, u32[]{:S(2)}) collective-permute-start(f32[10,8,16]{2,1,0:T(8,128)S(1)} %get-tuple-element.52), channel_id=1, source_target_pairs={{0,3},{1,0},{2,1},{3,2},{4,7},{5,4},{6,5},{7,6},{8,11},{9,8},{10,9... | collective-permute-start | bytes 15368 | tf_op jit(solution)/shard_map/ppermute | solution.py:24
  7.4 14.9 %collective-permute-start.2 = (f32[7,2176]{1,0:T(8,128)S(1)}, f32[7,2176]{1,0:T(8,128)S(1)}, u32[]{:S(2)}, u32[]{:S(2)}) collective-permute-start(f32[7,2176]{1,0:T(8,128)S(1)} %pad_maximum_fusion.1), channel_id=1, source_target_pairs={{0,4},{4,8},{8,12},{12,16},{16,20},{20,24},{24,28},{28,0},{1,5},{5... | collective-permute-start | bytes 182792 | tf_op jit(solution)/shard_map/ppermute | solution.py:761
  9.5 12.8 %collective-permute-start.3 = (f32[7,2176]{1,0:T(8,128)S(1)}, f32[7,2176]{1,0:T(8,128)S(1)}, u32[]{:S(2)}, u32[]{:S(2)}) collective-permute-start(f32[7,2176]{1,0:T(8,128)S(1)} %pad_maximum_fusion.2), channel_id=1, source_target_pairs={{0,28},{4,0},{8,4},{12,8},{16,12},{20,16},{24,20},{28,24},{1,29},{... | collective-permute-start | bytes 182792 | tf_op jit(solution)/shard_map/ppermute | solution.py:762
  12.6 26.8 %collective-permute-start.7 = (f32[4,6,2176]{2,1,0:T(8,128)S(1)}, f32[4,6,2176]{2,1,0:T(8,128)S(1)}, u32[]{:S(2)}, u32[]{:S(2)}) collective-permute-start(f32[4,6,2176]{2,1,0:T(8,128)S(1)} %get-tuple-element.41), channel_id=1, source_target_pairs={{0,28},{4,0},{8,4},{12,8},{16,12},{20,16},{24,20},{28,24},{1,29},{... | collective-permute-start | bytes 626696 | tf_op jit(solution)/shard_map/ppermute | solution.py:24
  14.7 24.7 %collective-permute-start.6 = (f32[4,6,2176]{2,1,0:T(8,128)S(1)}, f32[4,6,2176]{2,1,0:T(8,128)S(1)}, u32[]{:S(2)}, u32[]{:S(2)}) collective-permute-start(f32[4,6,2176]{2,1,0:T(8,128)S(1)} %get-tuple-element.42), channel_id=1, source_target_pairs={{0,4},{4,8},{8,12},{12,16},{16,20},{20,24},{24,28},{28,0},{1,5},{5... | collective-permute-start | bytes 626696 | tf_op jit(solution)/shard_map/ppermute | solution.py:23
  31.8 9.8 %collective-permute-start.5 = (f32[3,8,2176]{2,1,0:T(8,128)S(1)}, f32[3,8,2176]{2,1,0:T(8,128)S(1)}, u32[]{:S(2)}, u32[]{:S(2)}) collective-permute-start(f32[3,8,2176]{2,1,0:T(8,128)S(1)} %get-tuple-element.24.r_mid), channel_id=1, source_target_pairs={{0,28},{4,0},{8,4},{12,8},{16,12},{20,16},{24,20},{28,24},{1,29},{... | collective-permute-start | bytes 626696 | tf_op jit(solution)/shard_map/ppermute | solution.py:24
  36.5 10.0 %collective-permute-start.4 = (f32[3,8,2176]{2,1,0:T(8,128)S(1)}, f32[3,8,2176]{2,1,0:T(8,128)S(1)}, u32[]{:S(2)}, u32[]{:S(2)}) collective-permute-start(f32[3,8,2176]{2,1,0:T(8,128)S(1)} %get-tuple-element.24.r_mid), channel_id=1, source_target_pairs={{0,4},{4,8},{8,12},{12,16},{16,20},{20,24},{24,28},{28,0},{1,5},{5... | collective-permute-start | bytes 626696 | tf_op jit(solution)/shard_map/ppermute | solution.py:23

commit v7 on v6

--- a/solution.py
+++ b/solution.py
@@ -230,6 +230,18 @@
         where = pl.multiple_of(where, LANES)
     here = pl.ds(where, cols)
     return pltpu.make_async_copy(source.at[:, here, :], target.at[:, here, :], flags.at[line])
+
+
+def assemble_kernel(displacement, foundation, layup, load, fields, ids, flags):
+    moves = ((layup, ids), (displacement, fields.at[0:3]), (foundation, fields.at[3:6]),
+             (load, fields.at[7:10]))
+    copies = [pltpu.make_async_copy(a, b, flags.at[n]) for n, (a, b) in enumerate(moves)]
+    for copy in copies:
+        copy.start()
+    copies[0].wait()
+    fields[6] = ids[...].astype(jnp.float32)
+    for copy in copies[1:]:
+        copy.wait()
 
 
 def inner_kernel(
@@ -738,6 +750,7 @@
 
 
 LIMITS = {
+    "assemble": 4,
     "inner": 40, "outer": 40, "prepare": 8, "krylov": 10, "backward": 32, "gather": 4, "deliver": 4,
 }
 
@@ -750,7 +763,11 @@
     wide = cols + LANES
     tall = 3 * rows
     tiles = wide // LANES
-    fields = jnp.concatenate([displacement, foundation, layup.astype(f32)[None], load])
+    (fields,) = kernel_call(
+        assemble_kernel, "assemble", 0,
+        [((10, rows, cols), f32)], [((rows, cols), jnp.int32), 4],
+        displacement, foundation, layup, load, far=(0, 1, 2, 3),
+    )
     before, after = from_both(fields, "sub", 2, HY)
     gap = jnp.zeros(fields.shape[:2] + (LANES - 2 * HY,), f32)
     fields = jnp.concatenate([fields, after, gap, before], axis=2)

time: 105 us -> 104 us (level)
  other arithmetic: 5.03 us -> 2.99 us
  Pallas kernels: 45.1 us -> 46.3 us
    pallas_call x7 -> x8, Pallas kernels: 45.1 us -> 46.3 us  [kernel_call(): pl.pallas_call(body, in_specs=specs, out_specs=[IN_PLACE if n in far_outs...]
    concatenate x1 -> x0, other arithmetic: 1.16 us -> none  [per_device(): jnp.concatenate([displacement, foundation, layup.astype(f32)[None], load])]
where the time goes in v7:
time: 104 us
  Pallas kernels  46.3 us (45%)
  blocking collectives  32.4 us (31%)
  starting transfers between devices  14.5 us (14%)
  waiting for transfers between devices  5.2 us (5%)
  other arithmetic  2.99 us (3%)
  between operations  2.19 us (2%)
    pallas_call x8, Pallas kernels, kernel_call(): pl.pallas_call(body, in_specs=specs, out_specs=[IN_PLACE if n in far_outs...  46.3 us
    all_to_all x3, blocking collectives, everyone(): return lax.all_to_all(rows, AXES, 0, 0, tiled=True)  32.4 us
    ppermute x3, starting transfers between devices, from_both(): after = lax.ppermute(head, axis, ring(axis, -1))  8.81 us
    ppermute x3, waiting for transfers between devices, from_both(): before = lax.ppermute(tail, axis, ring(axis, 1))  4.9 us
    ppermute x1, starting transfers between devices, per_device(): down = lax.ppermute(sends[1], 'patch', ring('patch', -1))  3.11 us
  transfers between devices with their start and end apart: 8, of which 3 were waited for; matrix products, arithmetic and copies ran while one was open for 3% of the time, Pallas kernels for 18%

profile of v7, /device:TPU:0, one launch (start us, length us, event | category | flops | bytes accessed | tf_op | source)
XLA Modules:
  0.0 104.1 jit_solution(1805022231630773343)
XLA Ops:
  0.6 0.0 copy-start
  0.6 1.2 %shard_map.128 = f32[10,8,2048]{2,1,0:T(8,128)S(1)} custom-call(f32[3,8,2048]{2,1,0:T(8,128)} %displacement.1, f32[3,8,2048]{2,1,0:T(8,128)} %foundation.1, s32[8,2048]{1,0:T(8,128)} %layup.1, f32[3,8,2048]{2,1,0:T(8,128)} %load.1), custom_call_target="tpu_custom_call" | custom-call | tf_op jit(solution)/shard_map/pallas_call | solution.py:733
  1.9 0.1 fusion.1
  1.9 0.5 collective-permute-start.1
  2.4 2.0 %collective-permute-start = (f32[10,8,16]{2,1,0:T(8,128)S(1)}, f32[10,8,16]{2,1,0:T(8,128)S(1)}, u32[]{:S(2)}, u32[]{:S(2)}) collective-permute-start(f32[10,8,16]{2,1,0:T(8,128)S(1)} %get-tuple-element.52), channel_id=1, source_target_pairs={{0,3},{1,0},{2,1},{3,2},{4,7},{5,4},{6,5},{7,6},{8,11},{9,8},{10,9... | collective-permute-start | bytes 15368 | tf_op jit(solution)/shard_map/ppermute | solution.py:24
  4.4 0.8 multiply_multiply_fusion
  5.3 0.7 pad_maximum_fusion.2.ends
  6.0 0.1 reshape.17.table
  6.1 0.0 collective-permute-done.1
  6.1 0.2 collective-permute-done
  6.3 0.1 concatenate.12.fields
  6.6 2.1 %collective-permute-start.2 = (f32[7,2176]{1,0:T(8,128)S(1)}, f32[7,2176]{1,0:T(8,128)S(1)}, u32[]{:S(2)}, u32[]{:S(2)}) collective-permute-start(f32[7,2176]{1,0:T(8,128)S(1)} %pad_maximum_fusion), channel_id=1, source_target_pairs={{0,4},{4,8},{8,12},{12,16},{16,20},{20,24},{24,28},{28,0},{1,5},{5... | collective-permute-start | bytes 182792 | tf_op jit(solution)/shard_map/ppermute | solution.py:778
  8.7 3.1 %collective-permute-start.3 = (f32[7,2176]{1,0:T(8,128)S(1)}, f32[7,2176]{1,0:T(8,128)S(1)}, u32[]{:S(2)}, u32[]{:S(2)}) collective-permute-start(f32[7,2176]{1,0:T(8,128)S(1)} %pad_maximum_fusion.1), channel_id=1, source_target_pairs={{0,28},{4,0},{8,4},{12,8},{16,12},{20,16},{24,20},{28,24},{1,29},{... | collective-permute-start | bytes 182792 | tf_op jit(solution)/shard_map/ppermute | solution.py:779
  11.8 2.1 %collective-permute-start.7 = (f32[4,6,2176]{2,1,0:T(8,128)S(1)}, f32[4,6,2176]{2,1,0:T(8,128)S(1)}, u32[]{:S(2)}, u32[]{:S(2)}) collective-permute-start(f32[4,6,2176]{2,1,0:T(8,128)S(1)} %get-tuple-element.41), channel_id=1, source_target_pairs={{0,28},{4,0},{8,4},{12,8},{16,12},{20,16},{24,20},{28,24},{1,29},{... | collective-permute-start | bytes 626696 | tf_op jit(solution)/shard_map/ppermute | solution.py:24
  13.9 0.0 collective-permute-start.6
  13.9 0.0 copy-done
  13.9 7.6 %shard_map.129 = (f32[17,64,128]{2,1,0:T(8,128)S(1)}, bf16[4,12288,128]{2,1,0:T(8,128)(2,1)}, bf16[16,12288]{1,0:T(8,128)(2,1)S(1)}) custom-call(f32[10,8,2176]{2,1,0:T(8,128)S(1)} %concatenate.12.fields, bf16[32,128]{1,0:T(8,128)(2,1)S(1)} %pad_maximum_fusion.2.ends, bf16[3,128,128]{2,1,0:T(8,128)(2,1)S(1)} %copy-done), custom_call_target="tpu_custom_call" | custom-call | tf_op jit(solution)/shard_map/pallas_call | solution.py:733
  21.5 0.0 collective-permute-done.2.up
  21.5 0.0 collective-permute-done.3.down
  21.5 9.4 %shard_map.130 = (f32[3,8,2176]{2,1,0:T(8,128)S(1)}, f32[3,8,2048]{2,1,0:T(8,128)}, bf16[4,4096,128]{2,1,0:T(8,128)(2,1)}, bf16[16,4096]{1,0:T(8,128)(2,1)S(1)}) custom-call(f32[288]{0:T(512)S(1)} %reshape.17.table, f32[10,8,2176]{2,1,0:T(8,128)S(1)} %concatenate.12.fields, f32[7,2176]{1,0:T(8,128)S(1)} %collective-permute-done.2.up, ...), custom_call_target="tpu_custom_call" | custom-call | tf_op jit(solution)/shard_map/pallas_call | solution.py:733
  30.9 4.8 %collective-permute-start.5 = (f32[3,8,2176]{2,1,0:T(8,128)S(1)}, f32[3,8,2176]{2,1,0:T(8,128)S(1)}, u32[]{:S(2)}, u32[]{:S(2)}) collective-permute-start(f32[3,8,2176]{2,1,0:T(8,128)S(1)} %get-tuple-element.24.r_mid), channel_id=1, source_target_pairs={{0,28},{4,0},{8,4},{12,8},{16,12},{20,16},{24,20},{28,24},{1,29},{... | collective-permute-start | bytes 626696 | tf_op jit(solution)/shard_map/ppermute | solution.py:24
  35.7 0.0 collective-permute-start.4
  35.7 1.4 %slice_reduce_fusion = (f32[]{:T(128)}, f32[]{:T(128)}) fusion(f32[8,6,6]{2,0,1:T(8,128)} %param.13), kind=kLoop, calls=%fused_computation.12 | loop fusion | flops 14 | bytes 72 | tf_op jit(solution)/shard_map/reduce_sum | solution.py:716
  38.5 0.1 stack.39.numbers
  38.6 0.0 collective-permute-done.7.fl_down
  38.6 0.0 collective-permute-done.6.fl_up
  38.6 2.1 %shard_map.131 = (f32[21,24,2176]{2,1,0:T(8,128)S(1)}, f32[3,24,2176]{2,1,0:T(8,128)S(1)}) custom-call(f32[288]{0:T(512)S(1)} %reshape.17.table, f32[10,8,2176]{2,1,0:T(8,128)S(1)} %concatenate.12.fields, f32[4,6,2176]{2,1,0:T(8,128)S(1)} %collective-permute-done.6.fl_up, f32[4,6,2176]{2,1,0:T(8,128)S(1)} %collective-permute-done.7.fl_down), custom_call_target="tpu_custom_call" | custom-call | tf_op jit(solution)/shard_map/pallas_call | solution.py:733
  40.7 0.1 collective-permute-done.5.r_down
  40.8 4.9 %collective-permute-done.4.r_up = f32[3,8,2176]{2,1,0:T(8,128)S(1)} collective-permute-done((f32[3,8,2176]{2,1,0:T(8,128)S(1)}, f32[3,8,2176]{2,1,0:T(8,128)S(1)}, u32[]{:S(2)}, u32[]{:S(2)}) %collective-permute-start.4) | collective-permute-done | bytes 208928 | tf_op jit(solution)/shard_map/ppermute | solution.py:23
  45.7 11.5 %shard_map.132 = (f32[4,3,8,2176]{3,2,1,0:T(8,128)S(1)}, f32[4,17,48,128]{3,2,1,0:T(8,128)S(1)}, f32[32,1,128]{2,1,0:T(1,128)S(1)}) custom-call(f32[9]{0:T(128)S(1)} %stack.39.numbers, f32[3,8,2176]{2,1,0:T(8,128)S(1)} %get-tuple-element.24.r_mid, f32[3,8,2176]{2,1,0:T(8,128)S(1)} %collective-permute-done.4.r_up, ...), custom_call_target="tpu_custom_call" | custom-call | tf_op jit(solution)/shard_map/pallas_call | solution.py:733
  57.2 9.7 %all_to_all.15.sums = f32[32,1,128]{2,1,0:T(1,128)S(1)} all-to-all(f32[32,1,128]{2,1,0:T(1,128)S(1)} %get-tuple-element.27), channel_id=1, replica_groups=mesh['patch'=8,'sub'=4] {'patch','sub'}, dimensions={0} | all-to-all | bytes 32768 | tf_op jit(solution)/shard_map/all_to_all | solution.py:29
  66.9 13.6 %shard_map.133 = (f32[3,8,2048]{2,1,0:T(8,128)}, f32[32,13,1,128]{3,2,1,0:T(1,128)S(1)}) custom-call(f32[9]{0:T(128)S(1)} %stack.39.numbers, f32[32,1,128]{2,1,0:T(1,128)S(1)} %all_to_all.15.sums, f32[4,3,8,2176]{3,2,1,0:T(8,128)S(1)} %get-tuple-element.28.kept, f32[4,17,48,128]{3,2,1,0:T(8,128)S(1)} %get-tuple-element.29.bends, ...), custom_call_target="tpu_custom_call" | custom-call | tf_op jit(solution)/shard_map/pallas_call | solution.py:733
  80.5 11.1 %all_to_all.16.parts = f32[32,13,1,128]{3,2,1,0:T(1,128)S(1)} all-to-all(f32[32,13,1,128]{3,2,1,0:T(1,128)S(1)} %get-tuple-element.35), channel_id=1, replica_groups=mesh['patch'=8,'sub'=4] {'patch','sub'}, dimensions={0} | all-to-all | bytes 425984 | tf_op jit(solution)/shard_map/all_to_all | solution.py:29
  91.6 0.2 shard_map.134
  91.8 11.6 %all_to_all.17.parts = f32[32,13,1,128]{3,2,1,0:T(1,128)S(1)} all-to-all(f32[32,13,1,128]{3,2,1,0:T(1,128)S(1)} %shard_map.134), channel_id=1, replica_groups=mesh['patch'=8,'sub'=4] {'patch','sub'}, dimensions={0} | all-to-all | bytes 425984 | tf_op jit(solution)/shard_map/all_to_all | solution.py:29
  103.4 0.7 shard_map.135
  (8 shorter events, 0.2 us)
Async XLA Ops:
  0.6 13.3 %copy-start = (bf16[3,128,128]{2,1,0:T(8,128)(2,1)S(1)}, bf16[3,128,128]{2,1,0:T(8,128)(2,1)}, u32[]{:S(2)}) copy-start(bf16[3,128,128]{2,1,0:T(8,128)(2,1)} %w_mid.5) | copy-start | bytes 294916
  1.9 4.2 %collective-permute-start.1 = (f32[10,8,16]{2,1,0:T(8,128)S(1)}, f32[10,8,16]{2,1,0:T(8,128)S(1)}, u32[]{:S(2)}, u32[]{:S(2)}) collective-permute-start(f32[10,8,16]{2,1,0:T(8,128)S(1)} %get-tuple-element.51), channel_id=1, source_target_pairs={{0,1},{1,2},{2,3},{3,0},{4,5},{5,6},{6,7},{7,4},{8,9},{9,10},{10,1... | collective-permute-start | bytes 15368 | tf_op jit(solution)/shard_map/ppermute | solution.py:23
  2.4 3.9 %collective-permute-start = (f32[10,8,16]{2,1,0:T(8,128)S(1)}, f32[10,8,16]{2,1,0:T(8,128)S(1)}, u32[]{:S(2)}, u32[]{:S(2)}) collective-permute-start(f32[10,8,16]{2,1,0:T(8,128)S(1)} %get-tuple-element.52), channel_id=1, source_target_pairs={{0,3},{1,0},{2,1},{3,2},{4,7},{5,4},{6,5},{7,6},{8,11},{9,8},{10,9... | collective-permute-start | bytes 15368 | tf_op jit(solution)/shard_map/ppermute | solution.py:24
  6.6 14.9 %collective-permute-start.2 = (f32[7,2176]{1,0:T(8,128)S(1)}, f32[7,2176]{1,0:T(8,128)S(1)}, u32[]{:S(2)}, u32[]{:S(2)}) collective-permute-start(f32[7,2176]{1,0:T(8,128)S(1)} %pad_maximum_fusion), channel_id=1, source_target_pairs={{0,4},{4,8},{8,12},{12,16},{16,20},{20,24},{24,28},{28,0},{1,5},{5... | collective-permute-start | bytes 182792 | tf_op jit(solution)/shard_map/ppermute | solution.py:778
  8.7 12.8 %collective-permute-start.3 = (f32[7,2176]{1,0:T(8,128)S(1)}, f32[7,2176]{1,0:T(8,128)S(1)}, u32[]{:S(2)}, u32[]{:S(2)}) collective-permute-start(f32[7,2176]{1,0:T(8,128)S(1)} %pad_maximum_fusion.1), channel_id=1, source_target_pairs={{0,28},{4,0},{8,4},{12,8},{16,12},{20,16},{24,20},{28,24},{1,29},{... | collective-permute-start | bytes 182792 | tf_op jit(solution)/shard_map/ppermute | solution.py:779
  11.8 26.8 %collective-permute-start.7 = (f32[4,6,2176]{2,1,0:T(8,128)S(1)}, f32[4,6,2176]{2,1,0:T(8,128)S(1)}, u32[]{:S(2)}, u32[]{:S(2)}) collective-permute-start(f32[4,6,2176]{2,1,0:T(8,128)S(1)} %get-tuple-element.41), channel_id=1, source_target_pairs={{0,28},{4,0},{8,4},{12,8},{16,12},{20,16},{24,20},{28,24},{1,29},{... | collective-permute-start | bytes 626696 | tf_op jit(solution)/shard_map/ppermute | solution.py:24
  13.9 24.7 %collective-permute-start.6 = (f32[4,6,2176]{2,1,0:T(8,128)S(1)}, f32[4,6,2176]{2,1,0:T(8,128)S(1)}, u32[]{:S(2)}, u32[]{:S(2)}) collective-permute-start(f32[4,6,2176]{2,1,0:T(8,128)S(1)} %get-tuple-element.42), channel_id=1, source_target_pairs={{0,4},{4,8},{8,12},{12,16},{16,20},{20,24},{24,28},{28,0},{1,5},{5... | collective-permute-start | bytes 626696 | tf_op jit(solution)/shard_map/ppermute | solution.py:23
  30.9 9.8 %collective-permute-start.5 = (f32[3,8,2176]{2,1,0:T(8,128)S(1)}, f32[3,8,2176]{2,1,0:T(8,128)S(1)}, u32[]{:S(2)}, u32[]{:S(2)}) collective-permute-start(f32[3,8,2176]{2,1,0:T(8,128)S(1)} %get-tuple-element.24.r_mid), channel_id=1, source_target_pairs={{0,28},{4,0},{8,4},{12,8},{16,12},{20,16},{24,20},{28,24},{1,29},{... | collective-permute-start | bytes 626696 | tf_op jit(solution)/shard_map/ppermute | solution.py:24
  35.7 10.0 %collective-permute-start.4 = (f32[3,8,2176]{2,1,0:T(8,128)S(1)}, f32[3,8,2176]{2,1,0:T(8,128)S(1)}, u32[]{:S(2)}, u32[]{:S(2)}) collective-permute-start(f32[3,8,2176]{2,1,0:T(8,128)S(1)} %get-tuple-element.24.r_mid), channel_id=1, source_target_pairs={{0,4},{4,8},{8,12},{12,16},{16,20},{20,24},{24,28},{28,0},{1,5},{5... | collective-permute-start | bytes 626696 | tf_op jit(solution)/shard_map/ppermute | solution.py:23

commit v8 on v7

--- a/solution.py
+++ b/solution.py
@@ -205,15 +205,16 @@
     parts += [strain[rim, pl.ds(row, FIELDS, stride=spread), :] for row in rims]
     x = widened(jnp.concatenate(parts, axis=1))
     start, span = base * cols, kept * cols
-    inputs[:, pl.ds(start, span)] = x[:, :span]
     copies = []
+    if kept:
+        inputs[:, pl.ds(start, span)] = x[:, :span]
 
     def keep(k, h):
         hidden[k, pl.ds(start, span), :] = h[:span]
         copies.append(layer_copy(k, start, span, hidden, stored, flags[k]))
         copies[-1].start()
 
-    out = learn(x, *weights, keep)
+    out = learn(x, *weights, keep if kept else None)
     for n, row in enumerate(rows):
         for t in range(rim):
             at = n * cols + t * LANES
@@ -370,10 +371,14 @@
 
     lax.fori_loop(0, tiles, strains, 0)
     weights = (ends.at[0:PADDED], w_mid, ends.at[PADDED : 2 * PADDED])
-    lines = (rows, 2 * rows - 1, rows - 1, 2 * rows)
+    own_lines, far_lines = (rows, 2 * rows - 1), (rows - 1, 2 * rows)
     copies = learn_lines(
-        lines, lines, 2, 0, strain, learned, tall, cols, weights, hidden, stored, inputs,
+        own_lines, (), 2, 0, strain, learned, tall, cols, weights, hidden, stored, inputs,
         [flags.at[k] for k in range(w_mid.shape[0] + 1)],
+    )
+    learn_lines(
+        far_lines, own_lines + far_lines, 0, 0, strain, learned, tall, cols, weights, hidden,
+        stored, inputs, (),
     )
 
     def push(tile, carry):

time: 104 us -> 104 us (level)
  no operation moved by 1% of the time
where the time goes in v8:
time: 104 us
  Pallas kernels  46.3 us (45%)
  blocking collectives  32.4 us (31%)
  starting transfers between devices  14.5 us (14%)
  waiting for transfers between devices  5.2 us (5%)
  other arithmetic  2.99 us (3%)
  between operations  2.19 us (2%)
    pallas_call x8, Pallas kernels, kernel_call(): pl.pallas_call(body, in_specs=specs, out_specs=[IN_PLACE if n in far_outs...  46.3 us
    all_to_all x3, blocking collectives, everyone(): return lax.all_to_all(rows, AXES, 0, 0, tiled=True)  32.4 us
    ppermute x3, starting transfers between devices, from_both(): after = lax.ppermute(head, axis, ring(axis, -1))  8.81 us
    ppermute x3, waiting for transfers between devices, from_both(): before = lax.ppermute(tail, axis, ring(axis, 1))  4.9 us
    ppermute x1, starting transfers between devices, per_device(): down = lax.ppermute(sends[1], 'patch', ring('patch', -1))  3.11 us
  transfers between devices with their start and end apart: 8, of which 3 were waited for; matrix products, arithmetic and copies ran while one was open for 3% of the time, Pallas kernels for 18%

profile of v8, /device:TPU:0, one launch (start us, length us, event | category | flops | bytes accessed | tf_op | source)
XLA Modules:
  0.0 104.1 jit_solution(15987248000550564188)
XLA Ops:
  0.6 0.0 copy-start
  0.6 1.2 %shard_map.128 = f32[10,8,2048]{2,1,0:T(8,128)S(1)} custom-call(f32[3,8,2048]{2,1,0:T(8,128)} %displacement.1, f32[3,8,2048]{2,1,0:T(8,128)} %foundation.1, s32[8,2048]{1,0:T(8,128)} %layup.1, f32[3,8,2048]{2,1,0:T(8,128)} %load.1), custom_call_target="tpu_custom_call" | custom-call | tf_op jit(solution)/shard_map/pallas_call | solution.py:738
  1.9 0.1 fusion.1
  1.9 0.5 collective-permute-start.1
  2.4 2.0 %collective-permute-start = (f32[10,8,16]{2,1,0:T(8,128)S(1)}, f32[10,8,16]{2,1,0:T(8,128)S(1)}, u32[]{:S(2)}, u32[]{:S(2)}) collective-permute-start(f32[10,8,16]{2,1,0:T(8,128)S(1)} %get-tuple-element.52), channel_id=1, source_target_pairs={{0,3},{1,0},{2,1},{3,2},{4,7},{5,4},{6,5},{7,6},{8,11},{9,8},{10,9... | collective-permute-start | bytes 15368 | tf_op jit(solution)/shard_map/ppermute | solution.py:24
  4.4 0.8 multiply_multiply_fusion
  5.3 0.7 pad_maximum_fusion.2.ends
  6.0 0.1 reshape.17.table
  6.1 0.0 collective-permute-done.1
  6.1 0.2 collective-permute-done
  6.3 0.1 concatenate.12.fields
  6.6 2.1 %collective-permute-start.2 = (f32[7,2176]{1,0:T(8,128)S(1)}, f32[7,2176]{1,0:T(8,128)S(1)}, u32[]{:S(2)}, u32[]{:S(2)}) collective-permute-start(f32[7,2176]{1,0:T(8,128)S(1)} %pad_maximum_fusion), channel_id=1, source_target_pairs={{0,4},{4,8},{8,12},{12,16},{16,20},{20,24},{24,28},{28,0},{1,5},{5... | collective-permute-start | bytes 182792 | tf_op jit(solution)/shard_map/ppermute | solution.py:783
  8.7 3.1 %collective-permute-start.3 = (f32[7,2176]{1,0:T(8,128)S(1)}, f32[7,2176]{1,0:T(8,128)S(1)}, u32[]{:S(2)}, u32[]{:S(2)}) collective-permute-start(f32[7,2176]{1,0:T(8,128)S(1)} %pad_maximum_fusion.1), channel_id=1, source_target_pairs={{0,28},{4,0},{8,4},{12,8},{16,12},{20,16},{24,20},{28,24},{1,29},{... | collective-permute-start | bytes 182792 | tf_op jit(solution)/shard_map/ppermute | solution.py:784
  11.8 2.1 %collective-permute-start.7 = (f32[4,6,2176]{2,1,0:T(8,128)S(1)}, f32[4,6,2176]{2,1,0:T(8,128)S(1)}, u32[]{:S(2)}, u32[]{:S(2)}) collective-permute-start(f32[4,6,2176]{2,1,0:T(8,128)S(1)} %get-tuple-element.41), channel_id=1, source_target_pairs={{0,28},{4,0},{8,4},{12,8},{16,12},{20,16},{24,20},{28,24},{1,29},{... | collective-permute-start | bytes 626696 | tf_op jit(solution)/shard_map/ppermute | solution.py:24
  13.9 0.0 collective-permute-start.6
  13.9 0.0 copy-done
  13.9 7.6 %shard_map.129 = (f32[17,64,128]{2,1,0:T(8,128)S(1)}, bf16[4,12288,128]{2,1,0:T(8,128)(2,1)}, bf16[16,12288]{1,0:T(8,128)(2,1)S(1)}) custom-call(f32[10,8,2176]{2,1,0:T(8,128)S(1)} %concatenate.12.fields, bf16[32,128]{1,0:T(8,128)(2,1)S(1)} %pad_maximum_fusion.2.ends, bf16[3,128,128]{2,1,0:T(8,128)(2,1)S(1)} %copy-done), custom_call_target="tpu_custom_call" | custom-call | tf_op jit(solution)/shard_map/pallas_call | solution.py:738
  21.5 0.0 collective-permute-done.2.up
  21.5 0.0 collective-permute-done.3.down
  21.5 9.5 %shard_map.130 = (f32[3,8,2176]{2,1,0:T(8,128)S(1)}, f32[3,8,2048]{2,1,0:T(8,128)}, bf16[4,4096,128]{2,1,0:T(8,128)(2,1)}, bf16[16,4096]{1,0:T(8,128)(2,1)S(1)}) custom-call(f32[288]{0:T(512)S(1)} %reshape.17.table, f32[10,8,2176]{2,1,0:T(8,128)S(1)} %concatenate.12.fields, f32[7,2176]{1,0:T(8,128)S(1)} %collective-permute-done.2.up, ...), custom_call_target="tpu_custom_call" | custom-call | tf_op jit(solution)/shard_map/pallas_call | solution.py:738
  31.0 4.8 %collective-permute-start.5 = (f32[3,8,2176]{2,1,0:T(8,128)S(1)}, f32[3,8,2176]{2,1,0:T(8,128)S(1)}, u32[]{:S(2)}, u32[]{:S(2)}) collective-permute-start(f32[3,8,2176]{2,1,0:T(8,128)S(1)} %get-tuple-element.24.r_mid), channel_id=1, source_target_pairs={{0,28},{4,0},{8,4},{12,8},{16,12},{20,16},{24,20},{28,24},{1,29},{... | collective-permute-start | bytes 626696 | tf_op jit(solution)/shard_map/ppermute | solution.py:24
  35.7 0.0 collective-permute-start.4
  35.7 1.4 %slice_reduce_fusion = (f32[]{:T(128)}, f32[]{:T(128)}) fusion(f32[8,6,6]{2,0,1:T(8,128)} %param.13), kind=kLoop, calls=%fused_computation.12 | loop fusion | flops 14 | bytes 72 | tf_op jit(solution)/shard_map/reduce_sum | solution.py:721
  38.5 0.1 stack.39.numbers
  38.6 0.0 collective-permute-done.7.fl_down
  38.6 0.0 collective-permute-done.6.fl_up
  38.6 2.1 %shard_map.131 = (f32[21,24,2176]{2,1,0:T(8,128)S(1)}, f32[3,24,2176]{2,1,0:T(8,128)S(1)}) custom-call(f32[288]{0:T(512)S(1)} %reshape.17.table, f32[10,8,2176]{2,1,0:T(8,128)S(1)} %concatenate.12.fields, f32[4,6,2176]{2,1,0:T(8,128)S(1)} %collective-permute-done.6.fl_up, f32[4,6,2176]{2,1,0:T(8,128)S(1)} %collective-permute-done.7.fl_down), custom_call_target="tpu_custom_call" | custom-call | tf_op jit(solution)/shard_map/pallas_call | solution.py:738
  40.7 0.1 collective-permute-done.5.r_down
  40.8 4.9 %collective-permute-done.4.r_up = f32[3,8,2176]{2,1,0:T(8,128)S(1)} collective-permute-done((f32[3,8,2176]{2,1,0:T(8,128)S(1)}, f32[3,8,2176]{2,1,0:T(8,128)S(1)}, u32[]{:S(2)}, u32[]{:S(2)}) %collective-permute-start.4) | collective-permute-done | bytes 208928 | tf_op jit(solution)/shard_map/ppermute | solution.py:23
  45.7 11.5 %shard_map.132 = (f32[4,3,8,2176]{3,2,1,0:T(8,128)S(1)}, f32[4,17,48,128]{3,2,1,0:T(8,128)S(1)}, f32[32,1,128]{2,1,0:T(1,128)S(1)}) custom-call(f32[9]{0:T(128)S(1)} %stack.39.numbers, f32[3,8,2176]{2,1,0:T(8,128)S(1)} %get-tuple-element.24.r_mid, f32[3,8,2176]{2,1,0:T(8,128)S(1)} %collective-permute-done.4.r_up, ...), custom_call_target="tpu_custom_call" | custom-call | tf_op jit(solution)/shard_map/pallas_call | solution.py:738
  57.2 9.7 %all_to_all.15.sums = f32[32,1,128]{2,1,0:T(1,128)S(1)} all-to-all(f32[32,1,128]{2,1,0:T(1,128)S(1)} %get-tuple-element.27), channel_id=1, replica_groups=mesh['patch'=8,'sub'=4] {'patch','sub'}, dimensions={0} | all-to-all | bytes 32768 | tf_op jit(solution)/shard_map/all_to_all | solution.py:29
  66.9 13.6 %shard_map.133 = (f32[3,8,2048]{2,1,0:T(8,128)}, f32[32,13,1,128]{3,2,1,0:T(1,128)S(1)}) custom-call(f32[9]{0:T(128)S(1)} %stack.39.numbers, f32[32,1,128]{2,1,0:T(1,128)S(1)} %all_to_all.15.sums, f32[4,3,8,2176]{3,2,1,0:T(8,128)S(1)} %get-tuple-element.28.kept, f32[4,17,48,128]{3,2,1,0:T(8,128)S(1)} %get-tuple-element.29.bends, ...), custom_call_target="tpu_custom_call" | custom-call | tf_op jit(solution)/shard_map/pallas_call | solution.py:738
  80.5 11.1 %all_to_all.16.parts = f32[32,13,1,128]{3,2,1,0:T(1,128)S(1)} all-to-all(f32[32,13,1,128]{3,2,1,0:T(1,128)S(1)} %get-tuple-element.35), channel_id=1, replica_groups=mesh['patch'=8,'sub'=4] {'patch','sub'}, dimensions={0} | all-to-all | bytes 425984 | tf_op jit(solution)/shard_map/all_to_all | solution.py:29
  91.6 0.2 shard_map.134
  91.8 11.6 %all_to_all.17.parts = f32[32,13,1,128]{3,2,1,0:T(1,128)S(1)} all-to-all(f32[32,13,1,128]{3,2,1,0:T(1,128)S(1)} %shard_map.134), channel_id=1, replica_groups=mesh['patch'=8,'sub'=4] {'patch','sub'}, dimensions={0} | all-to-all | bytes 425984 | tf_op jit(solution)/shard_map/all_to_all | solution.py:29
  103.4 0.7 shard_map.135
  (8 shorter events, 0.2 us)
Async XLA Ops:
  0.6 13.3 %copy-start = (bf16[3,128,128]{2,1,0:T(8,128)(2,1)S(1)}, bf16[3,128,128]{2,1,0:T(8,128)(2,1)}, u32[]{:S(2)}) copy-start(bf16[3,128,128]{2,1,0:T(8,128)(2,1)} %w_mid.5) | copy-start | bytes 294916
  1.9 4.2 %collective-permute-start.1 = (f32[10,8,16]{2,1,0:T(8,128)S(1)}, f32[10,8,16]{2,1,0:T(8,128)S(1)}, u32[]{:S(2)}, u32[]{:S(2)}) collective-permute-start(f32[10,8,16]{2,1,0:T(8,128)S(1)} %get-tuple-element.51), channel_id=1, source_target_pairs={{0,1},{1,2},{2,3},{3,0},{4,5},{5,6},{6,7},{7,4},{8,9},{9,10},{10,1... | collective-permute-start | bytes 15368 | tf_op jit(solution)/shard_map/ppermute | solution.py:23
  2.4 3.9 %collective-permute-start = (f32[10,8,16]{2,1,0:T(8,128)S(1)}, f32[10,8,16]{2,1,0:T(8,128)S(1)}, u32[]{:S(2)}, u32[]{:S(2)}) collective-permute-start(f32[10,8,16]{2,1,0:T(8,128)S(1)} %get-tuple-element.52), channel_id=1, source_target_pairs={{0,3},{1,0},{2,1},{3,2},{4,7},{5,4},{6,5},{7,6},{8,11},{9,8},{10,9... | collective-permute-start | bytes 15368 | tf_op jit(solution)/shard_map/ppermute | solution.py:24
  6.6 14.9 %collective-permute-start.2 = (f32[7,2176]{1,0:T(8,128)S(1)}, f32[7,2176]{1,0:T(8,128)S(1)}, u32[]{:S(2)}, u32[]{:S(2)}) collective-permute-start(f32[7,2176]{1,0:T(8,128)S(1)} %pad_maximum_fusion), channel_id=1, source_target_pairs={{0,4},{4,8},{8,12},{12,16},{16,20},{20,24},{24,28},{28,0},{1,5},{5... | collective-permute-start | bytes 182792 | tf_op jit(solution)/shard_map/ppermute | solution.py:783
  8.7 12.8 %collective-permute-start.3 = (f32[7,2176]{1,0:T(8,128)S(1)}, f32[7,2176]{1,0:T(8,128)S(1)}, u32[]{:S(2)}, u32[]{:S(2)}) collective-permute-start(f32[7,2176]{1,0:T(8,128)S(1)} %pad_maximum_fusion.1), channel_id=1, source_target_pairs={{0,28},{4,0},{8,4},{12,8},{16,12},{20,16},{24,20},{28,24},{1,29},{... | collective-permute-start | bytes 182792 | tf_op jit(solution)/shard_map/ppermute | solution.py:784
  11.8 26.8 %collective-permute-start.7 = (f32[4,6,2176]{2,1,0:T(8,128)S(1)}, f32[4,6,2176]{2,1,0:T(8,128)S(1)}, u32[]{:S(2)}, u32[]{:S(2)}) collective-permute-start(f32[4,6,2176]{2,1,0:T(8,128)S(1)} %get-tuple-element.41), channel_id=1, source_target_pairs={{0,28},{4,0},{8,4},{12,8},{16,12},{20,16},{24,20},{28,24},{1,29},{... | collective-permute-start | bytes 626696 | tf_op jit(solution)/shard_map/ppermute | solution.py:24
  13.9 24.7 %collective-permute-start.6 = (f32[4,6,2176]{2,1,0:T(8,128)S(1)}, f32[4,6,2176]{2,1,0:T(8,128)S(1)}, u32[]{:S(2)}, u32[]{:S(2)}) collective-permute-start(f32[4,6,2176]{2,1,0:T(8,128)S(1)} %get-tuple-element.42), channel_id=1, source_target_pairs={{0,4},{4,8},{8,12},{12,16},{16,20},{20,24},{24,28},{28,0},{1,5},{5... | collective-permute-start | bytes 626696 | tf_op jit(solution)/shard_map/ppermute | solution.py:23
  31.0 9.8 %collective-permute-start.5 = (f32[3,8,2176]{2,1,0:T(8,128)S(1)}, f32[3,8,2176]{2,1,0:T(8,128)S(1)}, u32[]{:S(2)}, u32[]{:S(2)}) collective-permute-start(f32[3,8,2176]{2,1,0:T(8,128)S(1)} %get-tuple-element.24.r_mid), channel_id=1, source_target_pairs={{0,28},{4,0},{8,4},{12,8},{16,12},{20,16},{24,20},{28,24},{1,29},{... | collective-permute-start | bytes 626696 | tf_op jit(solution)/shard_map/ppermute | solution.py:24
  35.7 10.0 %collective-permute-start.4 = (f32[3,8,2176]{2,1,0:T(8,128)S(1)}, f32[3,8,2176]{2,1,0:T(8,128)S(1)}, u32[]{:S(2)}, u32[]{:S(2)}) collective-permute-start(f32[3,8,2176]{2,1,0:T(8,128)S(1)} %get-tuple-element.24.r_mid), channel_id=1, source_target_pairs={{0,4},{4,8},{8,12},{12,16},{16,20},{20,24},{24,28},{28,0},{1,5},{5... | collective-permute-start | bytes 626696 | tf_op jit(solution)/shard_map/ppermute | solution.py:23
